TPU v7x, 128 devices: a whole 4x4x4 slice. The times are simulated.
128 devices in a mesh: gy: 8 (over z, core), gx: 16 (over y, x).
Axes of the slice: x: 4, y: 4, z: 4, core: 2. Of those that a mesh axis runs over, the one named last changes fastest.
Arguments:
- radiance: bfloat16 [512, 512, 4096], P('gy', 'gx'), may hold values from -64 to 64
- kernel: float32 [3, 3, 4096], replicated, may hold values from 0.05 to 0.5
- test_matrix: bfloat16 [4096, 128], replicated, may hold values from -0.09375 to 0.09375
Outputs:
- basis_out: float32 [512, 512, 128], P('gy', 'gx')
- coeffs: float32 [128, 4096], replicated
All inputs are finite; a program needn't handle non-finite values.
Results may differ from a plain program's by a relative error of at most 0.00085.
The roundings to bfloat16 on the way count: a program that leaves them out, or rounds other values in their place, can miss the bound.
Values may be sent and summed in bfloat16 or wider, within the bound.
No kernel may reach another device: no remote copies, remote signals or barrier semaphores. Data moves between devices by JAX's collectives and lax.ppermute only.
A program may use at most 192 MiB of HBM per device.

v0:
```python
import math

import jax
import jax.numpy as jnp
from jax import lax
from jax.sharding import PartitionSpec as P


def from_partner(value, axis, apart):
    mask = 2**apart
    pairs = [(source, source ^ mask) for source in range(lax.axis_size(axis))]
    return lax.ppermute(value, axis, pairs)


def with_halo(array, sides, width):
    for axis, dim in sides:
        devices, length = (lax.axis_size(axis), array.shape[dim])
        up = [(i, (i + 1) % devices) for i in range(devices - 1)]
        down = [(j, i) for i, j in up]
        last = lax.slice_in_dim(array, length - width, length, axis=dim)
        first = lax.slice_in_dim(array, 0, width, axis=dim)
        before = lax.ppermute(last, axis, up)
        after = lax.ppermute(first, axis, down)
        array = jnp.concatenate([before, array, after], axis=dim)
    return array


def smooth_block(padded, kernel, row_total, col_total):
    summed = jnp.zeros((row_total, col_total, padded.shape[2]), jnp.float32)
    for row_shift in range(3):
        for col_shift in range(3):
            window = padded[
                row_shift : row_shift + row_total, col_shift : col_shift + col_total
            ].astype(jnp.float32)
            summed = summed + kernel[row_shift, col_shift] * window
    return summed.astype(jnp.bfloat16)


def gram_of(values):
    return jnp.dot(
        values.T, values, precision=lax.Precision.HIGHEST, preferred_element_type=jnp.float32
    )


def combine_pair(triangle, partner):
    joined = jnp.dot(
        triangle, triangle.T, precision=lax.Precision.HIGHEST, preferred_element_type=jnp.float32
    )
    joined = joined + jnp.dot(
        partner, partner.T, precision=lax.Precision.HIGHEST, preferred_element_type=jnp.float32
    )
    return jnp.linalg.cholesky(joined)


def rows_levels(triangle):
    for bit_number in range(lax.axis_size("gy").bit_length() - 1):
        triangle = combine_pair(triangle, from_partner(triangle, "gy", bit_number))
    return triangle


def cols_levels(triangle):
    for bit_number in range(lax.axis_size("gx").bit_length() - 1):
        triangle = combine_pair(triangle, from_partner(triangle, "gx", bit_number))
    return triangle


def factor_basis(values):
    local_gram = gram_of(values)
    triangle = jnp.linalg.cholesky(local_gram)
    triangle = cols_levels(rows_levels(triangle))
    return lax.linalg.triangular_solve(
        triangle, values, left_side=False, lower=True, transpose_a=True
    )


def on_device(radiance, kernel, test_matrix):
    height, breadth, channels = radiance.shape
    devices = lax.axis_size("gy") * lax.axis_size("gx")
    pixel_count = height * breadth * devices
    padded = with_halo(radiance, (("gy", 0), ("gx", 1)), 1)
    smoothed = smooth_block(padded, kernel, height, breadth)
    flattened = smoothed.reshape(height * breadth, channels)
    sketch = jnp.dot(flattened, test_matrix, preferred_element_type=jnp.float32)
    first_basis = factor_basis(sketch).astype(jnp.bfloat16)
    summed = lax.psum(
        jnp.dot(first_basis.T, flattened, preferred_element_type=jnp.float32), ("gy", "gx")
    )
    range_map = summed.astype(jnp.bfloat16)
    second = jnp.dot(flattened, range_map.T, preferred_element_type=jnp.float32)
    basis_out = factor_basis(second) * math.sqrt(pixel_count)
    basis_half = basis_out.astype(jnp.bfloat16)
    projected = jnp.dot(basis_half.T, flattened, preferred_element_type=jnp.float32)
    coeffs = lax.psum(projected, ("gy", "gx")) * (math.sqrt(channels) / pixel_count)
    return (basis_out.reshape(height, breadth, basis_out.shape[1]), coeffs)


def solution(mesh):
    placed = (P("gy", "gx", None), P(), P())
    return jax.shard_map(
        on_device, mesh=mesh, in_specs=placed, out_specs=(P("gy", "gx", None), P()), check_vma=False
    )
```

profile of v0, /device:TPU:1, one launch (start us, length us, event | category | flops | bytes accessed | tf_op | source)
XLA Modules:
  0.0 706.7 jit_solution(8181683742213125717)
XLA Ops:
  7.2 1.1 fusion.75
  8.4 4.9 collective-permute-start
  13.3 1.9 collective-permute-start.1
  15.2 1.4 collective-permute-done
  16.6 8.9 %constant_dynamic-update-slice_fusion.1 = bf16[66,32,4096]{2,1,0:T(8,128)(2,1)S(1)} fusion(bf16[66,32,4096]{2,1,0:T(8,128)(2,1)S(1)} %constant_dynamic-update-slice_fusion.2, bf16[64,32,4096]{2,1,0:T(8,128)(2,1)} %param.6), kind=kLoop, calls=%fused_computation.126 | loop fusion | bytes 33554432
  26.3 5.9 copy-done.2
  32.2 2.4 fusion.74
  35.8 1.3 collective-permute-start.3
  37.1 4.0 collective-permute-start.2
  41.8 7.2 %collective-permute-done.3 = bf16[66,1,4096]{2,0,1:T(8,128)(2,1)S(1)} collective-permute-done((bf16[66,1,4096]{2,0,1:T(8,128)(2,1)S(1)}, bf16[66,1,4096]{2,0,1:T(8,128)(2,1)S(1)}, u32[]{:S(2)}, u32[]{:S(2)}) %collective-permute-start.3) | collective-permute-done | bytes 540704 | tf_op jit(solution)/shard_map/ppermute | solution.py:23
  49.0 1.2 copy.149
  50.8 1.2 copy.147
  52.0 71.8 %add_convert_fusion = bf16[64,32,4096]{2,1,0:T(8,128)(2,1)} fusion(bf16[64,32,4096]{2,1,0:T(8,128)(2,1)} %param.6, bf16[66,32,4096]{2,1,0:T(8,128)(2,1)} %copy-done.2, bf16[66,1,4096]{2,1,0:T(2,128)(2,1)S(1)} %copy.149, bf16[66,1,4096]{2,1,0:T(2,128)(2,1)S(1)} %copy.147, bf16[1,32,4096]{2,1,0:T(8,128)(2,1)} %copy-done.3, ...), kind=kLoop, calls=%fused_computation | loop fusion | flops 427819008 | bytes 52609024 | tf_op jit(solution)/shard_map/convert_element_type | solution.py:36
  123.8 8.1 %fusion.77 = f32[2048,128]{1,0:T(8,128)S(1)} fusion(bf16[2048,4096]{1,0:T(8,128)(2,1)} %bitcast.162, bf16[4096,128]{1,0:T(8,128)(2,1)S(1)} %copy-done), kind=kOutput, calls=%fused_computation.147 | convolution fusion | flops 2147483648 | bytes 18874368 | tf_op jit(solution)/shard_map/dot_general | solution.py:83
  131.9 1.8 fusion.78
  133.8 11.7 %cholesky.254 = f32[128,128]{1,0:T(8,128)S(1)} custom-call(f32[128,128]{1,0:T(8,128)S(1)} %fusion.29), custom_call_target="Cholesky" | custom-call | tf_op jit(solution)/shard_map/jit(cholesky)/cholesky | solution.py:69
  148.8 11.7 %cholesky.265 = f32[128,128]{1,0:T(8,128)S(1)} custom-call(f32[128,128]{1,0:T(8,128)S(1)} %fusion.28), custom_call_target="Cholesky" | custom-call | tf_op jit(solution)/shard_map/jit(cholesky)/cholesky | solution.py:52
  161.9 5.2 collective-permute-start.5
  167.4 1.9 collective-permute-done.5
  169.6 11.7 %cholesky.276 = f32[128,128]{1,0:T(8,128)S(1)} custom-call(f32[128,128]{1,0:T(8,128)S(1)} %fusion.27), custom_call_target="Cholesky" | custom-call | tf_op jit(solution)/shard_map/jit(cholesky)/cholesky | solution.py:52
  182.7 3.2 collective-permute-start.6
  186.1 1.7 collective-permute-done.6
  188.1 11.7 %cholesky.287 = f32[128,128]{1,0:T(8,128)S(1)} custom-call(f32[128,128]{1,0:T(8,128)S(1)} %fusion.26), custom_call_target="Cholesky" | custom-call | tf_op jit(solution)/shard_map/jit(cholesky)/cholesky | solution.py:52
  201.2 2.3 collective-permute-start.7
  203.7 1.4 collective-permute-done.7
  205.5 11.7 %cholesky.298 = f32[128,128]{1,0:T(8,128)S(1)} custom-call(f32[128,128]{1,0:T(8,128)S(1)} %fusion.25), custom_call_target="Cholesky" | custom-call | tf_op jit(solution)/shard_map/jit(cholesky)/cholesky | solution.py:52
  218.6 3.9 collective-permute-start.8
  222.7 1.4 collective-permute-done.8
  224.4 11.7 %cholesky.309 = f32[128,128]{1,0:T(8,128)S(1)} custom-call(f32[128,128]{1,0:T(8,128)S(1)} %fusion.24), custom_call_target="Cholesky" | custom-call | tf_op jit(solution)/shard_map/jit(cholesky)/cholesky | solution.py:52
  237.5 5.2 collective-permute-start.9
  243.0 1.4 collective-permute-done.9
  244.7 11.7 %cholesky.320 = f32[128,128]{1,0:T(8,128)S(1)} custom-call(f32[128,128]{1,0:T(8,128)S(1)} %fusion.23), custom_call_target="Cholesky" | custom-call | tf_op jit(solution)/shard_map/jit(cholesky)/cholesky | solution.py:52
  257.8 3.4 collective-permute-start.10
  261.4 1.4 collective-permute-done.10
  263.2 11.7 %cholesky.331 = f32[128,128]{1,0:T(8,128)S(1)} custom-call(f32[128,128]{1,0:T(8,128)S(1)} %fusion.22), custom_call_target="Cholesky" | custom-call | tf_op jit(solution)/shard_map/jit(cholesky)/cholesky | solution.py:52
  276.3 9.8 %custom-call.6 = f32[1,128,128]{1,2,0:T(8,128)S(1)} custom-call(f32[1,128,128]{2,1,0:T(8,128)S(1)} %fusion.10), custom_call_target="InvertDiagBlocksLowerTriangular" | custom-call | tf_op jit(solution)/shard_map/triangular_solve/custom-call.0 | solution.py:71
  286.1 1.1 fusion.5
  287.2 8.1 %fusion.86 = f32[128,4096]{1,0:T(8,128)S(1)} fusion(bf16[2048,128]{0,1:T(8,128)(2,1)S(1)} %fusion.5, bf16[2048,4096]{1,0:T(8,128)(2,1)} %bitcast.163), kind=kOutput, calls=%fused_computation.156 | convolution fusion | flops 2147483648 | bytes 19398656 | tf_op jit(solution)/shard_map/dot_general | solution.py:86
  295.3 81.9 %all-reduce.4 = bf16[128,4096]{1,0:T(8,128)(2,1)S(1)} all-reduce(f32[128,4096]{1,0:T(8,128)S(1)} %fusion.86), channel_id=1, replica_groups=mesh['gy'=8,'gx'=16] {'gy','gx'}, use_global_device_ids=true, to_apply=%region_2.5 | all-reduce | flops 524288 | bytes 3145728 | tf_op jit(solution)/shard_map/psum | solution.py:85
  377.2 8.1 %fusion.95 = f32[2048,128]{1,0:T(8,128)S(1)} fusion(bf16[2048,4096]{1,0:T(8,128)(2,1)} %bitcast.164, bf16[128,4096]{1,0:T(8,128)(2,1)S(1)} %all-reduce.4), kind=kOutput, calls=%fused_computation.165 | convolution fusion | flops 2147483648 | bytes 18874368 | tf_op jit(solution)/shard_map/dot_general | solution.py:89
  385.3 1.8 fusion.87
  387.3 11.7 %cholesky.342 = f32[128,128]{1,0:T(8,128)S(1)} custom-call(f32[128,128]{1,0:T(8,128)S(1)} %fusion.20), custom_call_target="Cholesky" | custom-call | tf_op jit(solution)/shard_map/jit(cholesky)/cholesky | solution.py:69
  402.2 11.7 %cholesky.353 = f32[128,128]{1,0:T(8,128)S(1)} custom-call(f32[128,128]{1,0:T(8,128)S(1)} %fusion.19), custom_call_target="Cholesky" | custom-call | tf_op jit(solution)/shard_map/jit(cholesky)/cholesky | solution.py:52
  415.8 3.0 collective-permute-done.12
  419.2 11.7 %cholesky.364 = f32[128,128]{1,0:T(8,128)S(1)} custom-call(f32[128,128]{1,0:T(8,128)S(1)} %fusion.18), custom_call_target="Cholesky" | custom-call | tf_op jit(solution)/shard_map/jit(cholesky)/cholesky | solution.py:52
  432.3 2.2 collective-permute-start.13
  434.8 2.4 collective-permute-done.13
  437.6 11.7 %cholesky.375 = f32[128,128]{1,0:T(8,128)S(1)} custom-call(f32[128,128]{1,0:T(8,128)S(1)} %fusion.17), custom_call_target="Cholesky" | custom-call | tf_op jit(solution)/shard_map/jit(cholesky)/cholesky | solution.py:52
  451.2 2.6 collective-permute-done.14
  454.2 11.7 %cholesky.386 = f32[128,128]{1,0:T(8,128)S(1)} custom-call(f32[128,128]{1,0:T(8,128)S(1)} %fusion.16), custom_call_target="Cholesky" | custom-call | tf_op jit(solution)/shard_map/jit(cholesky)/cholesky | solution.py:52
  467.3 2.4 collective-permute-start.15
  469.9 2.4 collective-permute-done.15
  472.8 11.7 %cholesky.397 = f32[128,128]{1,0:T(8,128)S(1)} custom-call(f32[128,128]{1,0:T(8,128)S(1)} %fusion.15), custom_call_target="Cholesky" | custom-call | tf_op jit(solution)/shard_map/jit(cholesky)/cholesky | solution.py:52
  486.5 2.5 collective-permute-done.16
  489.4 11.7 %cholesky.408 = f32[128,128]{1,0:T(8,128)S(1)} custom-call(f32[128,128]{1,0:T(8,128)S(1)} %fusion.14), custom_call_target="Cholesky" | custom-call | tf_op jit(solution)/shard_map/jit(cholesky)/cholesky | solution.py:52
  502.4 2.3 collective-permute-start.17
  505.0 2.4 collective-permute-done.17
  507.7 11.7 %cholesky.419 = f32[128,128]{1,0:T(8,128)S(1)} custom-call(f32[128,128]{1,0:T(8,128)S(1)} %fusion.13), custom_call_target="Cholesky" | custom-call | tf_op jit(solution)/shard_map/jit(cholesky)/cholesky | solution.py:52
  520.8 9.8 %custom-call.7 = f32[1,128,128]{1,2,0:T(8,128)S(1)} custom-call(f32[1,128,128]{2,1,0:T(8,128)S(1)} %fusion.11), custom_call_target="InvertDiagBlocksLowerTriangular" | custom-call | tf_op jit(solution)/shard_map/triangular_solve/custom-call.0 | solution.py:71
  530.6 1.1 fusion.4
  531.7 9.4 %fusion.8 = f32[128,4096]{1,0:T(8,128)} fusion(bf16[2048,4096]{1,0:T(8,128)(2,1)} %bitcast.165, f32[2048,128]{0,1:T(8,128)S(1)} %fusion.4), kind=kOutput, calls=%fused_computation.38 | convolution fusion | flops 2147745792 | bytes 19922944 | tf_op jit(solution)/shard_map/dot_general | solution.py:92
  541.1 1.3 copy.194
  542.4 154.1 %all-reduce.3.cloned.1.call-done = f32[128,4096]{1,0:T(8,128)} async-done(((f32[128,4096]{1,0:T(8,128)}), f32[128,4096]{1,0:T(8,128)}) %all-reduce.3.cloned.1.call-update) | async-done | bytes 2097168 | tf_op jit(solution)/shard_map/psum | solution.py:93
  696.6 3.1 broadcast_multiply_fusion
  (133 shorter events, 37.2 us)
Async XLA Ops:
  7.2 116.6 %copy-start = (bf16[4096,128]{1,0:T(8,128)(2,1)S(1)}, bf16[4096,128]{1,0:T(8,128)(2,1)}, u32[]{:S(2)}) copy-start(bf16[4096,128]{1,0:T(8,128)(2,1)} %param.8) | copy-start | bytes 3145732
  7.2 689.4 %all-reduce.3.cloned.1.call-start = ((), (), s32[]{:S(2)}) async-start(), calls=%async_computation | async-start | bytes 4194304 | tf_op jit(solution)/shard_map/psum | solution.py:93
  8.4 8.2 %collective-permute-start = (bf16[1,32,4096]{2,1,0:T(8,128)(2,1)S(1)}, bf16[1,32,4096]{2,1,0:T(8,128)(2,1)S(1)}, u32[]{:S(2)}, u32[]{:S(2)}) collective-permute-start(bf16[1,32,4096]{2,1,0:T(8,128)(2,1)S(1)} %get-tuple-element.9), channel_id=1, source_target_pairs={{0,16},{16,32},{32,48},{48,64},{64,80},{80,96},{96,112},{1,17},{17... | collective-permute-start | bytes 786440 | tf_op jit(solution)/shard_map/ppermute | solution.py:22
  13.3 12.2 %collective-permute-start.1 = (bf16[1,32,4096]{2,1,0:T(8,128)(2,1)S(1)}, bf16[1,32,4096]{2,1,0:T(8,128)(2,1)S(1)}, u32[]{:S(2)}, u32[]{:S(2)}) collective-permute-start(bf16[1,32,4096]{2,1,0:T(8,128)(2,1)S(1)} %get-tuple-element.8), channel_id=1, source_target_pairs={{16,0},{32,16},{48,32},{64,48},{80,64},{96,80},{112,96},{17,1},{33... | collective-permute-start | bytes 786440 | tf_op jit(solution)/shard_map/ppermute | solution.py:23
  16.6 24.5 %copy-start.4 = (f32[3,3,4096]{2,1,0:T(4,128)S(1)}, f32[3,3,4096]{2,1,0:T(4,128)}, u32[]{:S(2)}) copy-start(f32[3,3,4096]{2,1,0:T(4,128)} %param.7) | copy-start | bytes 442372
  25.5 0.7 copy-start.3
  26.3 5.9 copy-start.2
  35.8 13.2 %collective-permute-start.3 = (bf16[66,1,4096]{2,0,1:T(8,128)(2,1)S(1)}, bf16[66,1,4096]{2,0,1:T(8,128)(2,1)S(1)}, u32[]{:S(2)}, u32[]{:S(2)}) collective-permute-start(bf16[66,1,4096]{2,0,1:T(8,128)(2,1)S(1)} %copy.148), channel_id=1, source_target_pairs={{1,0},{2,1},{3,2},{4,3},{5,4},{6,5},{7,6},{8,7},{9,8},{10,9},{11,1... | collective-permute-start | bytes 1622024 | tf_op jit(solution)/shard_map/ppermute | solution.py:23
  37.1 13.7 %collective-permute-start.2 = (bf16[66,1,4096]{2,0,1:T(8,128)(2,1)S(1)}, bf16[66,1,4096]{2,0,1:T(8,128)(2,1)S(1)}, u32[]{:S(2)}, u32[]{:S(2)}) collective-permute-start(bf16[66,1,4096]{2,0,1:T(8,128)(2,1)S(1)} %copy.146), channel_id=1, source_target_pairs={{0,1},{1,2},{2,3},{3,4},{4,5},{5,6},{6,7},{7,8},{8,9},{9,10},{10,1... | collective-permute-start | bytes 1622024 | tf_op jit(solution)/shard_map/ppermute | solution.py:22
  146.9 1.5 collective-permute-start.4
  161.9 7.3 %collective-permute-start.5 = (f32[128,128]{1,0:T(8,128)S(1)}, f32[128,128]{1,0:T(8,128)S(1)}, u32[]{:S(2)}, u32[]{:S(2)}) collective-permute-start(f32[128,128]{1,0:T(8,128)S(1)} %fusion.35), channel_id=1, source_target_pairs={{0,32},{16,48},{32,0},{48,16},{64,96},{80,112},{96,64},{112,80},{1... | collective-permute-start | bytes 196616 | tf_op jit(solution)/shard_map/ppermute | solution.py:12
  182.7 5.1 collective-permute-start.6
  201.2 3.9 collective-permute-start.7
  218.6 5.5 collective-permute-start.8
  237.5 6.9 collective-permute-start.9
  257.8 5.0 collective-permute-start.10
  400.3 1.5 collective-permute-start.11
  415.3 3.6 collective-permute-start.12
  432.3 4.9 collective-permute-start.13
  450.6 3.2 collective-permute-start.14
  467.3 5.1 collective-permute-start.15
  485.8 3.2 collective-permute-start.16
  502.4 4.9 collective-permute-start.17
  520.8 178.9 %copy-start.1 = (bf16[4096,128]{1,0:T(8,128)(2,1)S(1)}, bf16[4096,128]{1,0:T(8,128)(2,1)}, u32[]{:S(2)}) copy-start(bf16[4096,128]{1,0:T(8,128)(2,1)} %param.8) | copy-start | bytes 3145732
Sparse Core Ops, SparseCore 0:
  541.2 155.2 all-reduce.2
where the time goes:
time: 711 us; the launch traced here: 707 us
  other arithmetic  303 us (43%)
  waiting for transfers between devices  190 us (27%)
  blocking collectives  81.9 us (12%)
  matrix products  46.9 us (7%)
  starting transfers between devices  43.8 us (6%)
  local copies, waits for them, and re-layouts  26.1 us (4%)
  between operations  14.9 us (2%)
    another operation x42, other arithmetic, combine_pair(): return jnp.linalg.cholesky(joined)  173 us
    psum x1, waiting for transfers between devices, on_device(): lax.psum(projected, ('gy', 'gx')) * (math.sqrt(channels) / pixel_count)  154 us
    psum x1, blocking collectives, on_device(): lax.psum(jnp.dot(first_basis.T, flattened, preferred_element_type=jnp.flo...  81.9 us
    convert_element_type x1, other arithmetic, smooth_block(): return summed.astype(jnp.bfloat16)  71.8 us
    ppermute x14, starting transfers between devices, from_partner(): return lax.ppermute(value, axis, pairs)  31.6 us
    ppermute x14, waiting for transfers between devices, from_partner(): return lax.ppermute(value, axis, pairs)  26.4 us
    another operation x6, other arithmetic, factor_basis(): triangle = jnp.linalg.cholesky(local_gram)  24.8 us
    another operation x4, other arithmetic, factor_basis(): lax.linalg.triangular_solve(triangle, values, left_side=False, lower=True...  20.9 us
  transfers between devices with their start and end apart: 19, of which 18 were waited for; matrix products, arithmetic and copies ran while one was open for 2% of the time, Pallas kernels for 0%

commit v1 on v0

v1 whole, which is shorter than its diff:
```python
import math

import jax
import jax.numpy as jnp
from jax import lax
from jax.experimental import pallas as pl
from jax.experimental.pallas import tpu as pltpu
from jax.sharding import PartitionSpec as P

HIGH = lax.Precision.HIGHEST
BOTH = ("gy", "gx")


def xor_permute(value, axis, mask):
    return lax.ppermute(value, axis, [(i, i ^ mask) for i in range(lax.axis_size(axis))])


def shift_permute(value, axis, step):
    devices = lax.axis_size(axis)
    pairs = [(i, i + step) for i in range(devices) if 0 <= i + step < devices]
    return lax.ppermute(value, axis, pairs)


def params(mib, axes=0):
    return pltpu.CompilerParams(
        vmem_limit_bytes=mib << 20, dimension_semantics=("arbitrary",) * axes if axes else None
    )


def smooth_body(
    x_ref, top_ref, bot_ref, left_ref, right_ref, cl_ref, cr_ref, kern_ref, test_ref,
    flat_ref, sketch_ref, gram_ref, lt_ref, rt_ref,
):
    step, steps = pl.program_id(0), pl.num_programs(0)
    rows, cols, width = x_ref.shape
    f32 = jnp.float32

    def side(edge_ref, corner_ref, b):
        edge = edge_ref[...].astype(f32)
        corner = corner_ref[...].astype(f32)
        above = jnp.concatenate([corner[0:1], edge[:-1]], axis=0)
        below = jnp.concatenate([edge[1:], corner[1:2]], axis=0)
        taps = [kern_ref[3 * a + b : 3 * a + b + 1, :] for a in range(3)]
        return taps[0] * above + taps[1] * edge + taps[2] * below

    lt_ref[...] = side(left_ref, cl_ref, 0)
    rt_ref[...] = side(right_ref, cr_ref, 2)
    group = 8
    place = lax.broadcasted_iota(jnp.int32, (cols, 128), 0)
    for chunk in range(width // 128):
        lanes = slice(chunk * 128, chunk * 128 + 128)
        taps = [jnp.broadcast_to(kern_ref[i : i + 1, lanes], (cols, 128)) for i in range(9)]

        def body(g, carry, lanes=lanes, taps=taps):
            prev, here = carry
            start = pl.multiple_of(g * group, group)
            lefts = lt_ref[pl.ds(start, group), lanes]
            rights = rt_ref[pl.ds(start, group), lanes]
            for r in range(group):
                h = g * group + r
                if r == group - 1:
                    last = g == rows // group - 1
                    after = x_ref[jnp.minimum(h + 1, rows - 1), :, lanes]
                    after = jnp.where(last, bot_ref[:, lanes], after)
                else:
                    after = x_ref[h + 1, :, lanes]
                after = after.astype(f32)
                t = [taps[b] * prev + taps[3 + b] * here + taps[6 + b] * after for b in range(3)]
                left = jnp.where(place == 0, lefts[r : r + 1], pltpu.roll(t[0], 1, 0))
                right = jnp.where(
                    place == cols - 1, rights[r : r + 1], pltpu.roll(t[2], cols - 1, 0)
                )
                total = t[1] + left + right
                start = pl.multiple_of(h * cols, cols)
                flat_ref[pl.ds(start, cols), lanes] = total.astype(jnp.bfloat16)
                prev, here = here, after
            return prev, here

        first = (top_ref[:, lanes].astype(f32), x_ref[0, :, lanes].astype(f32))
        lax.fori_loop(0, rows // group, body, first)

    part = jnp.dot(flat_ref[...], test_ref[...], preferred_element_type=f32)

    @pl.when(step == 0)
    def _():
        sketch_ref[...] = part

    @pl.when(step > 0)
    def _():
        sketch_ref[...] += part

    @pl.when(step == steps - 1)
    def _():
        values = sketch_ref[...]
        gram_ref[...] = lax.dot_general(
            values, values, (((0,), (0,)), ((), ())), precision=HIGH, preferred_element_type=f32
        )


def smooth_sketch(x, halos, kernel, test_matrix):
    rows, cols, channels = x.shape
    k = test_matrix.shape[1]
    width = 512
    edge = lambda n: pl.BlockSpec((n, width), lambda j: (0, j))
    return pl.pallas_call(
        smooth_body,
        grid=(channels // width,),
        in_specs=[
            pl.BlockSpec((rows, cols, width), lambda j: (0, 0, j)),
            edge(cols), edge(cols), edge(rows), edge(rows), edge(2), edge(2), edge(9),
            pl.BlockSpec((width, k), lambda j: (j, 0)),
        ],
        out_specs=[
            pl.BlockSpec((rows * cols, width), lambda j: (0, j)),
            pl.BlockSpec((rows * cols, k), lambda j: (0, 0)),
            pl.BlockSpec((k, k), lambda j: (0, 0)),
        ],
        out_shape=[
            jax.ShapeDtypeStruct((rows * cols, channels), jnp.bfloat16),
            jax.ShapeDtypeStruct((rows * cols, k), jnp.float32),
            jax.ShapeDtypeStruct((k, k), jnp.float32),
        ],
        scratch_shapes=[pltpu.VMEM((rows, width), jnp.float32)] * 2,
        compiler_params=params(40, 1),
        name="smooth_sketch",
    )(x, *halos, kernel.reshape(9, channels), test_matrix)


def inverse_factor(gram, work_ref):
    n = gram.shape[0]
    f32 = jnp.float32
    row_id = lax.broadcasted_iota(jnp.int32, (n, n), 0)
    col_id = lax.broadcasted_iota(jnp.int32, (n, n), 1)
    work_ref[:, :n] = gram
    work_ref[:, n:] = (row_id == col_id).astype(f32)
    sub = lax.broadcasted_iota(jnp.int32, (8, 2 * n), 0)
    sub1 = lax.broadcasted_iota(jnp.int32, (8, 1), 0)
    for p in range(n // 8):
        panel = work_ref[8 * p : 8 * p + 8, :]
        for i in range(8):
            c = 8 * p + i
            column = panel[:, c : c + 1]
            scale = lax.rsqrt(column[i : i + 1])
            row = panel[i : i + 1, :] * scale
            factor = jnp.where(sub1 > i, column * scale, 0.0)
            panel = jnp.where(sub == i, row, panel - factor * row)
        work_ref[8 * p : 8 * p + 8, :] = panel
        rest = 8 * p + 8
        if rest < n:
            update = lax.dot_general(
                panel[:, :n], panel, (((0,), (0,)), ((), ())),
                precision=HIGH, preferred_element_type=f32,
            )
            work_ref[rest:, :] -= update[rest:, :]
    return jnp.where(row_id >= col_id, work_ref[:, n:], 0.0)


def times_transposed(values, matrix):
    return lax.dot_general(
        values, matrix, (((1,), (1,)), ((), ())), precision=HIGH,
        preferred_element_type=jnp.float32,
    )


def project_body(core_ref, gram_ref, sketch_ref, flat_ref, out_ref, work_ref, basis_ref):
    @pl.when(pl.program_id(0) == 0)
    def _():
        inverse = inverse_factor(gram_ref[...], work_ref)
        basis = times_transposed(sketch_ref[...], inverse)
        basis_ref[...] = basis.astype(jnp.bfloat16).T

    product = jnp.dot(basis_ref[...], flat_ref[...], preferred_element_type=jnp.float32)
    out_ref[0] = product.T


def project(core, gram, sketch, flat):
    pixels, channels = flat.shape
    k = gram.shape[0]
    width = 512
    half = channels // width // 2
    whole = lambda *shape: pl.BlockSpec(shape, lambda j, core: (0,) * len(shape))
    return pl.pallas_call(
        project_body,
        grid_spec=pltpu.PrefetchScalarGridSpec(
            num_scalar_prefetch=1,
            grid=(channels // width,),
            in_specs=[
                whole(k, k), whole(pixels, k),
                pl.BlockSpec((pixels, width), lambda j, core: (0, j)),
            ],
            out_specs=pl.BlockSpec(
                (1, width, k), lambda j, core: ((j // half) ^ core[0], j % half, 0)
            ),
            scratch_shapes=[
                pltpu.VMEM((k, 2 * k), jnp.float32), pltpu.VMEM((k, pixels), jnp.bfloat16),
            ],
        ),
        out_shape=jax.ShapeDtypeStruct((2, channels // 2, k), jnp.float32),
        compiler_params=params(40, 1),
        name="project",
    )(core, gram, sketch, flat)


def second_body(core_ref, flat_ref, range_ref, second_ref, out_ref, acc_ref):
    step, steps = pl.program_id(0), pl.num_programs(0)
    f32, bf16 = jnp.float32, jnp.bfloat16
    k = range_ref.shape[1]
    values = jnp.dot(flat_ref[...], range_ref[...], preferred_element_type=f32)
    second_ref[...] = values
    high = values.astype(bf16)
    low = (values - high.astype(f32)).astype(bf16)
    both = jnp.concatenate([high, low], axis=1).T

    @pl.when(step == 0)
    def _():
        acc_ref[...] = jnp.dot(both, flat_ref[...], preferred_element_type=f32)

    @pl.when(step > 0)
    def _():
        acc_ref[...] += jnp.dot(both, flat_ref[...], preferred_element_type=f32)

    @pl.when(step == steps - 1)
    def _():
        half = out_ref.shape[1]
        for part in range(2):
            lanes = slice(part * half, part * half + half)
            out_ref[part ^ core_ref[0]] = (acc_ref[:k, lanes] + acc_ref[k:, lanes]).T


def second_step(core, flat, range_map):
    pixels, channels = flat.shape
    k = range_map.shape[1]
    height = 512
    return pl.pallas_call(
        second_body,
        grid_spec=pltpu.PrefetchScalarGridSpec(
            num_scalar_prefetch=1,
            grid=(pixels // height,),
            in_specs=[
                pl.BlockSpec((height, channels), lambda i, core: (i, 0)),
                pl.BlockSpec((channels, k), lambda i, core: (0, 0)),
            ],
            out_specs=[
                pl.BlockSpec((height, k), lambda i, core: (i, 0)),
                pl.BlockSpec((2, channels // 2, k), lambda i, core: (0, 0, 0)),
            ],
            scratch_shapes=[pltpu.VMEM((2 * k, channels), jnp.float32)],
        ),
        out_shape=[
            jax.ShapeDtypeStruct((pixels, k), jnp.float32),
            jax.ShapeDtypeStruct((2, channels // 2, k), jnp.float32),
        ],
        compiler_params=params(44, 1),
        name="second_step",
    )(core, flat, range_map)


def finish_body(basis_scale, coeff_scale, range_ref, moment_ref, second_ref, basis_ref, coeffs_ref, work_ref):
    moment = moment_ref[...]
    gram = lax.dot_general(
        range_ref[...].astype(jnp.float32), moment, (((0,), (0,)), ((), ())), precision=HIGH,
        preferred_element_type=jnp.float32,
    )
    inverse = inverse_factor(gram, work_ref)
    basis_ref[...] = times_transposed(second_ref[...], inverse) * basis_scale
    coeffs_ref[...] = times_transposed(inverse, moment) * coeff_scale


def finish(range_map, moment, second, basis_scale, coeff_scale):
    channels, k = moment.shape

    def body(*refs):
        finish_body(basis_scale, coeff_scale, *refs)

    return pl.pallas_call(
        body,
        out_shape=[
            jax.ShapeDtypeStruct(second.shape, jnp.float32),
            jax.ShapeDtypeStruct((k, channels), jnp.float32),
        ],
        scratch_shapes=[pltpu.VMEM((k, 2 * k), jnp.float32)],
        compiler_params=params(40),
        name="finish",
    )(range_map, moment, second)


def all_sum(pair, core, dtype):
    gy, gx = lax.axis_size("gy"), lax.axis_size("gx")
    groups = [[y * gx + x for y in range(c, gy, 2) for x in range(gx)] for c in range(2)]
    half, k = pair.shape[1:]
    members = gy * gx // 2
    swap = lambda v: lax.all_to_all(v, BOTH, 0, 0, axis_index_groups=groups, tiled=True)
    mine = pair[0] + xor_permute(pair[1], "gy", 1)
    parts = swap(mine.reshape(members, half // members, k))
    chunk = jnp.sum(parts, axis=0).astype(dtype)
    chunk = lax.optimization_barrier(chunk)
    whole = swap(jnp.broadcast_to(chunk[None], (members,) + chunk.shape)).reshape(half, k)
    other = xor_permute(whole, "gy", 1)
    first, last = jnp.where(core == 0, whole, other), jnp.where(core == 0, other, whole)
    return jnp.concatenate([first, last], axis=0)


def on_device(radiance, kernel, test_matrix):
    height, breadth, channels = radiance.shape
    devices = lax.axis_size("gy") * lax.axis_size("gx")
    pixel_count = height * breadth * devices
    core = lax.axis_index("gy") % 2
    core_arg = core.astype(jnp.int32).reshape(1)

    top = shift_permute(radiance[-1], "gy", 1)
    bottom = shift_permute(radiance[0], "gy", -1)
    left = shift_permute(radiance[:, -1], "gx", 1)
    right = shift_permute(radiance[:, 0], "gx", -1)
    rims = jnp.stack([top, bottom])
    left_ends = shift_permute(rims[:, -1], "gx", 1)
    right_ends = shift_permute(rims[:, 0], "gx", -1)
    halos = (top, bottom, left, right, left_ends, right_ends)

    flat, sketch, gram = smooth_sketch(radiance, halos, kernel, test_matrix)
    for axis, mask in (("gy", 1), ("gx", 1), ("gx", 3), ("gx", 4), ("gx", 12), ("gy", 2), ("gy", 6)):
        gram = gram + xor_permute(gram, axis, mask)
    range_map = all_sum(project(core_arg, gram, sketch, flat), core, jnp.bfloat16)
    second, pair = second_step(core_arg, flat, range_map)
    moment = all_sum(pair, core, jnp.float32)
    scale = math.sqrt(pixel_count)
    basis_out, coeffs = finish(
        range_map, moment, second, scale, scale * math.sqrt(channels) / pixel_count
    )
    return (basis_out.reshape(height, breadth, basis_out.shape[1]), coeffs)


def solution(mesh):
    placed = (P("gy", "gx", None), P(), P())
    return jax.shard_map(
        on_device, mesh=mesh, in_specs=placed, out_specs=(P("gy", "gx", None), P()), check_vma=False
    )
```

time: 711 us -> 274 us (0.39)
  other arithmetic: 303 us -> 1 us
  waiting for transfers between devices: 190 us -> 28.3 us
  Pallas kernels: 0 us -> 101 us
  matrix products: 46.9 us -> 0 us
  between operations: 14.9 us -> 0.86 us
  local copies, waits for them, and re-layouts: 26.1 us -> 12.7 us
    another operation x52 -> x0, other arithmetic: 219 us -> none  [the longest x42 173 us: combine_pair(): return jnp.linalg.cholesky(joined)]
    psum x1 -> x0, waiting for transfers between devices: 154 us -> none  [on_device(): lax.psum(projected, ('gy', 'gx')) * (math.sqrt(channels) / pixel_count)]
    pallas_call x0 -> x4, Pallas kernels: none -> 101 us  [the longest x1 40.2 us: smooth_sketch(): pl.pallas_call(smooth_body, grid=(channels // width,), in_specs=[pl.Block...]
    all_to_all x0 -> x4, blocking collectives: none -> 85.4 us  [all_sum(): lax.all_to_all(v, BOTH, 0, 0, axis_index_groups=groups, tiled=True)]
    psum x1 -> x0, blocking collectives: 81.9 us -> none  [on_device(): lax.psum(jnp.dot(first_basis.T, flattened, preferred_element_type=jnp.flo...]
    convert_element_type x1 -> x0, other arithmetic: 71.8 us -> none  [smooth_block(): return summed.astype(jnp.bfloat16)]
    dot_general x34 -> x0, matrix products: 44.8 us -> none  [the longest x1 9.43 us: on_device(): jnp.dot(basis_half.T, flattened, preferred_element_type=jnp.float32)]
    unnamed x12 -> x8, local copies, waits for them, and re-layouts: 15.5 us -> 4.57 us
  transfers between devices with their start and end apart: 19 -> 17, of which waited for: 18 -> 13; matrix products, arithmetic and copies ran while one was open for 2% -> 3% of each run, Pallas kernels for 0% -> 0%
where the time goes in v1:
time: 274 us
  Pallas kernels  101 us (37%)
  blocking collectives  85.4 us (31%)
  starting transfers between devices  43.9 us (16%)
  waiting for transfers between devices  28.3 us (10%)
  local copies, waits for them, and re-layouts  12.7 us (5%)
    all_to_all x4, blocking collectives, all_sum(): lax.all_to_all(v, BOTH, 0, 0, axis_index_groups=groups, tiled=True)  85.4 us
    pallas_call x1, Pallas kernels, smooth_sketch(): pl.pallas_call(smooth_body, grid=(channels // width,), in_specs=[pl.Block...  40.2 us
    ppermute x11, starting transfers between devices, xor_permute(): lax.ppermute(value, axis, [(i, i ^ mask) for i in range(lax.axis_size(axi...  27.4 us
    pallas_call x1, Pallas kernels, project(): pl.pallas_call(project_body, grid_spec=pltpu.PrefetchScalarGridSpec(num_s...  26.5 us
    pallas_call x1, Pallas kernels, finish(): pl.pallas_call(body, out_shape=[jax.ShapeDtypeStruct(second.shape, jnp.fl...  21.6 us
    ppermute x11, waiting for transfers between devices, xor_permute(): lax.ppermute(value, axis, [(i, i ^ mask) for i in range(lax.axis_size(axi...  21.2 us
    ppermute x6, starting transfers between devices, shift_permute(): return lax.ppermute(value, axis, pairs)  16.5 us
    pallas_call x1, Pallas kernels, second_step(): pl.pallas_call(second_body, grid_spec=pltpu.PrefetchScalarGridSpec(num_sc...  13.1 us
  transfers between devices with their start and end apart: 17, of which 13 were waited for; matrix products, arithmetic and copies ran while one was open for 3% of the time, Pallas kernels for 0%

profile of v1, /device:TPU:1, one launch (start us, length us, event | category | flops | bytes accessed | tf_op | source)
XLA Modules:
  0.0 273.5 jit_solution(9322828274924780025)
XLA Ops:
  0.6 1.1 slice_bitcast_fusion.3
  1.7 3.3 %collective-permute-start.1 = (bf16[32,4096]{1,0:T(8,128)(2,1)S(1)}, bf16[32,4096]{1,0:T(8,128)(2,1)S(1)}, u32[]{:S(2)}, u32[]{:S(2)}) collective-permute-start(bf16[32,4096]{1,0:T(8,128)(2,1)S(1)} %get-tuple-element.18), channel_id=1, source_target_pairs={{16,0},{32,16},{48,32},{64,48},{80,64},{96,80},{112,96},{17,1},{33... | collective-permute-start | bytes 786440 | tf_op jit(solution)/shard_map/ppermute | solution.py:21
  5.0 3.6 %collective-permute-start = (bf16[32,4096]{1,0:T(8,128)(2,1)S(1)}, bf16[32,4096]{1,0:T(8,128)(2,1)S(1)}, u32[]{:S(2)}, u32[]{:S(2)}) collective-permute-start(bf16[32,4096]{1,0:T(8,128)(2,1)S(1)} %get-tuple-element.19), channel_id=1, source_target_pairs={{0,16},{16,32},{32,48},{48,64},{64,80},{80,96},{96,112},{1,17},{17... | collective-permute-start | bytes 786440 | tf_op jit(solution)/shard_map/ppermute | solution.py:21
  8.6 4.6 %fusion.2 = (bf16[64,1,4096]{2,1,0:T(2,128)(2,1)S(1)}, bf16[64,1,4096]{2,1,0:T(2,128)(2,1)S(1)}) fusion(bf16[64,32,4096]{2,1,0:T(8,128)(2,1)} %x_ref.1), kind=kLoop, calls=%fused_computation.18 | loop fusion | bytes 2097152 | tf_op jit(solution)/shard_map/slice | solution.py:313
  13.2 1.4 copy.16
  14.5 3.1 %collective-permute-start.2 = (bf16[64,4096]{1,0:T(8,128)(2,1)}, bf16[64,4096]{1,0:T(8,128)(2,1)S(1)}, u32[]{:S(2)}, u32[]{:S(2)}) collective-permute-start(bf16[64,4096]{1,0:T(8,128)(2,1)} %bitcast.35), channel_id=1, source_target_pairs={{0,1},{1,2},{2,3},{3,4},{4,5},{5,6},{6,7},{7,8},{8,9},{9,10},{10,1... | collective-permute-start | bytes 1572872 | tf_op jit(solution)/shard_map/ppermute | solution.py:21
  17.7 0.0 copy-start
  17.7 1.4 copy.15
  19.1 1.3 collective-permute-start.3
  20.4 0.0 collective-permute-done.1.bot_ref
  20.4 0.5 copy.10
  20.9 0.0 collective-permute-done.top_ref
  20.9 0.5 copy.9
  21.5 0.1 fusion.1
  21.6 4.0 %collective-permute-start.4 = (bf16[2,4096]{1,0:T(2,128)(2,1)S(1)}, bf16[2,4096]{1,0:T(2,128)(2,1)S(1)}, u32[]{:S(2)}, u32[]{:S(2)}) collective-permute-start(bf16[2,4096]{1,0:T(2,128)(2,1)S(1)} %get-tuple-element.25), channel_id=1, source_target_pairs={{0,1},{1,2},{2,3},{3,4},{4,5},{5,6},{6,7},{7,8},{8,9},{9,10},{10,1... | collective-permute-start | bytes 49160 | tf_op jit(solution)/shard_map/ppermute | solution.py:21
  25.6 1.3 collective-permute-start.5
  26.9 1.0 reshape.28.kern_ref
  27.9 1.5 collective-permute-done.4.cl_ref
  29.4 5.5 %collective-permute-done.5.cr_ref = bf16[2,4096]{1,0:T(2,128)(2,1)S(1)} collective-permute-done((bf16[2,4096]{1,0:T(2,128)(2,1)S(1)}, bf16[2,4096]{1,0:T(2,128)(2,1)S(1)}, u32[]{:S(2)}, u32[]{:S(2)}) %collective-permute-start.5) | collective-permute-done | bytes 16416 | tf_op jit(solution)/shard_map/ppermute | solution.py:21
  34.9 0.0 collective-permute-done.2.left_ref
  34.9 0.8 copy-done.1
  35.7 1.0 copy-done.2
  36.8 40.2 %smooth_sketch.1 = (bf16[2048,4096]{1,0:T(8,128)(2,1)}, f32[2048,128]{1,0:T(8,128)S(1)}, f32[128,128]{1,0:T(8,128)S(1)}) custom-call(bf16[64,32,4096]{2,1,0:T(8,128)(2,1)} %x_ref.1, bf16[32,4096]{1,0:T(8,128)(2,1)S(1)} %collective-permute-done.top_ref, bf16[32,4096]{1,0:T(8,128)(2,1)S(1)} %collective-permute-done.1.bot_ref, ...), custom_call_target="tpu_custom_call" | custom-call | tf_op jit(solution)/shard_map/smooth_sketch/pallas_call | solution.py:105
  77.0 0.4 collective-permute-start.6
  77.4 0.9 collective-permute-done.6
  78.3 1.3 collective-permute-start.7
  79.5 1.9 collective-permute-done.7
  81.5 4.6 %collective-permute-start.8 = (f32[128,128]{1,0:T(8,128)S(1)}, f32[128,128]{1,0:T(8,128)S(1)}, u32[]{:S(2)}, u32[]{:S(2)}) collective-permute-start(f32[128,128]{1,0:T(8,128)S(1)} %add.33), channel_id=1, source_target_pairs={{0,3},{1,2},{2,1},{3,0},{4,7},{5,6},{6,5},{7,4},{8,11},{9,10},{10,... | collective-permute-start | bytes 196616 | tf_op jit(solution)/shard_map/ppermute | solution.py:15
  86.1 1.7 collective-permute-done.8
  87.8 1.4 collective-permute-start.9
  89.2 1.8 collective-permute-done.9
  91.0 1.7 collective-permute-start.10
  92.7 2.7 collective-permute-done.10
  95.4 1.7 collective-permute-start.11
  97.1 2.0 collective-permute-done.11
  99.1 2.8 %collective-permute-start.12 = (f32[128,128]{1,0:T(8,128)S(1)}, f32[128,128]{1,0:T(8,128)S(1)}, u32[]{:S(2)}, u32[]{:S(2)}) collective-permute-start(f32[128,128]{1,0:T(8,128)S(1)} %add.37), channel_id=1, source_target_pairs={{0,96},{16,112},{32,64},{48,80},{64,32},{80,48},{96,0},{112,16},{1... | collective-permute-start | bytes 196616 | tf_op jit(solution)/shard_map/ppermute | solution.py:15
  101.9 1.8 collective-permute-done.12
  103.7 26.5 %project.1 = f32[2,2048,128]{2,1,0:T(8,128)S(1)} custom-call(s32[1]{0:T(128)} %bitcast.core_ref, f32[128,128]{1,0:T(8,128)S(1)} %add.38.gram_ref, f32[2048,128]{1,0:T(8,128)S(1)} %get-tuple-element.10.sketch_ref, bf16[2048,4096]{1,0:T(8,128)(2,1)} %get-tuple-element.11.flat_ref), custom_call_target="tpu_custom_call" | custom-call | tf_op jit(solution)/shard_map/project/pallas_call | solution.py:182
  130.1 0.1 slice_bitcast_fusion
  130.2 6.6 %collective-permute-start.13 = (f32[2048,128]{1,0:T(8,128)S(1)}, f32[2048,128]{1,0:T(8,128)S(1)}, u32[]{:S(2)}, u32[]{:S(2)}) collective-permute-start(f32[2048,128]{1,0:T(8,128)S(1)} %slice_bitcast_fusion), channel_id=1, source_target_pairs={{0,16},{16,0},{32,48},{48,32},{64,80},{80,64},{96,112},{112,96},{1... | collective-permute-start | bytes 3145736 | tf_op jit(solution)/shard_map/ppermute | solution.py:15
  136.8 2.3 collective-permute-done.13
  139.1 0.1 fusion
  139.2 26.6 %all_to_all.20 = f32[64,32,128]{2,1,0:T(8,128)S(1)} all-to-all(f32[64,32,128]{2,1,0:T(8,128)S(1)} %bitcast.39), channel_id=1, replica_groups={{0,1,2,3,4,5,6,7,8,9,10,11,12,13,14,15,32,33,34,35,36,37,38,39,40,41,42..., dimensions={0} | all-to-all | bytes 2097152 | tf_op jit(solution)/shard_map/all_to_all | solution.py:292
  165.8 0.1 reduce_sum.18
  165.9 0.1 broadcast_in_dim.4
  166.0 15.5 %all_to_all.21 = bf16[64,32,128]{2,1,0:T(8,128)(2,1)S(1)} all-to-all(bf16[64,32,128]{2,1,0:T(8,128)(2,1)S(1)} %broadcast_in_dim.4), channel_id=1, replica_groups={{0,1,2,3,4,5,6,7,8,9,10,11,12,13,14,15,32,33,34,35,36,37,38,39,40,41,42..., dimensions={0} | all-to-all | bytes 1048576 | tf_op jit(solution)/shard_map/all_to_all | solution.py:292
  181.5 3.1 %collective-permute-start.14 = (bf16[2048,128]{1,0:T(8,128)(2,1)S(1)}, bf16[2048,128]{1,0:T(8,128)(2,1)S(1)}, u32[]{:S(2)}, u32[]{:S(2)}) collective-permute-start(bf16[2048,128]{1,0:T(8,128)(2,1)S(1)} %bitcast.41), channel_id=1, source_target_pairs={{0,16},{16,0},{32,48},{48,32},{64,80},{80,64},{96,112},{112,96},{1... | collective-permute-start | bytes 1572872 | tf_op jit(solution)/shard_map/ppermute | solution.py:15
  184.6 1.5 collective-permute-done.14
  186.2 0.1 broadcast_select_fusion.3
  186.3 0.1 pad_maximum_fusion.1.range_ref.refs_0_
  186.3 13.1 %second_step.1 = (f32[2048,128]{1,0:T(8,128)S(1)}, f32[2,2048,128]{2,1,0:T(8,128)S(1)}) custom-call(s32[1]{0:T(128)} %bitcast.core_ref, bf16[2048,4096]{1,0:T(8,128)(2,1)} %get-tuple-element.11.flat_ref, bf16[4096,128]{1,0:T(8,128)(2,1)S(1)} %pad_maximum_fusion.1.range_ref.refs_0_), custom_call_target="tpu_custom_call" | custom-call | tf_op jit(solution)/shard_map/second_step/pallas_call | solution.py:234
  199.5 0.1 slice_bitcast_fusion.2
  199.6 0.7 collective-permute-start.15
  200.2 2.3 collective-permute-done.15
  202.5 0.1 bitcast_add_fusion
  202.6 22.3 %all_to_all.22 = f32[64,32,128]{2,1,0:T(8,128)S(1)} all-to-all(f32[64,32,128]{2,1,0:T(8,128)S(1)} %bitcast.40), channel_id=1, replica_groups={{0,1,2,3,4,5,6,7,8,9,10,11,12,13,14,15,32,33,34,35,36,37,38,39,40,41,42..., dimensions={0} | all-to-all | bytes 2097152 | tf_op jit(solution)/shard_map/all_to_all | solution.py:292
  225.0 0.1 reduce_sum.19
  225.1 0.1 broadcast_in_dim.5
  225.2 21.0 %all_to_all.23 = f32[64,32,128]{2,1,0:T(8,128)S(1)} all-to-all(f32[64,32,128]{2,1,0:T(8,128)S(1)} %broadcast_in_dim.5), channel_id=1, replica_groups={{0,1,2,3,4,5,6,7,8,9,10,11,12,13,14,15,32,33,34,35,36,37,38,39,40,41,42..., dimensions={0} | all-to-all | bytes 2097152 | tf_op jit(solution)/shard_map/all_to_all | solution.py:292
  246.2 3.2 %collective-permute-start.16 = (f32[2048,128]{1,0:T(8,128)S(1)}, f32[2048,128]{1,0:T(8,128)S(1)}, u32[]{:S(2)}, u32[]{:S(2)}) collective-permute-start(f32[2048,128]{1,0:T(8,128)S(1)} %bitcast.38), channel_id=1, source_target_pairs={{0,16},{16,0},{32,48},{48,32},{64,80},{80,64},{96,112},{112,96},{1... | collective-permute-start | bytes 3145736 | tf_op jit(solution)/shard_map/ppermute | solution.py:15
  249.3 2.3 collective-permute-done.16
  251.6 0.1 broadcast_select_fusion.1
  251.8 0.1 pad_maximum_fusion.refs_1_
  251.9 21.6 %finish.1 = (f32[2048,128]{1,0:T(8,128)}, f32[128,4096]{1,0:T(8,128)}) custom-call(bf16[4096,128]{1,0:T(8,128)(2,1)S(1)} %pad_maximum_fusion.1.range_ref.refs_0_, f32[4096,128]{1,0:T(8,128)S(1)} %pad_maximum_fusion.refs_1_, f32[2048,128]{1,0:T(8,128)S(1)} %get-tuple-element.13.refs_2_), custom_call_target="tpu_custom_call" | custom-call | tf_op jit(solution)/shard_map/finish/pallas_call | solution.py:275
  (11 shorter events, 0.1 us)
Async XLA Ops:
  1.7 18.7 %collective-permute-start.1 = (bf16[32,4096]{1,0:T(8,128)(2,1)S(1)}, bf16[32,4096]{1,0:T(8,128)(2,1)S(1)}, u32[]{:S(2)}, u32[]{:S(2)}) collective-permute-start(bf16[32,4096]{1,0:T(8,128)(2,1)S(1)} %get-tuple-element.18), channel_id=1, source_target_pairs={{16,0},{32,16},{48,32},{64,48},{80,64},{96,80},{112,96},{17,1},{33... | collective-permute-start | bytes 786440 | tf_op jit(solution)/shard_map/ppermute | solution.py:21
  5.0 15.9 %collective-permute-start = (bf16[32,4096]{1,0:T(8,128)(2,1)S(1)}, bf16[32,4096]{1,0:T(8,128)(2,1)S(1)}, u32[]{:S(2)}, u32[]{:S(2)}) collective-permute-start(bf16[32,4096]{1,0:T(8,128)(2,1)S(1)} %get-tuple-element.19), channel_id=1, source_target_pairs={{0,16},{16,32},{32,48},{48,64},{64,80},{80,96},{96,112},{1,17},{17... | collective-permute-start | bytes 786440 | tf_op jit(solution)/shard_map/ppermute | solution.py:21
  14.5 20.4 %collective-permute-start.2 = (bf16[64,4096]{1,0:T(8,128)(2,1)}, bf16[64,4096]{1,0:T(8,128)(2,1)S(1)}, u32[]{:S(2)}, u32[]{:S(2)}) collective-permute-start(bf16[64,4096]{1,0:T(8,128)(2,1)} %bitcast.35), channel_id=1, source_target_pairs={{0,1},{1,2},{2,3},{3,4},{4,5},{5,6},{6,7},{7,8},{8,9},{9,10},{10,1... | collective-permute-start | bytes 1572872 | tf_op jit(solution)/shard_map/ppermute | solution.py:21
  17.7 18.0 %copy-start = (bf16[4096,128]{1,0:T(8,128)(2,1)S(1)}, bf16[4096,128]{1,0:T(8,128)(2,1)}, u32[]{:S(2)}) copy-start(bf16[4096,128]{1,0:T(8,128)(2,1)} %test_ref.1) | copy-start | bytes 3145732
  19.1 15.8 %collective-permute-start.3 = (bf16[64,4096]{1,0:T(8,128)(2,1)}, bf16[64,4096]{1,0:T(8,128)(2,1)S(1)}, u32[]{:S(2)}, u32[]{:S(2)}) collective-permute-start(bf16[64,4096]{1,0:T(8,128)(2,1)} %bitcast.34), channel_id=1, source_target_pairs={{1,0},{2,1},{3,2},{4,3},{5,4},{6,5},{7,6},{8,7},{9,8},{10,9},{11,1... | collective-permute-start | bytes 1572872 | tf_op jit(solution)/shard_map/ppermute | solution.py:21
  21.6 7.8 %collective-permute-start.4 = (bf16[2,4096]{1,0:T(2,128)(2,1)S(1)}, bf16[2,4096]{1,0:T(2,128)(2,1)S(1)}, u32[]{:S(2)}, u32[]{:S(2)}) collective-permute-start(bf16[2,4096]{1,0:T(2,128)(2,1)S(1)} %get-tuple-element.25), channel_id=1, source_target_pairs={{0,1},{1,2},{2,3},{3,4},{4,5},{5,6},{6,7},{7,8},{8,9},{9,10},{10,1... | collective-permute-start | bytes 49160 | tf_op jit(solution)/shard_map/ppermute | solution.py:21
  25.6 9.3 %collective-permute-start.5 = (bf16[2,4096]{1,0:T(2,128)(2,1)S(1)}, bf16[2,4096]{1,0:T(2,128)(2,1)S(1)}, u32[]{:S(2)}, u32[]{:S(2)}) collective-permute-start(bf16[2,4096]{1,0:T(2,128)(2,1)S(1)} %get-tuple-element.24), channel_id=1, source_target_pairs={{1,0},{2,1},{3,2},{4,3},{5,4},{6,5},{7,6},{8,7},{9,8},{10,9},{11,1... | collective-permute-start | bytes 49160 | tf_op jit(solution)/shard_map/ppermute | solution.py:21
  34.9 0.8 copy-start.1
  35.7 1.0 copy-start.2
  77.0 1.3 collective-permute-start.6
  78.3 3.2 %collective-permute-start.7 = (f32[128,128]{1,0:T(8,128)S(1)}, f32[128,128]{1,0:T(8,128)S(1)}, u32[]{:S(2)}, u32[]{:S(2)}) collective-permute-start(f32[128,128]{1,0:T(8,128)S(1)} %add.32), channel_id=1, source_target_pairs={{0,1},{1,0},{2,3},{3,2},{4,5},{5,4},{6,7},{7,6},{8,9},{9,8},{10,11... | collective-permute-start | bytes 196616 | tf_op jit(solution)/shard_map/ppermute | solution.py:15
  81.5 6.3 %collective-permute-start.8 = (f32[128,128]{1,0:T(8,128)S(1)}, f32[128,128]{1,0:T(8,128)S(1)}, u32[]{:S(2)}, u32[]{:S(2)}) collective-permute-start(f32[128,128]{1,0:T(8,128)S(1)} %add.33), channel_id=1, source_target_pairs={{0,3},{1,2},{2,1},{3,0},{4,7},{5,6},{6,5},{7,4},{8,11},{9,10},{10,... | collective-permute-start | bytes 196616 | tf_op jit(solution)/shard_map/ppermute | solution.py:15
  87.8 3.2 %collective-permute-start.9 = (f32[128,128]{1,0:T(8,128)S(1)}, f32[128,128]{1,0:T(8,128)S(1)}, u32[]{:S(2)}, u32[]{:S(2)}) collective-permute-start(f32[128,128]{1,0:T(8,128)S(1)} %add.34), channel_id=1, source_target_pairs={{0,4},{1,5},{2,6},{3,7},{4,0},{5,1},{6,2},{7,3},{8,12},{9,13},{10,... | collective-permute-start | bytes 196616 | tf_op jit(solution)/shard_map/ppermute | solution.py:15
  91.0 4.4 %collective-permute-start.10 = (f32[128,128]{1,0:T(8,128)S(1)}, f32[128,128]{1,0:T(8,128)S(1)}, u32[]{:S(2)}, u32[]{:S(2)}) collective-permute-start(f32[128,128]{1,0:T(8,128)S(1)} %add.35), channel_id=1, source_target_pairs={{0,12},{1,13},{2,14},{3,15},{4,8},{5,9},{6,10},{7,11},{8,4},{9,5},... | collective-permute-start | bytes 196616 | tf_op jit(solution)/shard_map/ppermute | solution.py:15
  95.4 3.6 %collective-permute-start.11 = (f32[128,128]{1,0:T(8,128)S(1)}, f32[128,128]{1,0:T(8,128)S(1)}, u32[]{:S(2)}, u32[]{:S(2)}) collective-permute-start(f32[128,128]{1,0:T(8,128)S(1)} %add.36), channel_id=1, source_target_pairs={{0,32},{16,48},{32,0},{48,16},{64,96},{80,112},{96,64},{112,80},{1... | collective-permute-start | bytes 196616 | tf_op jit(solution)/shard_map/ppermute | solution.py:15
  99.1 4.6 %collective-permute-start.12 = (f32[128,128]{1,0:T(8,128)S(1)}, f32[128,128]{1,0:T(8,128)S(1)}, u32[]{:S(2)}, u32[]{:S(2)}) collective-permute-start(f32[128,128]{1,0:T(8,128)S(1)} %add.37), channel_id=1, source_target_pairs={{0,96},{16,112},{32,64},{48,80},{64,32},{80,48},{96,0},{112,16},{1... | collective-permute-start | bytes 196616 | tf_op jit(solution)/shard_map/ppermute | solution.py:15
  130.2 8.9 %collective-permute-start.13 = (f32[2048,128]{1,0:T(8,128)S(1)}, f32[2048,128]{1,0:T(8,128)S(1)}, u32[]{:S(2)}, u32[]{:S(2)}) collective-permute-start(f32[2048,128]{1,0:T(8,128)S(1)} %slice_bitcast_fusion), channel_id=1, source_target_pairs={{0,16},{16,0},{32,48},{48,32},{64,80},{80,64},{96,112},{112,96},{1... | collective-permute-start | bytes 3145736 | tf_op jit(solution)/shard_map/ppermute | solution.py:15
  181.5 4.6 %collective-permute-start.14 = (bf16[2048,128]{1,0:T(8,128)(2,1)S(1)}, bf16[2048,128]{1,0:T(8,128)(2,1)S(1)}, u32[]{:S(2)}, u32[]{:S(2)}) collective-permute-start(bf16[2048,128]{1,0:T(8,128)(2,1)S(1)} %bitcast.41), channel_id=1, source_target_pairs={{0,16},{16,0},{32,48},{48,32},{64,80},{80,64},{96,112},{112,96},{1... | collective-permute-start | bytes 1572872 | tf_op jit(solution)/shard_map/ppermute | solution.py:15
  199.6 3.0 %collective-permute-start.15 = (f32[2048,128]{1,0:T(8,128)S(1)}, f32[2048,128]{1,0:T(8,128)S(1)}, u32[]{:S(2)}, u32[]{:S(2)}) collective-permute-start(f32[2048,128]{1,0:T(8,128)S(1)} %slice_bitcast_fusion.2), channel_id=1, source_target_pairs={{0,16},{16,0},{32,48},{48,32},{64,80},{80,64},{96,112},{112,96},{1... | collective-permute-start | bytes 3145736 | tf_op jit(solution)/shard_map/ppermute | solution.py:15
  246.2 5.4 %collective-permute-start.16 = (f32[2048,128]{1,0:T(8,128)S(1)}, f32[2048,128]{1,0:T(8,128)S(1)}, u32[]{:S(2)}, u32[]{:S(2)}) collective-permute-start(f32[2048,128]{1,0:T(8,128)S(1)} %bitcast.38), channel_id=1, source_target_pairs={{0,16},{16,0},{32,48},{48,32},{64,80},{80,64},{96,112},{112,96},{1... | collective-permute-start | bytes 3145736 | tf_op jit(solution)/shard_map/ppermute | solution.py:15

commit v2 on v1

v2 whole, which is shorter than its diff:
```python
import math

import jax
import jax.numpy as jnp
from jax import lax
from jax.experimental import pallas as pl
from jax.experimental.pallas import tpu as pltpu
from jax.sharding import PartitionSpec as P

HIGH = lax.Precision.HIGHEST
BOTH = ("gy", "gx")


def xor_permute(value, axis, mask):
    return lax.ppermute(value, axis, [(i, i ^ mask) for i in range(lax.axis_size(axis))])


def shift_permute(value, axis, step):
    devices = lax.axis_size(axis)
    pairs = [(i, i + step) for i in range(devices) if 0 <= i + step < devices]
    return lax.ppermute(value, axis, pairs)


def params(mib, axes=0):
    return pltpu.CompilerParams(
        vmem_limit_bytes=mib << 20, dimension_semantics=("arbitrary",) * axes if axes else None
    )


def smooth_body(
    core_ref, x_ref, top_ref, bot_ref, left_ref, right_ref, kern_ref, test_ref,
    flat_ref, sketch_ref, keep_ref, send_ref, lt_ref, rt_ref, pad_ref,
):
    step, steps = pl.program_id(0), pl.num_programs(0)
    rows, cols, width = x_ref.shape
    f32 = jnp.float32
    group = 8
    groups = rows // group

    def ordered(edge_ref):
        edge = edge_ref[...].astype(f32)
        spare = jnp.zeros((group - 2, width), f32)
        return jnp.concatenate(
            [edge[rows : rows + 1], edge[:rows], edge[rows + 1 : rows + 2], spare], axis=0
        )

    lt_ref[...] = ordered(left_ref)
    rt_ref[...] = ordered(right_ref)

    @pl.when(step == 0)
    def _():
        sketch_ref[...] = jnp.zeros_like(sketch_ref)

    def project_rows(g):
        span = pl.ds(pl.multiple_of(g * group * cols, group * cols), group * cols)
        return span, jnp.dot(flat_ref[span, :], test_ref[...], preferred_element_type=f32)

    def smooth_rows(g):
        base = pl.multiple_of(g * group, group)
        for chunk in range(width // 128):
            lanes = slice(chunk * 128, chunk * 128 + 128)
            pad = pad_ref.at[chunk % 2]
            taps = [
                [jnp.broadcast_to(kern_ref[a, b : b + 1, lanes], (cols, 128)) for b in range(3)]
                for a in range(3)
            ]
            lefts = lt_ref[pl.ds(base, 2 * group), lanes]
            rights = rt_ref[pl.ds(base, 2 * group), lanes]

            def fetch(q):
                if q == 0:
                    above = x_ref[jnp.maximum(base - 1, 0), :, lanes]
                    row = jnp.where(g == 0, top_ref[:, lanes], above)
                elif q == group + 1:
                    below = x_ref[jnp.minimum(base + group, rows - 1), :, lanes]
                    row = jnp.where(g == groups - 1, bot_ref[:, lanes], below)
                else:
                    row = x_ref[base + q - 1, :, lanes]
                row = row.astype(f32)
                at = q * (cols + 16) + 8
                pad[at - 1 : at, :] = lefts[q : q + 1]
                pad[at : at + cols, :] = row
                pad[at + cols : at + cols + 1, :] = rights[q : q + 1]
                return [pad[at - 1 : at - 1 + cols, :], row, pad[at + 1 : at + 1 + cols, :]]

            near = [fetch(0), fetch(1)]
            for r in range(group):
                near = near[-2:] + [fetch(r + 2)]
                total = None
                for a in range(3):
                    for b in range(3):
                        term = taps[a][b] * near[a][b]
                        total = term if total is None else total + term
                start = pl.multiple_of((base + r) * cols, cols)
                flat_ref[pl.ds(start, cols), lanes] = total.astype(jnp.bfloat16)

    def body(g, carry):
        span, part = project_rows(g - 1)
        smooth_rows(g)
        sketch_ref[span, :] += part
        return carry

    smooth_rows(0)
    lax.fori_loop(1, groups, body, 0)
    span, part = project_rows(groups - 1)
    sketch_ref[span, :] += part

    @pl.when(step == steps - 1)
    def _():
        values = sketch_ref[...]
        gram = lax.dot_general(
            values, values, (((0,), (0,)), ((), ())), precision=HIGH, preferred_element_type=f32
        )
        half = keep_ref.shape[0]

        @pl.when(core_ref[0] == 0)
        def _():
            keep_ref[...] = gram[:half]
            send_ref[...] = gram[half:]

        @pl.when(core_ref[0] == 1)
        def _():
            keep_ref[...] = gram[half:]
            send_ref[...] = gram[:half]


def smooth_sketch(core, x, halos, kernel, test_matrix):
    rows, cols, channels = x.shape
    k = test_matrix.shape[1]
    width = 512
    edge = lambda n: pl.BlockSpec((n, width), lambda j, core: (0, j))
    fixed = lambda n: pl.BlockSpec((n, k), lambda j, core: (0, 0))
    return pl.pallas_call(
        smooth_body,
        grid_spec=pltpu.PrefetchScalarGridSpec(
            num_scalar_prefetch=1,
            grid=(channels // width,),
            in_specs=[
                pl.BlockSpec((rows, cols, width), lambda j, core: (0, 0, j)),
                edge(cols), edge(cols), edge(rows + 8), edge(rows + 8),
                pl.BlockSpec((3, 3, width), lambda j, core: (0, 0, j)),
                pl.BlockSpec((width, k), lambda j, core: (j, 0)),
            ],
            out_specs=[edge(rows * cols), fixed(rows * cols), fixed(k // 2), fixed(k // 2)],
            scratch_shapes=[pltpu.VMEM((rows + 8, width), jnp.float32)] * 2
            + [pltpu.VMEM((2, 10 * (cols + 16), 128), jnp.float32)],
        ),
        out_shape=[
            jax.ShapeDtypeStruct((rows * cols, channels), jnp.bfloat16),
            jax.ShapeDtypeStruct((rows * cols, k), jnp.float32),
            jax.ShapeDtypeStruct((k // 2, k), jnp.float32),
            jax.ShapeDtypeStruct((k // 2, k), jnp.float32),
        ],
        compiler_params=params(40, 1),
        name="smooth_sketch",
    )(core, x, *halos, kernel, test_matrix)


def columns_body(x_ref, top_ref, bot_ref, first_ref, last_ref, low_ref, high_ref, sems):
    rows, cols, _ = x_ref.shape
    copies = [
        pltpu.make_async_copy(x_ref.at[:, pl.ds(0, 8), :], low_ref, sems.at[0]),
        pltpu.make_async_copy(x_ref.at[:, pl.ds(cols - 8, 8), :], high_ref, sems.at[1]),
    ]
    for copy in copies:
        copy.start()
    for copy, place, held_ref, out_ref in zip(
        copies, (0, cols - 1), (low_ref, high_ref), (first_ref, last_ref)
    ):
        copy.wait()
        for lane in range(0, out_ref.shape[1], 512):
            lanes = slice(lane, lane + 512)
            column = held_ref[:, :, lanes].astype(jnp.float32)[:, place % 8]
            ends = [r[:, lanes].astype(jnp.float32)[place : place + 1] for r in (top_ref, bot_ref)]
            spare = jnp.zeros((6, 512), jnp.float32)
            joined = jnp.concatenate([column] + ends + [spare], axis=0)
            out_ref[:, lanes] = joined.astype(jnp.bfloat16)


def edge_columns(x, top, bottom):
    rows, cols, channels = x.shape
    return pl.pallas_call(
        columns_body,
        in_specs=[pl.BlockSpec(memory_space=pltpu.HBM)]
        + [pl.BlockSpec(memory_space=pltpu.VMEM)] * 2,
        out_shape=[jax.ShapeDtypeStruct((rows + 8, channels), x.dtype)] * 2,
        scratch_shapes=[pltpu.VMEM((rows, 8, channels), x.dtype)] * 2
        + [pltpu.SemaphoreType.DMA((2,))],
        compiler_params=params(20),
        name="edge_columns",
    )(x, top, bottom)


def factor_block(panel, low, sub, lane):
    shape = panel.shape
    d = [
        [jnp.broadcast_to(panel[i : i + 1, low + j : low + j + 1], shape) for j in range(i + 1)]
        for i in range(8)
    ]
    e = [[None] * 8 for _ in range(8)]
    for j in range(8):
        scale = lax.rsqrt(d[j][j])
        column = [d[i][j] * scale if i > j else None for i in range(8)]
        for k in range(j):
            e[j][k] = e[j][k] * scale
        e[j][j] = scale
        for i in range(j + 1, 8):
            for k in range(j + 1, i + 1):
                d[i][k] = d[i][k] - column[i] * column[k]
            for k in range(j):
                e[i][k] = e[i][k] - column[i] * e[j][k]
            e[i][j] = -column[i] * scale
    unit = jnp.where(lane == sub + low, 1.0, 0.0)
    panel = jnp.where((lane >= low) & (lane < low + 8), unit, panel)
    total = None
    for k in range(8):
        column = jnp.where(sub == k, e[k][k], 0.0)
        for i in range(k + 1, 8):
            column = jnp.where(sub == i, e[i][k], column)
        term = column * jnp.broadcast_to(panel[k : k + 1, :], shape)
        total = term if total is None else total + term
    return total


def inverse_factor(work_ref):
    n = work_ref.shape[0]
    row_id = lax.broadcasted_iota(jnp.int32, (n, n), 0)
    col_id = lax.broadcasted_iota(jnp.int32, (n, n), 1)
    sub = lax.broadcasted_iota(jnp.int32, (8, n), 0)
    lane = lax.broadcasted_iota(jnp.int32, (8, n), 1)
    panel = work_ref[0:8, :]
    for low in range(0, n, 8):
        near, far = low + 8, low + 16
        done = factor_block(panel, low, sub, lane)
        work_ref[low:near, :] = done
        if far < n:
            update = lax.dot_general(
                done, done, (((0,), (0,)), ((), ())), precision=HIGH,
                preferred_element_type=jnp.float32,
            )
            keep = (col_id[far:] < low) | (col_id[far:] >= near)
            rest = jnp.where(keep, work_ref[far:, :], 0.0) - update[far:, :]
        if near < n:
            turned = done.T[near:far, :]
            panel = jnp.where((lane < low) | (lane >= near), work_ref[near:far, :], 0.0)
            for k in range(8):
                panel = panel - jnp.broadcast_to(turned[:, k : k + 1], panel.shape) * (
                    jnp.broadcast_to(done[k : k + 1, :], panel.shape)
                )
        if far < n:
            work_ref[far:, :] = rest
    return jnp.where(row_id >= col_id, work_ref[...], 0.0)


def times_transposed(values, matrix):
    return lax.dot_general(
        values, matrix, (((1,), (1,)), ((), ())), precision=HIGH,
        preferred_element_type=jnp.float32,
    )


def project_body(
    core_ref, mine_ref, other_ref, sketch_ref, flat_ref, out_ref, work_ref, basis_ref
):
    @pl.when(pl.program_id(0) == 0)
    def _():
        half = mine_ref.shape[0]
        work_ref[pl.ds(pl.multiple_of(core_ref[0] * half, half), half), :] = mine_ref[...]
        work_ref[pl.ds(pl.multiple_of((1 - core_ref[0]) * half, half), half), :] = other_ref[...]
        inverse = inverse_factor(work_ref)
        basis = times_transposed(sketch_ref[...], inverse)
        basis_ref[...] = basis.astype(jnp.bfloat16).T

    product = jnp.dot(basis_ref[...], flat_ref[...], preferred_element_type=jnp.float32)
    out_ref[0] = product.T


def project(core, mine, other, sketch, flat):
    pixels, channels = flat.shape
    k = sketch.shape[1]
    width = 512
    half = channels // width // 2
    whole = lambda *shape: pl.BlockSpec(shape, lambda j, core: (0,) * len(shape))
    return pl.pallas_call(
        project_body,
        grid_spec=pltpu.PrefetchScalarGridSpec(
            num_scalar_prefetch=1,
            grid=(channels // width,),
            in_specs=[
                whole(k // 2, k), whole(k // 2, k), whole(pixels, k),
                pl.BlockSpec((pixels, width), lambda j, core: (0, j)),
            ],
            out_specs=pl.BlockSpec(
                (1, width, k), lambda j, core: ((j // half) ^ core[0], j % half, 0)
            ),
            scratch_shapes=[
                pltpu.VMEM((k, k), jnp.float32), pltpu.VMEM((k, pixels), jnp.bfloat16),
            ],
        ),
        out_shape=jax.ShapeDtypeStruct((2, channels // 2, k), jnp.float32),
        compiler_params=params(40, 1),
        name="project",
    )(core, mine, other, sketch, flat)


def second_body(core_ref, flat_ref, range_ref, second_ref, out_ref, acc_ref):
    step, steps = pl.program_id(0), pl.num_programs(0)
    f32, bf16 = jnp.float32, jnp.bfloat16
    k = range_ref.shape[1]
    values = jnp.dot(flat_ref[...], range_ref[...], preferred_element_type=f32)
    second_ref[...] = values
    high = values.astype(bf16)
    low = (values - high.astype(f32)).astype(bf16)
    both = jnp.concatenate([high, low], axis=1).T

    @pl.when(step == 0)
    def _():
        acc_ref[...] = jnp.dot(both, flat_ref[...], preferred_element_type=f32)

    @pl.when(step > 0)
    def _():
        acc_ref[...] += jnp.dot(both, flat_ref[...], preferred_element_type=f32)

    @pl.when(step == steps - 1)
    def _():
        half = out_ref.shape[1]
        for part in range(2):
            lanes = slice(part * half, part * half + half)
            out_ref[part ^ core_ref[0]] = (acc_ref[:k, lanes] + acc_ref[k:, lanes]).T


def second_step(core, flat, range_map):
    pixels, channels = flat.shape
    k = range_map.shape[1]
    height = 512
    return pl.pallas_call(
        second_body,
        grid_spec=pltpu.PrefetchScalarGridSpec(
            num_scalar_prefetch=1,
            grid=(pixels // height,),
            in_specs=[
                pl.BlockSpec((height, channels), lambda i, core: (i, 0)),
                pl.BlockSpec((channels, k), lambda i, core: (0, 0)),
            ],
            out_specs=[
                pl.BlockSpec((height, k), lambda i, core: (i, 0)),
                pl.BlockSpec((2, channels // 2, k), lambda i, core: (0, 0, 0)),
            ],
            scratch_shapes=[pltpu.VMEM((2 * k, channels), jnp.float32)],
        ),
        out_shape=[
            jax.ShapeDtypeStruct((pixels, k), jnp.float32),
            jax.ShapeDtypeStruct((2, channels // 2, k), jnp.float32),
        ],
        compiler_params=params(44, 1),
        name="second_step",
    )(core, flat, range_map)


def finish_body(basis_scale, coeff_scale, range_ref, moment_ref, second_ref, basis_ref, coeffs_ref, work_ref):
    moment = moment_ref[...]
    gram = lax.dot_general(
        range_ref[...].astype(jnp.float32), moment, (((0,), (0,)), ((), ())), precision=HIGH,
        preferred_element_type=jnp.float32,
    )
    work_ref[...] = gram
    inverse = inverse_factor(work_ref)
    basis_ref[...] = times_transposed(second_ref[...], inverse) * basis_scale
    coeffs_ref[...] = times_transposed(inverse, moment) * coeff_scale


def finish(range_map, moment, second, basis_scale, coeff_scale):
    channels, k = moment.shape

    def body(*refs):
        finish_body(basis_scale, coeff_scale, *refs)

    return pl.pallas_call(
        body,
        out_shape=[
            jax.ShapeDtypeStruct(second.shape, jnp.float32),
            jax.ShapeDtypeStruct((k, channels), jnp.float32),
        ],
        scratch_shapes=[pltpu.VMEM((k, k), jnp.float32)],
        compiler_params=params(40),
        name="finish",
    )(range_map, moment, second)


def all_sum(pair, core, dtype):
    gy, gx = lax.axis_size("gy"), lax.axis_size("gx")
    groups = [[y * gx + x for y in range(c, gy, 2) for x in range(gx)] for c in range(2)]
    half, k = pair.shape[1:]
    members = gy * gx // 2
    swap = lambda v: lax.all_to_all(v, BOTH, 0, 0, axis_index_groups=groups, tiled=True)
    mine = pair[0] + xor_permute(pair[1], "gy", 1)
    parts = swap(mine.reshape(members, half // members, k))
    chunk = jnp.sum(parts, axis=0).astype(dtype)
    chunk = lax.optimization_barrier(chunk)
    whole = swap(jnp.broadcast_to(chunk[None], (members,) + chunk.shape)).reshape(half, k)
    other = xor_permute(whole, "gy", 1)
    first, last = jnp.where(core == 0, whole, other), jnp.where(core == 0, other, whole)
    return jnp.concatenate([first, last], axis=0)


def on_device(radiance, kernel, test_matrix):
    height, breadth, channels = radiance.shape
    devices = lax.axis_size("gy") * lax.axis_size("gx")
    pixel_count = height * breadth * devices
    core = lax.axis_index("gy") % 2
    core_arg = core.astype(jnp.int32).reshape(1)

    top = shift_permute(radiance[-1], "gy", 1)
    bottom = shift_permute(radiance[0], "gy", -1)
    first, last = edge_columns(radiance, top, bottom)
    left = shift_permute(last, "gx", 1)
    right = shift_permute(first, "gx", -1)
    halos = (top, bottom, left, right)

    flat, sketch, mine, send = smooth_sketch(core_arg, radiance, halos, kernel, test_matrix)
    mine = mine + xor_permute(send, "gy", 1)
    for axis, mask in (("gx", 1), ("gx", 3), ("gx", 4), ("gx", 12), ("gy", 2), ("gy", 6)):
        mine = mine + xor_permute(mine, axis, mask)
    other = xor_permute(mine, "gy", 1)
    range_map = all_sum(project(core_arg, mine, other, sketch, flat), core, jnp.bfloat16)
    second, pair = second_step(core_arg, flat, range_map)
    moment = all_sum(pair, core, jnp.float32)
    scale = math.sqrt(pixel_count)
    basis_out, coeffs = finish(
        range_map, moment, second, scale, scale * math.sqrt(channels) / pixel_count
    )
    return (basis_out.reshape(height, breadth, basis_out.shape[1]), coeffs)


def solution(mesh):
    placed = (P("gy", "gx", None), P(), P())
    return jax.shard_map(
        on_device, mesh=mesh, in_specs=placed, out_specs=(P("gy", "gx", None), P()), check_vma=False
    )
```

time: 274 us -> 255 us (0.931)
  Pallas kernels: 101 us -> 82.6 us
  waiting for transfers between devices: 28.3 us -> 38.3 us
  local copies, waits for them, and re-layouts: 12.7 us -> 7.17 us
  starting transfers between devices: 43.9 us -> 40 us
    ppermute x6 -> x4, waiting for transfers between devices: 7.04 us -> 17.9 us  [shift_permute(): return lax.ppermute(value, axis, pairs)]
    pallas_call x1, Pallas kernels: 21.6 us -> 11.8 us  [finish(): pl.pallas_call(body, out_shape=[jax.ShapeDtypeStruct(second.shape, jnp.fl...]
    pallas_call x1, Pallas kernels: 26.5 us -> 16.7 us  [project(): pl.pallas_call(project_body, grid_spec=pltpu.PrefetchScalarGridSpec(num_s...]
    ppermute x6 -> x4, starting transfers between devices: 16.5 us -> 11.3 us  [shift_permute(): return lax.ppermute(value, axis, pairs)]
    slice x1 -> x0, local copies, waits for them, and re-layouts: 4.61 us -> none  [on_device(): right = shift_permute(radiance[:, 0], 'gx', -1)]
    ppermute x11 -> x12, starting transfers between devices: 27.4 us -> 28.8 us  [xor_permute(): lax.ppermute(value, axis, [(i, i ^ mask) for i in range(lax.axis_size(axi...]
    unnamed x8 -> x6, local copies, waits for them, and re-layouts: 4.57 us -> 5.78 us
    ppermute x11 -> x12, waiting for transfers between devices: 21.2 us -> 20.4 us  [xor_permute(): lax.ppermute(value, axis, [(i, i ^ mask) for i in range(lax.axis_size(axi...]
  transfers between devices with their start and end apart: 17 -> 16, of which waited for: 13 -> 16; matrix products, arithmetic and copies ran while one was open for 3% -> 0% of each run, Pallas kernels for 0% -> 0%
where the time goes in v2:
time: 255 us
  blocking collectives  85.3 us (33%)
  Pallas kernels  82.6 us (32%)
  starting transfers between devices  40 us (16%)
  waiting for transfers between devices  38.3 us (15%)
  local copies, waits for them, and re-layouts  7.17 us (3%)
    all_to_all x4, blocking collectives, all_sum(): lax.all_to_all(v, BOTH, 0, 0, axis_index_groups=groups, tiled=True)  85.3 us
    pallas_call x1, Pallas kernels, smooth_sketch(): pl.pallas_call(smooth_body, grid_spec=pltpu.PrefetchScalarGridSpec(num_sc...  36.6 us
    ppermute x12, starting transfers between devices, xor_permute(): lax.ppermute(value, axis, [(i, i ^ mask) for i in range(lax.axis_size(axi...  28.8 us
    ppermute x12, waiting for transfers between devices, xor_permute(): lax.ppermute(value, axis, [(i, i ^ mask) for i in range(lax.axis_size(axi...  20.4 us
    ppermute x4, waiting for transfers between devices, shift_permute(): return lax.ppermute(value, axis, pairs)  17.9 us
    pallas_call x1, Pallas kernels, project(): pl.pallas_call(project_body, grid_spec=pltpu.PrefetchScalarGridSpec(num_s...  16.7 us
    pallas_call x1, Pallas kernels, second_step(): pl.pallas_call(second_body, grid_spec=pltpu.PrefetchScalarGridSpec(num_sc...  13.1 us
    pallas_call x1, Pallas kernels, finish(): pl.pallas_call(body, out_shape=[jax.ShapeDtypeStruct(second.shape, jnp.fl...  11.8 us
  transfers between devices with their start and end apart: 16, of which 16 were waited for; matrix products, arithmetic and copies ran while one was open for 0% of the time, Pallas kernels for 0%

profile of v2, /device:TPU:1, one launch (start us, length us, event | category | flops | bytes accessed | tf_op | source)
XLA Modules:
  0.0 255.0 jit_solution(11072182042933614113)
XLA Ops:
  0.6 1.1 slice_bitcast_fusion.3
  1.7 4.9 %collective-permute-start = (bf16[32,4096]{1,0:T(8,128)(2,1)S(1)}, bf16[32,4096]{1,0:T(8,128)(2,1)S(1)}, u32[]{:S(2)}, u32[]{:S(2)}) collective-permute-start(bf16[32,4096]{1,0:T(8,128)(2,1)S(1)} %get-tuple-element.23), channel_id=1, source_target_pairs={{0,16},{16,32},{32,48},{48,64},{64,80},{80,96},{96,112},{1,17},{17... | collective-permute-start | bytes 786440 | tf_op jit(solution)/shard_map/ppermute | solution.py:21
  6.6 1.9 collective-permute-start.1
  8.6 1.4 collective-permute-done.top_ref
  9.9 4.4 %collective-permute-done.1.bot_ref = bf16[32,4096]{1,0:T(8,128)(2,1)S(1)} collective-permute-done((bf16[32,4096]{1,0:T(8,128)(2,1)S(1)}, bf16[32,4096]{1,0:T(8,128)(2,1)S(1)}, u32[]{:S(2)}, u32[]{:S(2)}) %collective-permute-start.1) | collective-permute-done | bytes 262176 | tf_op jit(solution)/shard_map/ppermute | solution.py:21
  14.3 0.0 copy-start
  14.3 5.8 %copy-done = bf16[64,32,4096]{2,1,0:T(8,128)(2,1)S(1)} copy-done((bf16[64,32,4096]{2,1,0:T(8,128)(2,1)S(1)}, bf16[64,32,4096]{2,1,0:T(8,128)(2,1)}, u32[]{:S(2)}) %copy-start) | copy-done | bytes 16777240
  20.1 0.0 copy-start.1
  20.1 0.0 copy-start.2
  20.1 4.4 %edge_columns.1 = (bf16[72,4096]{1,0:T(8,128)(2,1)S(1)}, bf16[72,4096]{1,0:T(8,128)(2,1)}) custom-call(bf16[64,32,4096]{2,1,0:T(8,128)(2,1)S(1)} %copy-done, bf16[32,4096]{1,0:T(8,128)(2,1)S(1)} %collective-permute-done.top_ref, bf16[32,4096]{1,0:T(8,128)(2,1)S(1)} %collective-permute-done.1.bot_ref), custom_call_target="tpu_custom_call" | custom-call | tf_op jit(solution)/shard_map/edge_columns/pallas_call | solution.py:182
  24.5 3.2 %collective-permute-start.2 = (bf16[72,4096]{1,0:T(8,128)(2,1)}, bf16[72,4096]{1,0:T(8,128)(2,1)S(1)}, u32[]{:S(2)}, u32[]{:S(2)}) collective-permute-start(bf16[72,4096]{1,0:T(8,128)(2,1)} %get-tuple-element.12), channel_id=1, source_target_pairs={{0,1},{1,2},{2,3},{3,4},{4,5},{5,6},{6,7},{7,8},{8,9},{9,10},{10,1... | collective-permute-start | bytes 1769480 | tf_op jit(solution)/shard_map/ppermute | solution.py:21
  27.7 1.3 collective-permute-start.3
  29.0 8.3 %collective-permute-done.2.left_ref = bf16[72,4096]{1,0:T(8,128)(2,1)S(1)} collective-permute-done((bf16[72,4096]{1,0:T(8,128)(2,1)}, bf16[72,4096]{1,0:T(8,128)(2,1)S(1)}, u32[]{:S(2)}, u32[]{:S(2)}) %collective-permute-start.2) | collective-permute-done | bytes 589856 | tf_op jit(solution)/shard_map/ppermute | solution.py:21
  37.3 3.8 %collective-permute-done.3.right_ref = bf16[72,4096]{1,0:T(8,128)(2,1)S(1)} collective-permute-done((bf16[72,4096]{1,0:T(8,128)(2,1)S(1)}, bf16[72,4096]{1,0:T(8,128)(2,1)S(1)}, u32[]{:S(2)}, u32[]{:S(2)}) %collective-permute-start.3) | collective-permute-done | bytes 589856 | tf_op jit(solution)/shard_map/ppermute | solution.py:21
  41.1 0.0 copy-done.1
  41.1 0.0 copy-done.2
  41.1 36.6 %smooth_sketch.1 = (bf16[2048,4096]{1,0:T(8,128)(2,1)}, f32[2048,128]{1,0:T(8,128)S(1)}, f32[64,128]{1,0:T(8,128)S(1)}, f32[64,128]{1,0:T(8,128)S(1)}) custom-call(s32[1]{0:T(128)} %bitcast.core_ref, bf16[64,32,4096]{2,1,0:T(8,128)(2,1)} %x_ref.3, bf16[32,4096]{1,0:T(8,128)(2,1)S(1)} %collective-permute-done.top_ref, ...), custom_call_target="tpu_custom_call" | custom-call | tf_op jit(solution)/shard_map/smooth_sketch/pallas_call | solution.py:133
  77.7 0.0 collective-permute-start.4
  77.7 1.2 collective-permute-done.4
  78.9 1.2 collective-permute-start.5
  80.1 1.6 collective-permute-done.5
  81.7 4.6 %collective-permute-start.6 = (f32[64,128]{1,0:T(8,128)S(1)}, f32[64,128]{1,0:T(8,128)S(1)}, u32[]{:S(2)}, u32[]{:S(2)}) collective-permute-start(f32[64,128]{1,0:T(8,128)S(1)} %add.33), channel_id=1, source_target_pairs={{0,3},{1,2},{2,1},{3,0},{4,7},{5,6},{6,5},{7,4},{8,11},{9,10},{10,... | collective-permute-start | bytes 98312 | tf_op jit(solution)/shard_map/ppermute | solution.py:15
  86.2 1.3 collective-permute-done.6
  87.5 1.3 collective-permute-start.7
  88.8 1.5 collective-permute-done.7
  90.3 1.4 collective-permute-start.8
  91.7 2.5 collective-permute-done.8
  94.3 4.2 %collective-permute-start.9 = (f32[64,128]{1,0:T(8,128)S(1)}, f32[64,128]{1,0:T(8,128)S(1)}, u32[]{:S(2)}, u32[]{:S(2)}) collective-permute-start(f32[64,128]{1,0:T(8,128)S(1)} %add.36), channel_id=1, source_target_pairs={{0,32},{16,48},{32,0},{48,16},{64,96},{80,112},{96,64},{112,80},{1... | collective-permute-start | bytes 98312 | tf_op jit(solution)/shard_map/ppermute | solution.py:15
  98.5 1.3 collective-permute-done.9
  99.8 2.2 collective-permute-start.10
  102.0 1.7 collective-permute-done.10
  103.8 6.5 %collective-permute-start.11 = (f32[64,128]{1,0:T(8,128)S(1)}, f32[64,128]{1,0:T(8,128)S(1)}, u32[]{:S(2)}, u32[]{:S(2)}) collective-permute-start(f32[64,128]{1,0:T(8,128)S(1)} %add.38.mine_ref), channel_id=1, source_target_pairs={{0,16},{16,0},{32,48},{48,32},{64,80},{80,64},{96,112},{112,96},{1... | collective-permute-start | bytes 98312 | tf_op jit(solution)/shard_map/ppermute | solution.py:15
  110.3 0.9 collective-permute-done.11.other_ref
  111.1 16.7 %project.1 = f32[2,2048,128]{2,1,0:T(8,128)S(1)} custom-call(s32[1]{0:T(128)} %bitcast.core_ref, f32[64,128]{1,0:T(8,128)S(1)} %add.38.mine_ref, f32[64,128]{1,0:T(8,128)S(1)} %collective-permute-done.11.other_ref, f32[2048,128]{1,0:T(8,128)S(1)} %get-tuple-element.16.sketch_ref, bf16[2048,4096]{1,0:T(8,128)(2,1)} %get-tuple-element.17.flat_ref), custom_call_target="tpu_custom_call" | custom-call | tf_op jit(solution)/shard_map/project/pallas_call | solution.py:284
  127.8 0.1 slice_bitcast_fusion
  127.9 0.6 collective-permute-start.12
  128.5 2.3 collective-permute-done.12
  130.8 0.1 fusion
  130.9 26.5 %all_to_all.20 = f32[64,32,128]{2,1,0:T(8,128)S(1)} all-to-all(f32[64,32,128]{2,1,0:T(8,128)S(1)} %bitcast.25), channel_id=1, replica_groups={{0,1,2,3,4,5,6,7,8,9,10,11,12,13,14,15,32,33,34,35,36,37,38,39,40,41,42..., dimensions={0} | all-to-all | bytes 2097152 | tf_op jit(solution)/shard_map/all_to_all | solution.py:395
  157.4 0.1 reduce_sum.18
  157.5 0.1 broadcast_in_dim.4
  157.5 15.5 %all_to_all.21 = bf16[64,32,128]{2,1,0:T(8,128)(2,1)S(1)} all-to-all(bf16[64,32,128]{2,1,0:T(8,128)(2,1)S(1)} %broadcast_in_dim.4), channel_id=1, replica_groups={{0,1,2,3,4,5,6,7,8,9,10,11,12,13,14,15,32,33,34,35,36,37,38,39,40,41,42..., dimensions={0} | all-to-all | bytes 1048576 | tf_op jit(solution)/shard_map/all_to_all | solution.py:395
  173.0 3.1 %collective-permute-start.13 = (bf16[2048,128]{1,0:T(8,128)(2,1)S(1)}, bf16[2048,128]{1,0:T(8,128)(2,1)S(1)}, u32[]{:S(2)}, u32[]{:S(2)}) collective-permute-start(bf16[2048,128]{1,0:T(8,128)(2,1)S(1)} %bitcast.27), channel_id=1, source_target_pairs={{0,16},{16,0},{32,48},{48,32},{64,80},{80,64},{96,112},{112,96},{1... | collective-permute-start | bytes 1572872 | tf_op jit(solution)/shard_map/ppermute | solution.py:15
  176.1 1.5 collective-permute-done.13
  177.7 0.1 broadcast_select_fusion.3
  177.8 0.1 pad_maximum_fusion.1.range_ref.refs_0_
  177.9 13.1 %second_step.1 = (f32[2048,128]{1,0:T(8,128)S(1)}, f32[2,2048,128]{2,1,0:T(8,128)S(1)}) custom-call(s32[1]{0:T(128)} %bitcast.core_ref, bf16[2048,4096]{1,0:T(8,128)(2,1)} %get-tuple-element.17.flat_ref, bf16[4096,128]{1,0:T(8,128)(2,1)S(1)} %pad_maximum_fusion.1.range_ref.refs_0_), custom_call_target="tpu_custom_call" | custom-call | tf_op jit(solution)/shard_map/second_step/pallas_call | solution.py:336
  191.0 0.1 slice_bitcast_fusion.2
  191.1 0.5 collective-permute-start.14
  191.5 2.3 collective-permute-done.14
  193.8 0.1 bitcast_add_fusion
  193.9 22.3 %all_to_all.22 = f32[64,32,128]{2,1,0:T(8,128)S(1)} all-to-all(f32[64,32,128]{2,1,0:T(8,128)S(1)} %bitcast.26), channel_id=1, replica_groups={{0,1,2,3,4,5,6,7,8,9,10,11,12,13,14,15,32,33,34,35,36,37,38,39,40,41,42..., dimensions={0} | all-to-all | bytes 2097152 | tf_op jit(solution)/shard_map/all_to_all | solution.py:395
  216.3 0.1 reduce_sum.19
  216.4 0.1 broadcast_in_dim.5
  216.5 21.0 %all_to_all.23 = f32[64,32,128]{2,1,0:T(8,128)S(1)} all-to-all(f32[64,32,128]{2,1,0:T(8,128)S(1)} %broadcast_in_dim.5), channel_id=1, replica_groups={{0,1,2,3,4,5,6,7,8,9,10,11,12,13,14,15,32,33,34,35,36,37,38,39,40,41,42..., dimensions={0} | all-to-all | bytes 2097152 | tf_op jit(solution)/shard_map/all_to_all | solution.py:395
  237.5 3.2 %collective-permute-start.15 = (f32[2048,128]{1,0:T(8,128)S(1)}, f32[2048,128]{1,0:T(8,128)S(1)}, u32[]{:S(2)}, u32[]{:S(2)}) collective-permute-start(f32[2048,128]{1,0:T(8,128)S(1)} %bitcast.24), channel_id=1, source_target_pairs={{0,16},{16,0},{32,48},{48,32},{64,80},{80,64},{96,112},{112,96},{1... | collective-permute-start | bytes 3145736 | tf_op jit(solution)/shard_map/ppermute | solution.py:15
  240.6 2.3 collective-permute-done.15
  242.9 0.1 broadcast_select_fusion.1
  243.1 0.1 pad_maximum_fusion.refs_1_
  243.2 11.8 %finish.1 = (f32[2048,128]{1,0:T(8,128)}, f32[128,4096]{1,0:T(8,128)}) custom-call(bf16[4096,128]{1,0:T(8,128)(2,1)S(1)} %pad_maximum_fusion.1.range_ref.refs_0_, f32[4096,128]{1,0:T(8,128)S(1)} %pad_maximum_fusion.refs_1_, f32[2048,128]{1,0:T(8,128)S(1)} %get-tuple-element.19.refs_2_), custom_call_target="tpu_custom_call" | custom-call | tf_op jit(solution)/shard_map/finish/pallas_call | solution.py:378
  (7 shorter events, 0.0 us)
Async XLA Ops:
  1.7 8.2 %collective-permute-start = (bf16[32,4096]{1,0:T(8,128)(2,1)S(1)}, bf16[32,4096]{1,0:T(8,128)(2,1)S(1)}, u32[]{:S(2)}, u32[]{:S(2)}) collective-permute-start(bf16[32,4096]{1,0:T(8,128)(2,1)S(1)} %get-tuple-element.23), channel_id=1, source_target_pairs={{0,16},{16,32},{32,48},{48,64},{64,80},{80,96},{96,112},{1,17},{17... | collective-permute-start | bytes 786440 | tf_op jit(solution)/shard_map/ppermute | solution.py:21
  6.6 7.7 %collective-permute-start.1 = (bf16[32,4096]{1,0:T(8,128)(2,1)S(1)}, bf16[32,4096]{1,0:T(8,128)(2,1)S(1)}, u32[]{:S(2)}, u32[]{:S(2)}) collective-permute-start(bf16[32,4096]{1,0:T(8,128)(2,1)S(1)} %get-tuple-element.22), channel_id=1, source_target_pairs={{16,0},{32,16},{48,32},{64,48},{80,64},{96,80},{112,96},{17,1},{33... | collective-permute-start | bytes 786440 | tf_op jit(solution)/shard_map/ppermute | solution.py:21
  14.3 5.8 %copy-start = (bf16[64,32,4096]{2,1,0:T(8,128)(2,1)S(1)}, bf16[64,32,4096]{2,1,0:T(8,128)(2,1)}, u32[]{:S(2)}) copy-start(bf16[64,32,4096]{2,1,0:T(8,128)(2,1)} %x_ref.3) | copy-start | bytes 50331652
  20.1 21.0 %copy-start.1 = (bf16[4096,128]{1,0:T(8,128)(2,1)S(1)}, bf16[4096,128]{1,0:T(8,128)(2,1)}, u32[]{:S(2)}) copy-start(bf16[4096,128]{1,0:T(8,128)(2,1)} %test_ref.1) | copy-start | bytes 3145732
  20.1 21.0 %copy-start.2 = (f32[3,3,4096]{2,1,0:T(4,128)S(1)}, f32[3,3,4096]{2,1,0:T(4,128)}, u32[]{:S(2)}) copy-start(f32[3,3,4096]{2,1,0:T(4,128)} %kern_ref.1) | copy-start | bytes 442372
  24.5 12.8 %collective-permute-start.2 = (bf16[72,4096]{1,0:T(8,128)(2,1)}, bf16[72,4096]{1,0:T(8,128)(2,1)S(1)}, u32[]{:S(2)}, u32[]{:S(2)}) collective-permute-start(bf16[72,4096]{1,0:T(8,128)(2,1)} %get-tuple-element.12), channel_id=1, source_target_pairs={{0,1},{1,2},{2,3},{3,4},{4,5},{5,6},{6,7},{7,8},{8,9},{9,10},{10,1... | collective-permute-start | bytes 1769480 | tf_op jit(solution)/shard_map/ppermute | solution.py:21
  27.7 13.4 %collective-permute-start.3 = (bf16[72,4096]{1,0:T(8,128)(2,1)S(1)}, bf16[72,4096]{1,0:T(8,128)(2,1)S(1)}, u32[]{:S(2)}, u32[]{:S(2)}) collective-permute-start(bf16[72,4096]{1,0:T(8,128)(2,1)S(1)} %get-tuple-element.13), channel_id=1, source_target_pairs={{1,0},{2,1},{3,2},{4,3},{5,4},{6,5},{7,6},{8,7},{9,8},{10,9},{11,1... | collective-permute-start | bytes 1769480 | tf_op jit(solution)/shard_map/ppermute | solution.py:21
  77.7 1.2 collective-permute-start.4
  78.9 2.8 %collective-permute-start.5 = (f32[64,128]{1,0:T(8,128)S(1)}, f32[64,128]{1,0:T(8,128)S(1)}, u32[]{:S(2)}, u32[]{:S(2)}) collective-permute-start(f32[64,128]{1,0:T(8,128)S(1)} %add.32), channel_id=1, source_target_pairs={{0,1},{1,0},{2,3},{3,2},{4,5},{5,4},{6,7},{7,6},{8,9},{9,8},{10,11... | collective-permute-start | bytes 98312 | tf_op jit(solution)/shard_map/ppermute | solution.py:15
  81.7 5.9 %collective-permute-start.6 = (f32[64,128]{1,0:T(8,128)S(1)}, f32[64,128]{1,0:T(8,128)S(1)}, u32[]{:S(2)}, u32[]{:S(2)}) collective-permute-start(f32[64,128]{1,0:T(8,128)S(1)} %add.33), channel_id=1, source_target_pairs={{0,3},{1,2},{2,1},{3,0},{4,7},{5,6},{6,5},{7,4},{8,11},{9,10},{10,... | collective-permute-start | bytes 98312 | tf_op jit(solution)/shard_map/ppermute | solution.py:15
  87.5 2.8 %collective-permute-start.7 = (f32[64,128]{1,0:T(8,128)S(1)}, f32[64,128]{1,0:T(8,128)S(1)}, u32[]{:S(2)}, u32[]{:S(2)}) collective-permute-start(f32[64,128]{1,0:T(8,128)S(1)} %add.34), channel_id=1, source_target_pairs={{0,4},{1,5},{2,6},{3,7},{4,0},{5,1},{6,2},{7,3},{8,12},{9,13},{10,... | collective-permute-start | bytes 98312 | tf_op jit(solution)/shard_map/ppermute | solution.py:15
  90.3 4.0 %collective-permute-start.8 = (f32[64,128]{1,0:T(8,128)S(1)}, f32[64,128]{1,0:T(8,128)S(1)}, u32[]{:S(2)}, u32[]{:S(2)}) collective-permute-start(f32[64,128]{1,0:T(8,128)S(1)} %add.35), channel_id=1, source_target_pairs={{0,12},{1,13},{2,14},{3,15},{4,8},{5,9},{6,10},{7,11},{8,4},{9,5},... | collective-permute-start | bytes 98312 | tf_op jit(solution)/shard_map/ppermute | solution.py:15
  94.3 5.5 %collective-permute-start.9 = (f32[64,128]{1,0:T(8,128)S(1)}, f32[64,128]{1,0:T(8,128)S(1)}, u32[]{:S(2)}, u32[]{:S(2)}) collective-permute-start(f32[64,128]{1,0:T(8,128)S(1)} %add.36), channel_id=1, source_target_pairs={{0,32},{16,48},{32,0},{48,16},{64,96},{80,112},{96,64},{112,80},{1... | collective-permute-start | bytes 98312 | tf_op jit(solution)/shard_map/ppermute | solution.py:15
  99.8 4.0 %collective-permute-start.10 = (f32[64,128]{1,0:T(8,128)S(1)}, f32[64,128]{1,0:T(8,128)S(1)}, u32[]{:S(2)}, u32[]{:S(2)}) collective-permute-start(f32[64,128]{1,0:T(8,128)S(1)} %add.37), channel_id=1, source_target_pairs={{0,96},{16,112},{32,64},{48,80},{64,32},{80,48},{96,0},{112,16},{1... | collective-permute-start | bytes 98312 | tf_op jit(solution)/shard_map/ppermute | solution.py:15
  103.8 7.4 %collective-permute-start.11 = (f32[64,128]{1,0:T(8,128)S(1)}, f32[64,128]{1,0:T(8,128)S(1)}, u32[]{:S(2)}, u32[]{:S(2)}) collective-permute-start(f32[64,128]{1,0:T(8,128)S(1)} %add.38.mine_ref), channel_id=1, source_target_pairs={{0,16},{16,0},{32,48},{48,32},{64,80},{80,64},{96,112},{112,96},{1... | collective-permute-start | bytes 98312 | tf_op jit(solution)/shard_map/ppermute | solution.py:15
  127.9 2.9 %collective-permute-start.12 = (f32[2048,128]{1,0:T(8,128)S(1)}, f32[2048,128]{1,0:T(8,128)S(1)}, u32[]{:S(2)}, u32[]{:S(2)}) collective-permute-start(f32[2048,128]{1,0:T(8,128)S(1)} %slice_bitcast_fusion), channel_id=1, source_target_pairs={{0,16},{16,0},{32,48},{48,32},{64,80},{80,64},{96,112},{112,96},{1... | collective-permute-start | bytes 3145736 | tf_op jit(solution)/shard_map/ppermute | solution.py:15
  173.0 4.6 %collective-permute-start.13 = (bf16[2048,128]{1,0:T(8,128)(2,1)S(1)}, bf16[2048,128]{1,0:T(8,128)(2,1)S(1)}, u32[]{:S(2)}, u32[]{:S(2)}) collective-permute-start(bf16[2048,128]{1,0:T(8,128)(2,1)S(1)} %bitcast.27), channel_id=1, source_target_pairs={{0,16},{16,0},{32,48},{48,32},{64,80},{80,64},{96,112},{112,96},{1... | collective-permute-start | bytes 1572872 | tf_op jit(solution)/shard_map/ppermute | solution.py:15
  191.1 2.7 %collective-permute-start.14 = (f32[2048,128]{1,0:T(8,128)S(1)}, f32[2048,128]{1,0:T(8,128)S(1)}, u32[]{:S(2)}, u32[]{:S(2)}) collective-permute-start(f32[2048,128]{1,0:T(8,128)S(1)} %slice_bitcast_fusion.2), channel_id=1, source_target_pairs={{0,16},{16,0},{32,48},{48,32},{64,80},{80,64},{96,112},{112,96},{1... | collective-permute-start | bytes 3145736 | tf_op jit(solution)/shard_map/ppermute | solution.py:15
  237.5 5.5 %collective-permute-start.15 = (f32[2048,128]{1,0:T(8,128)S(1)}, f32[2048,128]{1,0:T(8,128)S(1)}, u32[]{:S(2)}, u32[]{:S(2)}) collective-permute-start(f32[2048,128]{1,0:T(8,128)S(1)} %bitcast.24), channel_id=1, source_target_pairs={{0,16},{16,0},{32,48},{48,32},{64,80},{80,64},{96,112},{112,96},{1... | collective-permute-start | bytes 3145736 | tf_op jit(solution)/shard_map/ppermute | solution.py:15

commit v3 on v2

--- a/solution.py
+++ b/solution.py
@@ -9,6 +9,7 @@
 
 HIGH = lax.Precision.HIGHEST
 BOTH = ("gy", "gx")
+BORDER = 256
 
 
 def xor_permute(value, axis, mask):
@@ -27,25 +28,13 @@
     )
 
 
-def smooth_body(
-    core_ref, x_ref, top_ref, bot_ref, left_ref, right_ref, kern_ref, test_ref,
-    flat_ref, sketch_ref, keep_ref, send_ref, lt_ref, rt_ref, pad_ref,
-):
+def smooth_body(x_ref, kern_ref, test_ref, flat_ref, sketch_ref, gram_ref, pad_ref):
     step, steps = pl.program_id(0), pl.num_programs(0)
     rows, cols, width = x_ref.shape
     f32 = jnp.float32
     group = 8
     groups = rows // group
-
-    def ordered(edge_ref):
-        edge = edge_ref[...].astype(f32)
-        spare = jnp.zeros((group - 2, width), f32)
-        return jnp.concatenate(
-            [edge[rows : rows + 1], edge[:rows], edge[rows + 1 : rows + 2], spare], axis=0
-        )
-
-    lt_ref[...] = ordered(left_ref)
-    rt_ref[...] = ordered(right_ref)
+    sub = lax.broadcasted_iota(jnp.int32, (8, 128), 0)
 
     @pl.when(step == 0)
     def _():
@@ -64,23 +53,16 @@
                 [jnp.broadcast_to(kern_ref[a, b : b + 1, lanes], (cols, 128)) for b in range(3)]
                 for a in range(3)
             ]
-            lefts = lt_ref[pl.ds(base, 2 * group), lanes]
-            rights = rt_ref[pl.ds(base, 2 * group), lanes]
 
             def fetch(q):
+                place = base + q - 1
                 if q == 0:
-                    above = x_ref[jnp.maximum(base - 1, 0), :, lanes]
-                    row = jnp.where(g == 0, top_ref[:, lanes], above)
+                    place = jnp.maximum(place, 0)
                 elif q == group + 1:
-                    below = x_ref[jnp.minimum(base + group, rows - 1), :, lanes]
-                    row = jnp.where(g == groups - 1, bot_ref[:, lanes], below)
-                else:
-                    row = x_ref[base + q - 1, :, lanes]
-                row = row.astype(f32)
+                    place = jnp.minimum(place, rows - 1)
+                row = x_ref[place, :, lanes].astype(f32)
                 at = q * (cols + 16) + 8
-                pad[at - 1 : at, :] = lefts[q : q + 1]
                 pad[at : at + cols, :] = row
-                pad[at + cols : at + cols + 1, :] = rights[q : q + 1]
                 return [pad[at - 1 : at - 1 + cols, :], row, pad[at + 1 : at + 1 + cols, :]]
 
             near = [fetch(0), fetch(1)]
@@ -91,6 +73,13 @@
                     for b in range(3):
                         term = taps[a][b] * near[a][b]
                         total = term if total is None else total + term
+                head = jnp.where(sub == 0, 0.0, total[:8])
+                tail = jnp.where(sub == 7, 0.0, total[cols - 8 :])
+                total = jnp.concatenate([head, total[8 : cols - 8], tail], axis=0)
+                if r == 0:
+                    total = jnp.where(g == 0, 0.0, total)
+                if r == group - 1:
+                    total = jnp.where(g == groups - 1, 0.0, total)
                 start = pl.multiple_of((base + r) * cols, cols)
                 flat_ref[pl.ds(start, cols), lanes] = total.astype(jnp.bfloat16)
 
@@ -107,10 +96,116 @@
 
     @pl.when(step == steps - 1)
     def _():
-        values = sketch_ref[...]
-        gram = lax.dot_general(
-            values, values, (((0,), (0,)), ((), ())), precision=HIGH, preferred_element_type=f32
-        )
+        gram_ref[...] = gram_of(sketch_ref[...])
+
+
+def gram_of(values):
+    return lax.dot_general(
+        values, values, (((0,), (0,)), ((), ())), precision=HIGH,
+        preferred_element_type=jnp.float32,
+    )
+
+
+def smooth_sketch(x, kernel, test_matrix):
+    rows, cols, channels = x.shape
+    k = test_matrix.shape[1]
+    width = 512
+    total = rows * cols + BORDER
+    fixed = lambda n: pl.BlockSpec((n, k), lambda j: (0, 0))
+    return pl.pallas_call(
+        smooth_body,
+        grid=(channels // width,),
+        in_specs=[
+            pl.BlockSpec((rows, cols, width), lambda j: (0, 0, j)),
+            pl.BlockSpec((3, 3, width), lambda j: (0, 0, j)),
+            pl.BlockSpec((width, k), lambda j: (j, 0)),
+        ],
+        out_specs=[
+            pl.BlockSpec((rows * cols, width), lambda j: (0, j)), fixed(rows * cols), fixed(k),
+        ],
+        out_shape=[
+            jax.ShapeDtypeStruct((total, channels), jnp.bfloat16),
+            jax.ShapeDtypeStruct((total, k), jnp.float32),
+            jax.ShapeDtypeStruct((k, k), jnp.float32),
+        ],
+        scratch_shapes=[pltpu.VMEM((2, 10 * (cols + 16), 128), jnp.float32)],
+        compiler_params=params(54, 1),
+        cost_estimate=pl.CostEstimate(
+            flops=2 * rows * cols * channels * (k + 900), transcendentals=0,
+            bytes_accessed=4 * rows * cols * channels,
+        ),
+        name="smooth_sketch",
+    )(x, kernel, test_matrix)
+
+
+def border_body(
+    core_ref, upper_ref, lower_ref, c0_ref, c1_ref, c2_ref, c3_ref, top_ref, bot_ref,
+    left_ref, right_ref, kern_ref, test_ref, gram_ref, flat_in_ref, sketch_in_ref,
+    edge_ref, sketch_ref, keep_ref, send_ref,
+):
+    step, steps = pl.program_id(0), pl.num_programs(0)
+    cols, width = top_ref.shape
+    rows = c1_ref.shape[0]
+    f32 = jnp.float32
+    left, right = left_ref[...].astype(f32), right_ref[...].astype(f32)
+    top, bot = top_ref[...].astype(f32), bot_ref[...].astype(f32)
+    taps = [[kern_ref[a, b : b + 1, :] for b in range(3)] for a in range(3)]
+
+    def along_row(pixels, lefts, rights):
+        total = None
+        for a in range(3):
+            before = jnp.concatenate([lefts[a], pixels[a][:-1]], axis=0)
+            behind = jnp.concatenate([pixels[a][1:], rights[a]], axis=0)
+            for b, moved in enumerate((before, pixels[a], behind)):
+                term = taps[a][b] * moved
+                total = term if total is None else total + term
+        return total
+
+    def along_column(columns):
+        total = None
+        for b in range(3):
+            middle, above, below = columns[b]
+            up = jnp.concatenate([above, middle[:-1]], axis=0)
+            down = jnp.concatenate([middle[1:], below], axis=0)
+            for a, moved in enumerate((up, middle, down)):
+                term = taps[a][b] * moved
+                total = term if total is None else total + term
+        place = lax.broadcasted_iota(jnp.int32, total.shape, 0)
+        return jnp.where((place == 0) | (place == rows - 1), 0.0, total)
+
+    upper, lower = upper_ref[...].astype(f32), lower_ref[...].astype(f32)
+    own = [r[...].astype(f32) for r in (c0_ref, c1_ref, c2_ref, c3_ref)]
+    take = lambda v, i: v[i : i + 1]
+    first_row = along_row(
+        (top, upper[0], upper[1]),
+        (take(left, rows), take(left, 0), take(left, 1)),
+        (take(right, rows), take(right, 0), take(right, 1)),
+    )
+    last_row = along_row(
+        (lower[0], lower[1], bot),
+        (take(left, rows - 2), take(left, rows - 1), take(left, rows + 1)),
+        (take(right, rows - 2), take(right, rows - 1), take(right, rows + 1)),
+    )
+    halo = lambda v: (v[:rows], take(v, rows), take(v, rows + 1))
+    ours = lambda i, w: (own[i][:rows], take(top, w), take(bot, w))
+    first_column = along_column((halo(left), ours(0, 0), ours(1, 1)))
+    last_column = along_column((ours(2, cols - 2), ours(3, cols - 1), halo(right)))
+    spare = jnp.zeros((BORDER - 2 * (rows + cols), width), f32)
+    edge = jnp.concatenate([first_row, last_row, first_column, last_column, spare], axis=0)
+    edge_ref[...] = edge.astype(jnp.bfloat16)
+    part = jnp.dot(edge_ref[...], test_ref[...], preferred_element_type=f32)
+
+    @pl.when(step == 0)
+    def _():
+        sketch_ref[...] = part
+
+    @pl.when(step > 0)
+    def _():
+        sketch_ref[...] += part
+
+    @pl.when(step == steps - 1)
+    def _():
+        gram = gram_ref[...] + gram_of(sketch_ref[...])
         half = keep_ref.shape[0]
 
         @pl.when(core_ref[0] == 0)
@@ -124,71 +219,87 @@
             send_ref[...] = gram[:half]
 
 
-def smooth_sketch(core, x, halos, kernel, test_matrix):
+def border_sketch(core, x, columns, halos, kernel, test_matrix, gram, flat, sketch):
     rows, cols, channels = x.shape
     k = test_matrix.shape[1]
-    width = 512
-    edge = lambda n: pl.BlockSpec((n, width), lambda j, core: (0, j))
-    fixed = lambda n: pl.BlockSpec((n, k), lambda j, core: (0, 0))
+    width = 1024
+    edge = lambda n, at=0: pl.BlockSpec((n, width), lambda j, core: (at, j))
+    fixed = lambda n, at=0: pl.BlockSpec((n, k), lambda j, core: (at, 0))
+    behind = rows * cols // BORDER
     return pl.pallas_call(
-        smooth_body,
+        border_body,
         grid_spec=pltpu.PrefetchScalarGridSpec(
             num_scalar_prefetch=1,
             grid=(channels // width,),
             in_specs=[
-                pl.BlockSpec((rows, cols, width), lambda j, core: (0, 0, j)),
+                pl.BlockSpec((2, cols, width), lambda j, core: (0, 0, j)),
+                pl.BlockSpec((2, cols, width), lambda j, core: (rows // 2 - 1, 0, j)),
+                edge(rows + 8), edge(rows), edge(rows), edge(rows + 8),
                 edge(cols), edge(cols), edge(rows + 8), edge(rows + 8),
                 pl.BlockSpec((3, 3, width), lambda j, core: (0, 0, j)),
                 pl.BlockSpec((width, k), lambda j, core: (j, 0)),
+                fixed(k),
+                pl.BlockSpec(memory_space=pl.ANY),
+                pl.BlockSpec(memory_space=pl.ANY),
             ],
-            out_specs=[edge(rows * cols), fixed(rows * cols), fixed(k // 2), fixed(k // 2)],
-            scratch_shapes=[pltpu.VMEM((rows + 8, width), jnp.float32)] * 2
-            + [pltpu.VMEM((2, 10 * (cols + 16), 128), jnp.float32)],
+            out_specs=[edge(BORDER, behind), fixed(BORDER, behind), fixed(k // 2), fixed(k // 2)],
         ),
         out_shape=[
-            jax.ShapeDtypeStruct((rows * cols, channels), jnp.bfloat16),
-            jax.ShapeDtypeStruct((rows * cols, k), jnp.float32),
+            jax.ShapeDtypeStruct(flat.shape, flat.dtype),
+            jax.ShapeDtypeStruct(sketch.shape, sketch.dtype),
             jax.ShapeDtypeStruct((k // 2, k), jnp.float32),
             jax.ShapeDtypeStruct((k // 2, k), jnp.float32),
         ],
-        compiler_params=params(40, 1),
-        name="smooth_sketch",
-    )(core, x, *halos, kernel, test_matrix)
-
-
-def columns_body(x_ref, top_ref, bot_ref, first_ref, last_ref, low_ref, high_ref, sems):
-    rows, cols, _ = x_ref.shape
-    copies = [
-        pltpu.make_async_copy(x_ref.at[:, pl.ds(0, 8), :], low_ref, sems.at[0]),
-        pltpu.make_async_copy(x_ref.at[:, pl.ds(cols - 8, 8), :], high_ref, sems.at[1]),
-    ]
-    for copy in copies:
-        copy.start()
-    for copy, place, held_ref, out_ref in zip(
-        copies, (0, cols - 1), (low_ref, high_ref), (first_ref, last_ref)
-    ):
-        copy.wait()
-        for lane in range(0, out_ref.shape[1], 512):
-            lanes = slice(lane, lane + 512)
-            column = held_ref[:, :, lanes].astype(jnp.float32)[:, place % 8]
-            ends = [r[:, lanes].astype(jnp.float32)[place : place + 1] for r in (top_ref, bot_ref)]
-            spare = jnp.zeros((6, 512), jnp.float32)
-            joined = jnp.concatenate([column] + ends + [spare], axis=0)
-            out_ref[:, lanes] = joined.astype(jnp.bfloat16)
+        input_output_aliases={14: 0, 15: 1},
+        compiler_params=params(52, 1),
+        name="border_sketch",
+    )(core, x, x, *columns, *halos, kernel, test_matrix, gram, flat, sketch)
+
+
+def columns_body(low_ref, high_ref, top_ref, bot_ref, c0_ref, c1_ref, c2_ref, c3_ref):
+    rows, _, width = low_ref.shape
+    cols = top_ref.shape[0]
+    f32, bf16 = jnp.float32, jnp.bfloat16
+    out_id = lax.broadcasted_iota(jnp.int32, (2 * rows, 8 * rows), 0)
+    in_id = lax.broadcasted_iota(jnp.int32, (2 * rows, 8 * rows), 1)
+    spare = jnp.zeros((6, width), f32)
+
+    def cut(held_ref, at):
+        wanted = (out_id % rows) * 8 + at + out_id // rows
+        pick = jnp.where(in_id == wanted, 1.0, 0.0).astype(bf16)
+        held = held_ref[...].reshape(8 * rows, width)
+        return jnp.dot(pick, held, preferred_element_type=f32)
+
+    def with_ends(column, place):
+        ends = [r[...].astype(f32)[place : place + 1] for r in (top_ref, bot_ref)]
+        return jnp.concatenate([column] + ends + [spare], axis=0).astype(bf16)
+
+    low, high = cut(low_ref, 0), cut(high_ref, 6)
+    c0_ref[...] = with_ends(low[:rows], 0)
+    c1_ref[...] = low[rows:].astype(bf16)
+    c2_ref[...] = high[:rows].astype(bf16)
+    c3_ref[...] = with_ends(high[rows:], cols - 1)
 
 
 def edge_columns(x, top, bottom):
     rows, cols, channels = x.shape
+    width = 1024
+    edge = lambda n: pl.BlockSpec((n, width), lambda j: (0, j))
     return pl.pallas_call(
         columns_body,
-        in_specs=[pl.BlockSpec(memory_space=pltpu.HBM)]
-        + [pl.BlockSpec(memory_space=pltpu.VMEM)] * 2,
-        out_shape=[jax.ShapeDtypeStruct((rows + 8, channels), x.dtype)] * 2,
-        scratch_shapes=[pltpu.VMEM((rows, 8, channels), x.dtype)] * 2
-        + [pltpu.SemaphoreType.DMA((2,))],
-        compiler_params=params(20),
+        grid=(channels // width,),
+        in_specs=[
+            pl.BlockSpec((rows, 8, width), lambda j: (0, 0, j)),
+            pl.BlockSpec((rows, 8, width), lambda j: (0, cols // 8 - 1, j)),
+            edge(cols), edge(cols),
+        ],
+        out_specs=[edge(rows + 8), edge(rows), edge(rows), edge(rows + 8)],
+        out_shape=[
+            jax.ShapeDtypeStruct((n, channels), x.dtype) for n in (rows + 8, rows, rows, rows + 8)
+        ],
+        compiler_params=params(52, 1),
         name="edge_columns",
-    )(x, top, bottom)
+    )(x, x, top, bottom)
 
 
 def factor_block(panel, low, sub, lane):
@@ -332,7 +443,7 @@
 def second_step(core, flat, range_map):
     pixels, channels = flat.shape
     k = range_map.shape[1]
-    height = 512
+    height = 768
     return pl.pallas_call(
         second_body,
         grid_spec=pltpu.PrefetchScalarGridSpec(
@@ -352,24 +463,35 @@
             jax.ShapeDtypeStruct((pixels, k), jnp.float32),
             jax.ShapeDtypeStruct((2, channels // 2, k), jnp.float32),
         ],
-        compiler_params=params(44, 1),
+        compiler_params=params(48, 1),
         name="second_step",
     )(core, flat, range_map)
 
 
-def finish_body(basis_scale, coeff_scale, range_ref, moment_ref, second_ref, basis_ref, coeffs_ref, work_ref):
+def finish_body(
+    basis_scale, coeff_scale, range_ref, moment_ref, second_ref,
+    basis_ref, coeffs_ref, work_ref,
+):
+    rows, cols, k = basis_ref.shape
     moment = moment_ref[...]
-    gram = lax.dot_general(
+    work_ref[...] = lax.dot_general(
         range_ref[...].astype(jnp.float32), moment, (((0,), (0,)), ((), ())), precision=HIGH,
         preferred_element_type=jnp.float32,
     )
-    work_ref[...] = gram
     inverse = inverse_factor(work_ref)
-    basis_ref[...] = times_transposed(second_ref[...], inverse) * basis_scale
+    basis = times_transposed(second_ref[...], inverse) * basis_scale
+    inner = basis[: rows * cols].reshape(rows, cols, k)
+    border = basis[rows * cols :]
+    place = lax.broadcasted_iota(jnp.int32, inner.shape, 1)
+    first = border[2 * cols : 2 * cols + rows].reshape(rows, 1, k)
+    last = border[2 * cols + rows : 2 * (cols + rows)].reshape(rows, 1, k)
+    basis_ref[...] = jnp.where(place == 0, first, jnp.where(place == cols - 1, last, inner))
+    basis_ref[0] = border[:cols]
+    basis_ref[rows - 1] = border[cols : 2 * cols]
     coeffs_ref[...] = times_transposed(inverse, moment) * coeff_scale
 
 
-def finish(range_map, moment, second, basis_scale, coeff_scale):
+def finish(range_map, moment, second, tile, basis_scale, coeff_scale):
     channels, k = moment.shape
 
     def body(*refs):
@@ -378,7 +500,7 @@
     return pl.pallas_call(
         body,
         out_shape=[
-            jax.ShapeDtypeStruct(second.shape, jnp.float32),
+            jax.ShapeDtypeStruct(tile + (k,), jnp.float32),
             jax.ShapeDtypeStruct((k, channels), jnp.float32),
         ],
         scratch_shapes=[pltpu.VMEM((k, k), jnp.float32)],
@@ -412,12 +534,15 @@
 
     top = shift_permute(radiance[-1], "gy", 1)
     bottom = shift_permute(radiance[0], "gy", -1)
-    first, last = edge_columns(radiance, top, bottom)
-    left = shift_permute(last, "gx", 1)
-    right = shift_permute(first, "gx", -1)
+    columns = edge_columns(radiance, top, bottom)
+    left = shift_permute(columns[3], "gx", 1)
+    right = shift_permute(columns[0], "gx", -1)
     halos = (top, bottom, left, right)
 
-    flat, sketch, mine, send = smooth_sketch(core_arg, radiance, halos, kernel, test_matrix)
+    flat, sketch, gram = smooth_sketch(radiance, kernel, test_matrix)
+    flat, sketch, mine, send = border_sketch(
+        core_arg, radiance, columns, halos, kernel, test_matrix, gram, flat, sketch
+    )
     mine = mine + xor_permute(send, "gy", 1)
     for axis, mask in (("gx", 1), ("gx", 3), ("gx", 4), ("gx", 12), ("gy", 2), ("gy", 6)):
         mine = mine + xor_permute(mine, axis, mask)
@@ -426,10 +551,10 @@
     second, pair = second_step(core_arg, flat, range_map)
     moment = all_sum(pair, core, jnp.float32)
     scale = math.sqrt(pixel_count)
-    basis_out, coeffs = finish(
-        range_map, moment, second, scale, scale * math.sqrt(channels) / pixel_count
-    )
-    return (basis_out.reshape(height, breadth, basis_out.shape[1]), coeffs)
+    return finish(
+        range_map, moment, second, (height, breadth),
+        scale, scale * math.sqrt(channels) / pixel_count,
+    )
 
 
 def solution(mesh):

time: 255 us -> 248 us (0.973)
  waiting for transfers between devices: 38.3 us -> 25.2 us
  Pallas kernels: 82.6 us -> 92.3 us
  local copies, waits for them, and re-layouts: 7.17 us -> 4.52 us
    ppermute x4, waiting for transfers between devices: 17.9 us -> 5.77 us  [shift_permute(): return lax.ppermute(value, axis, pairs)]
    pallas_call x3 -> x4, Pallas kernels: 52.8 us -> 60.7 us  [the longest x1 35.7 us: smooth_sketch(): pl.pallas_call(smooth_body, grid=(channels // width,), in_specs=[pl.Block...]
    unnamed x6 -> x10, local copies, waits for them, and re-layouts: 5.78 us -> 3.12 us
  transfers between devices with their start and end apart: 16 -> 16, of which waited for: 16 -> 14; matrix products, arithmetic and copies ran while one was open for 0% -> 0% of each run, Pallas kernels for 0% -> 14%
where the time goes in v3:
time: 248 us
  Pallas kernels  92.3 us (37%)
  blocking collectives  84.3 us (34%)
  starting transfers between devices  39.6 us (16%)
  waiting for transfers between devices  25.2 us (10%)
  local copies, waits for them, and re-layouts  4.52 us (2%)
    all_to_all x4, blocking collectives, all_sum(): lax.all_to_all(v, BOTH, 0, 0, axis_index_groups=groups, tiled=True)  84.3 us
    pallas_call x1, Pallas kernels, smooth_sketch(): pl.pallas_call(smooth_body, grid=(channels // width,), in_specs=[pl.Block...  35.7 us
    ppermute x12, starting transfers between devices, xor_permute(): lax.ppermute(value, axis, [(i, i ^ mask) for i in range(lax.axis_size(axi...  28.2 us
    ppermute x12, waiting for transfers between devices, xor_permute(): lax.ppermute(value, axis, [(i, i ^ mask) for i in range(lax.axis_size(axi...  19.4 us
    pallas_call x1, Pallas kernels, project(): pl.pallas_call(project_body, grid_spec=pltpu.PrefetchScalarGridSpec(num_s...  17.3 us
    pallas_call x1, Pallas kernels, second_step(): pl.pallas_call(second_body, grid_spec=pltpu.PrefetchScalarGridSpec(num_sc...  14.4 us
    pallas_call x1, Pallas kernels, finish(): pl.pallas_call(body, out_shape=[jax.ShapeDtypeStruct(tile + (k,), jnp.flo...  11.9 us
    ppermute x4, starting transfers between devices, shift_permute(): return lax.ppermute(value, axis, pairs)  11.4 us
  transfers between devices with their start and end apart: 16, of which 14 were waited for; matrix products, arithmetic and copies ran while one was open for 0% of the time, Pallas kernels for 14%

profile of v3, /device:TPU:1, one launch (start us, length us, event | category | flops | bytes accessed | tf_op | source)
XLA Modules:
  0.0 247.6 jit_solution(9862498374689928961)
XLA Ops:
  0.6 1.1 slice_bitcast_fusion.3
  1.7 4.9 %collective-permute-start = (bf16[32,4096]{1,0:T(8,128)(2,1)S(1)}, bf16[32,4096]{1,0:T(8,128)(2,1)S(1)}, u32[]{:S(2)}, u32[]{:S(2)}) collective-permute-start(bf16[32,4096]{1,0:T(8,128)(2,1)S(1)} %get-tuple-element.29), channel_id=1, source_target_pairs={{0,16},{16,32},{32,48},{48,64},{64,80},{80,96},{96,112},{1,17},{17... | collective-permute-start | bytes 786440 | tf_op jit(solution)/shard_map/ppermute | solution.py:22
  6.6 1.9 collective-permute-start.1
  8.6 1.4 collective-permute-done.top_ref
  9.9 4.4 %collective-permute-done.1.bot_ref = bf16[32,4096]{1,0:T(8,128)(2,1)S(1)} collective-permute-done((bf16[32,4096]{1,0:T(8,128)(2,1)S(1)}, bf16[32,4096]{1,0:T(8,128)(2,1)S(1)}, u32[]{:S(2)}, u32[]{:S(2)}) %collective-permute-start.1) | collective-permute-done | bytes 262176 | tf_op jit(solution)/shard_map/ppermute | solution.py:22
  14.3 5.6 %edge_columns.1 = (bf16[72,4096]{1,0:T(8,128)(2,1)}, bf16[64,4096]{1,0:T(8,128)(2,1)S(1)}, bf16[64,4096]{1,0:T(8,128)(2,1)S(1)}, bf16[72,4096]{1,0:T(8,128)(2,1)}) custom-call(bf16[64,32,4096]{2,1,0:T(8,128)(2,1)} %lower_ref.1, bf16[64,32,4096]{2,1,0:T(8,128)(2,1)} %lower_ref.1, bf16[32,4096]{1,0:T(8,128)(2,1)S(1)} %collective-permute-done.top_ref, ...), custom_call_target="tpu_custom_call" | custom-call | tf_op jit(solution)/shard_map/edge_columns/pallas_call | solution.py:288
  20.0 3.1 %collective-permute-start.2 = (bf16[72,4096]{1,0:T(8,128)(2,1)}, bf16[72,4096]{1,0:T(8,128)(2,1)S(1)}, u32[]{:S(2)}, u32[]{:S(2)}) collective-permute-start(bf16[72,4096]{1,0:T(8,128)(2,1)} %get-tuple-element.18.c3_ref), channel_id=1, source_target_pairs={{0,1},{1,2},{2,3},{3,4},{4,5},{5,6},{6,7},{7,8},{8,9},{9,10},{10,1... | collective-permute-start | bytes 1769480 | tf_op jit(solution)/shard_map/ppermute | solution.py:22
  23.1 0.0 copy-start.1
  23.1 1.4 collective-permute-start.3
  24.6 35.7 %smooth_sketch.1 = (bf16[2304,4096]{1,0:T(8,128)(2,1)}, f32[2304,128]{1,0:T(8,128)}, f32[128,128]{1,0:T(8,128)}) custom-call(bf16[64,32,4096]{2,1,0:T(8,128)(2,1)} %lower_ref.1, f32[3,3,4096]{2,1,0:T(4,128)} %kern_ref.3, bf16[4096,128]{1,0:T(8,128)(2,1)} %test_ref.3), custom_call_target="tpu_custom_call" | custom-call | flops 17246978048 | bytes 33554432 | tf_op jit(solution)/shard_map/smooth_sketch/pallas_call | solution.py:115
  60.3 0.0 collective-permute-done.2.left_ref
  60.3 0.0 copy-start.3
  60.3 0.0 collective-permute-done.3.right_ref
  60.3 0.0 copy-start.4
  60.3 0.8 copy-done.3
  61.1 0.2 copy-done.4
  61.3 0.0 copy-done.1
  61.3 0.0 copy-start.2
  61.3 0.8 copy-done.2
  62.1 7.4 %border_sketch.1 = (bf16[2304,4096]{1,0:T(8,128)(2,1)}, f32[2304,128]{1,0:T(8,128)}, f32[64,128]{1,0:T(8,128)S(1)}, f32[64,128]{1,0:T(8,128)S(1)}) custom-call(s32[1]{0:T(128)} %bitcast.core_ref, bf16[64,32,4096]{2,1,0:T(8,128)(2,1)} %lower_ref.1, bf16[64,32,4096]{2,1,0:T(8,128)(2,1)} %lower_ref.1, ...), custom_call_target="tpu_custom_call", output_to_operand_aliasing={{0}: (14, {}), {1}: (15, {})} | custom-call | tf_op jit(solution)/shard_map/border_sketch/pallas_call | solution.py:229
  69.5 0.0 collective-permute-start.4
  69.5 1.2 collective-permute-done.4
  70.7 2.1 collective-permute-start.5
  72.8 1.6 collective-permute-done.5
  74.4 2.4 collective-permute-start.6
  76.8 1.6 collective-permute-done.6
  78.4 3.3 %collective-permute-start.7 = (f32[64,128]{1,0:T(8,128)S(1)}, f32[64,128]{1,0:T(8,128)S(1)}, u32[]{:S(2)}, u32[]{:S(2)}) collective-permute-start(f32[64,128]{1,0:T(8,128)S(1)} %add.34), channel_id=1, source_target_pairs={{0,4},{1,5},{2,6},{3,7},{4,0},{5,1},{6,2},{7,3},{8,12},{9,13},{10,... | collective-permute-start | bytes 98312 | tf_op jit(solution)/shard_map/ppermute | solution.py:16
  81.7 1.3 collective-permute-done.7
  83.0 2.9 %collective-permute-start.8 = (f32[64,128]{1,0:T(8,128)S(1)}, f32[64,128]{1,0:T(8,128)S(1)}, u32[]{:S(2)}, u32[]{:S(2)}) collective-permute-start(f32[64,128]{1,0:T(8,128)S(1)} %add.35), channel_id=1, source_target_pairs={{0,12},{1,13},{2,14},{3,15},{4,8},{5,9},{6,10},{7,11},{8,4},{9,5},... | collective-permute-start | bytes 98312 | tf_op jit(solution)/shard_map/ppermute | solution.py:16
  85.9 1.3 collective-permute-done.8
  87.2 1.6 collective-permute-start.9
  88.9 1.3 collective-permute-done.9
  90.2 2.1 collective-permute-start.10
  92.3 1.9 collective-permute-done.10
  94.2 6.6 %collective-permute-start.11 = (f32[64,128]{1,0:T(8,128)S(1)}, f32[64,128]{1,0:T(8,128)S(1)}, u32[]{:S(2)}, u32[]{:S(2)}) collective-permute-start(f32[64,128]{1,0:T(8,128)S(1)} %add.38.mine_ref), channel_id=1, source_target_pairs={{0,16},{16,0},{32,48},{48,32},{64,80},{80,64},{96,112},{112,96},{1... | collective-permute-start | bytes 98312 | tf_op jit(solution)/shard_map/ppermute | solution.py:16
  100.8 0.9 collective-permute-done.11.other_ref
  101.6 1.3 copy-done
  102.9 17.3 %project.1 = f32[2,2048,128]{2,1,0:T(8,128)S(1)} custom-call(s32[1]{0:T(128)} %bitcast.core_ref, f32[64,128]{1,0:T(8,128)S(1)} %add.38.mine_ref, f32[64,128]{1,0:T(8,128)S(1)} %collective-permute-done.11.other_ref, f32[2304,128]{1,0:T(8,128)S(1)} %copy-done, bf16[2304,4096]{1,0:T(8,128)(2,1)} %get-tuple-element.25.flat_ref), custom_call_target="tpu_custom_call" | custom-call | tf_op jit(solution)/shard_map/project/pallas_call | solution.py:395
  120.2 0.1 slice_bitcast_fusion
  120.3 0.4 collective-permute-start.12
  120.7 2.3 collective-permute-done.12
  123.0 0.1 fusion
  123.1 25.4 %all_to_all.20 = f32[64,32,128]{2,1,0:T(8,128)S(1)} all-to-all(f32[64,32,128]{2,1,0:T(8,128)S(1)} %bitcast.24), channel_id=1, replica_groups={{0,1,2,3,4,5,6,7,8,9,10,11,12,13,14,15,32,33,34,35,36,37,38,39,40,41,42..., dimensions={0} | all-to-all | bytes 2097152 | tf_op jit(solution)/shard_map/all_to_all | solution.py:517
  148.6 0.1 reduce_sum.18
  148.7 0.1 broadcast_in_dim.4
  148.8 15.5 %all_to_all.21 = bf16[64,32,128]{2,1,0:T(8,128)(2,1)S(1)} all-to-all(bf16[64,32,128]{2,1,0:T(8,128)(2,1)S(1)} %broadcast_in_dim.4), channel_id=1, replica_groups={{0,1,2,3,4,5,6,7,8,9,10,11,12,13,14,15,32,33,34,35,36,37,38,39,40,41,42..., dimensions={0} | all-to-all | bytes 1048576 | tf_op jit(solution)/shard_map/all_to_all | solution.py:517
  164.3 3.1 %collective-permute-start.13 = (bf16[2048,128]{1,0:T(8,128)(2,1)S(1)}, bf16[2048,128]{1,0:T(8,128)(2,1)S(1)}, u32[]{:S(2)}, u32[]{:S(2)}) collective-permute-start(bf16[2048,128]{1,0:T(8,128)(2,1)S(1)} %bitcast.26), channel_id=1, source_target_pairs={{0,16},{16,0},{32,48},{48,32},{64,80},{80,64},{96,112},{112,96},{1... | collective-permute-start | bytes 1572872 | tf_op jit(solution)/shard_map/ppermute | solution.py:16
  167.4 1.5 collective-permute-done.13
  168.9 0.1 broadcast_select_fusion.3
  169.0 0.1 pad_maximum_fusion.1.range_ref.refs_0_
  169.1 14.4 %second_step.1 = (f32[2304,128]{1,0:T(8,128)S(1)}, f32[2,2048,128]{2,1,0:T(8,128)S(1)}) custom-call(s32[1]{0:T(128)} %bitcast.core_ref, bf16[2304,4096]{1,0:T(8,128)(2,1)} %get-tuple-element.25.flat_ref, bf16[4096,128]{1,0:T(8,128)(2,1)S(1)} %pad_maximum_fusion.1.range_ref.refs_0_), custom_call_target="tpu_custom_call" | custom-call | tf_op jit(solution)/shard_map/second_step/pallas_call | solution.py:447
  183.5 0.1 slice_bitcast_fusion.2
  183.5 0.4 collective-permute-start.14
  184.0 2.3 collective-permute-done.14
  186.3 0.1 bitcast_add_fusion
  186.4 22.3 %all_to_all.22 = f32[64,32,128]{2,1,0:T(8,128)S(1)} all-to-all(f32[64,32,128]{2,1,0:T(8,128)S(1)} %bitcast.25), channel_id=1, replica_groups={{0,1,2,3,4,5,6,7,8,9,10,11,12,13,14,15,32,33,34,35,36,37,38,39,40,41,42..., dimensions={0} | all-to-all | bytes 2097152 | tf_op jit(solution)/shard_map/all_to_all | solution.py:517
  208.7 0.1 reduce_sum.19
  208.8 0.1 broadcast_in_dim.5
  208.9 21.0 %all_to_all.23 = f32[64,32,128]{2,1,0:T(8,128)S(1)} all-to-all(f32[64,32,128]{2,1,0:T(8,128)S(1)} %broadcast_in_dim.5), channel_id=1, replica_groups={{0,1,2,3,4,5,6,7,8,9,10,11,12,13,14,15,32,33,34,35,36,37,38,39,40,41,42..., dimensions={0} | all-to-all | bytes 2097152 | tf_op jit(solution)/shard_map/all_to_all | solution.py:517
  229.9 3.2 %collective-permute-start.15 = (f32[2048,128]{1,0:T(8,128)S(1)}, f32[2048,128]{1,0:T(8,128)S(1)}, u32[]{:S(2)}, u32[]{:S(2)}) collective-permute-start(f32[2048,128]{1,0:T(8,128)S(1)} %bitcast.23), channel_id=1, source_target_pairs={{0,16},{16,0},{32,48},{48,32},{64,80},{80,64},{96,112},{112,96},{1... | collective-permute-start | bytes 3145736 | tf_op jit(solution)/shard_map/ppermute | solution.py:16
  233.1 2.3 collective-permute-done.15
  235.4 0.1 broadcast_select_fusion.1
  235.5 0.1 pad_maximum_fusion.refs_1_
  235.7 11.9 %finish.1 = (f32[64,32,128]{2,1,0:T(8,128)}, f32[128,4096]{1,0:T(8,128)}) custom-call(bf16[4096,128]{1,0:T(8,128)(2,1)S(1)} %pad_maximum_fusion.1.range_ref.refs_0_, f32[4096,128]{1,0:T(8,128)S(1)} %pad_maximum_fusion.refs_1_, f32[2304,128]{1,0:T(8,128)S(1)} %get-tuple-element.27.refs_2_), custom_call_target="tpu_custom_call" | custom-call | tf_op jit(solution)/shard_map/finish/pallas_call | solution.py:500
  (8 shorter events, 0.0 us)
Async XLA Ops:
  1.7 8.2 %collective-permute-start = (bf16[32,4096]{1,0:T(8,128)(2,1)S(1)}, bf16[32,4096]{1,0:T(8,128)(2,1)S(1)}, u32[]{:S(2)}, u32[]{:S(2)}) collective-permute-start(bf16[32,4096]{1,0:T(8,128)(2,1)S(1)} %get-tuple-element.29), channel_id=1, source_target_pairs={{0,16},{16,32},{32,48},{48,64},{64,80},{80,96},{96,112},{1,17},{17... | collective-permute-start | bytes 786440 | tf_op jit(solution)/shard_map/ppermute | solution.py:22
  6.6 7.7 %collective-permute-start.1 = (bf16[32,4096]{1,0:T(8,128)(2,1)S(1)}, bf16[32,4096]{1,0:T(8,128)(2,1)S(1)}, u32[]{:S(2)}, u32[]{:S(2)}) collective-permute-start(bf16[32,4096]{1,0:T(8,128)(2,1)S(1)} %get-tuple-element.28), channel_id=1, source_target_pairs={{16,0},{32,16},{48,32},{64,48},{80,64},{96,80},{112,96},{17,1},{33... | collective-permute-start | bytes 786440 | tf_op jit(solution)/shard_map/ppermute | solution.py:22
  20.0 40.3 %collective-permute-start.2 = (bf16[72,4096]{1,0:T(8,128)(2,1)}, bf16[72,4096]{1,0:T(8,128)(2,1)S(1)}, u32[]{:S(2)}, u32[]{:S(2)}) collective-permute-start(bf16[72,4096]{1,0:T(8,128)(2,1)} %get-tuple-element.18.c3_ref), channel_id=1, source_target_pairs={{0,1},{1,2},{2,3},{3,4},{4,5},{5,6},{6,7},{7,8},{8,9},{9,10},{10,1... | collective-permute-start | bytes 1769480 | tf_op jit(solution)/shard_map/ppermute | solution.py:22
  23.1 38.2 %copy-start.1 = (f32[3,3,4096]{2,1,0:T(4,128)S(1)}, f32[3,3,4096]{2,1,0:T(4,128)}, u32[]{:S(2)}) copy-start(f32[3,3,4096]{2,1,0:T(4,128)} %kern_ref.3) | copy-start | bytes 442372
  23.1 37.2 %collective-permute-start.3 = (bf16[72,4096]{1,0:T(8,128)(2,1)}, bf16[72,4096]{1,0:T(8,128)(2,1)S(1)}, u32[]{:S(2)}, u32[]{:S(2)}) collective-permute-start(bf16[72,4096]{1,0:T(8,128)(2,1)} %get-tuple-element.15.c0_ref), channel_id=1, source_target_pairs={{1,0},{2,1},{3,2},{4,3},{5,4},{6,5},{7,6},{8,7},{9,8},{10,9},{11,1... | collective-permute-start | bytes 1769480 | tf_op jit(solution)/shard_map/ppermute | solution.py:22
  60.3 0.8 copy-start.3
  60.3 1.0 copy-start.4
  61.3 0.8 copy-start.2
  69.5 1.2 collective-permute-start.4
  70.7 3.7 %collective-permute-start.5 = (f32[64,128]{1,0:T(8,128)S(1)}, f32[64,128]{1,0:T(8,128)S(1)}, u32[]{:S(2)}, u32[]{:S(2)}) collective-permute-start(f32[64,128]{1,0:T(8,128)S(1)} %add.32), channel_id=1, source_target_pairs={{0,1},{1,0},{2,3},{3,2},{4,5},{5,4},{6,7},{7,6},{8,9},{9,8},{10,11... | collective-permute-start | bytes 98312 | tf_op jit(solution)/shard_map/ppermute | solution.py:16
  74.4 4.0 %collective-permute-start.6 = (f32[64,128]{1,0:T(8,128)S(1)}, f32[64,128]{1,0:T(8,128)S(1)}, u32[]{:S(2)}, u32[]{:S(2)}) collective-permute-start(f32[64,128]{1,0:T(8,128)S(1)} %add.33), channel_id=1, source_target_pairs={{0,3},{1,2},{2,1},{3,0},{4,7},{5,6},{6,5},{7,4},{8,11},{9,10},{10,... | collective-permute-start | bytes 98312 | tf_op jit(solution)/shard_map/ppermute | solution.py:16
  78.4 4.6 %collective-permute-start.7 = (f32[64,128]{1,0:T(8,128)S(1)}, f32[64,128]{1,0:T(8,128)S(1)}, u32[]{:S(2)}, u32[]{:S(2)}) collective-permute-start(f32[64,128]{1,0:T(8,128)S(1)} %add.34), channel_id=1, source_target_pairs={{0,4},{1,5},{2,6},{3,7},{4,0},{5,1},{6,2},{7,3},{8,12},{9,13},{10,... | collective-permute-start | bytes 98312 | tf_op jit(solution)/shard_map/ppermute | solution.py:16
  83.0 4.2 %collective-permute-start.8 = (f32[64,128]{1,0:T(8,128)S(1)}, f32[64,128]{1,0:T(8,128)S(1)}, u32[]{:S(2)}, u32[]{:S(2)}) collective-permute-start(f32[64,128]{1,0:T(8,128)S(1)} %add.35), channel_id=1, source_target_pairs={{0,12},{1,13},{2,14},{3,15},{4,8},{5,9},{6,10},{7,11},{8,4},{9,5},... | collective-permute-start | bytes 98312 | tf_op jit(solution)/shard_map/ppermute | solution.py:16
  87.2 2.9 %collective-permute-start.9 = (f32[64,128]{1,0:T(8,128)S(1)}, f32[64,128]{1,0:T(8,128)S(1)}, u32[]{:S(2)}, u32[]{:S(2)}) collective-permute-start(f32[64,128]{1,0:T(8,128)S(1)} %add.36), channel_id=1, source_target_pairs={{0,32},{16,48},{32,0},{48,16},{64,96},{80,112},{96,64},{112,80},{1... | collective-permute-start | bytes 98312 | tf_op jit(solution)/shard_map/ppermute | solution.py:16
  90.2 4.0 %collective-permute-start.10 = (f32[64,128]{1,0:T(8,128)S(1)}, f32[64,128]{1,0:T(8,128)S(1)}, u32[]{:S(2)}, u32[]{:S(2)}) collective-permute-start(f32[64,128]{1,0:T(8,128)S(1)} %add.37), channel_id=1, source_target_pairs={{0,96},{16,112},{32,64},{48,80},{64,32},{80,48},{96,0},{112,16},{1... | collective-permute-start | bytes 98312 | tf_op jit(solution)/shard_map/ppermute | solution.py:16
  94.2 7.5 %collective-permute-start.11 = (f32[64,128]{1,0:T(8,128)S(1)}, f32[64,128]{1,0:T(8,128)S(1)}, u32[]{:S(2)}, u32[]{:S(2)}) collective-permute-start(f32[64,128]{1,0:T(8,128)S(1)} %add.38.mine_ref), channel_id=1, source_target_pairs={{0,16},{16,0},{32,48},{48,32},{64,80},{80,64},{96,112},{112,96},{1... | collective-permute-start | bytes 98312 | tf_op jit(solution)/shard_map/ppermute | solution.py:16
  101.6 1.3 copy-start
  120.3 2.7 %collective-permute-start.12 = (f32[2048,128]{1,0:T(8,128)S(1)}, f32[2048,128]{1,0:T(8,128)S(1)}, u32[]{:S(2)}, u32[]{:S(2)}) collective-permute-start(f32[2048,128]{1,0:T(8,128)S(1)} %slice_bitcast_fusion), channel_id=1, source_target_pairs={{0,16},{16,0},{32,48},{48,32},{64,80},{80,64},{96,112},{112,96},{1... | collective-permute-start | bytes 3145736 | tf_op jit(solution)/shard_map/ppermute | solution.py:16
  164.3 4.6 %collective-permute-start.13 = (bf16[2048,128]{1,0:T(8,128)(2,1)S(1)}, bf16[2048,128]{1,0:T(8,128)(2,1)S(1)}, u32[]{:S(2)}, u32[]{:S(2)}) collective-permute-start(bf16[2048,128]{1,0:T(8,128)(2,1)S(1)} %bitcast.26), channel_id=1, source_target_pairs={{0,16},{16,0},{32,48},{48,32},{64,80},{80,64},{96,112},{112,96},{1... | collective-permute-start | bytes 1572872 | tf_op jit(solution)/shard_map/ppermute | solution.py:16
  183.5 2.7 %collective-permute-start.14 = (f32[2048,128]{1,0:T(8,128)S(1)}, f32[2048,128]{1,0:T(8,128)S(1)}, u32[]{:S(2)}, u32[]{:S(2)}) collective-permute-start(f32[2048,128]{1,0:T(8,128)S(1)} %slice_bitcast_fusion.2), channel_id=1, source_target_pairs={{0,16},{16,0},{32,48},{48,32},{64,80},{80,64},{96,112},{112,96},{1... | collective-permute-start | bytes 3145736 | tf_op jit(solution)/shard_map/ppermute | solution.py:16
  229.9 5.4 %collective-permute-start.15 = (f32[2048,128]{1,0:T(8,128)S(1)}, f32[2048,128]{1,0:T(8,128)S(1)}, u32[]{:S(2)}, u32[]{:S(2)}) collective-permute-start(f32[2048,128]{1,0:T(8,128)S(1)} %bitcast.23), channel_id=1, source_target_pairs={{0,16},{16,0},{32,48},{48,32},{64,80},{80,64},{96,112},{112,96},{1... | collective-permute-start | bytes 3145736 | tf_op jit(solution)/shard_map/ppermute | solution.py:16

commit v4 on v3

--- a/solution.py
+++ b/solution.py
@@ -139,9 +139,9 @@
 
 
 def border_body(
-    core_ref, upper_ref, lower_ref, c0_ref, c1_ref, c2_ref, c3_ref, top_ref, bot_ref,
+    upper_ref, lower_ref, c0_ref, c1_ref, c2_ref, c3_ref, top_ref, bot_ref,
     left_ref, right_ref, kern_ref, test_ref, gram_ref, flat_in_ref, sketch_in_ref,
-    edge_ref, sketch_ref, keep_ref, send_ref,
+    edge_ref, sketch_ref, gram_out_ref,
 ):
     step, steps = pl.program_id(0), pl.num_programs(0)
     cols, width = top_ref.shape
@@ -205,83 +205,65 @@
 
     @pl.when(step == steps - 1)
     def _():
-        gram = gram_ref[...] + gram_of(sketch_ref[...])
-        half = keep_ref.shape[0]
-
-        @pl.when(core_ref[0] == 0)
-        def _():
-            keep_ref[...] = gram[:half]
-            send_ref[...] = gram[half:]
-
-        @pl.when(core_ref[0] == 1)
-        def _():
-            keep_ref[...] = gram[half:]
-            send_ref[...] = gram[:half]
-
-
-def border_sketch(core, x, columns, halos, kernel, test_matrix, gram, flat, sketch):
+        gram_out_ref[...] = gram_ref[...] + gram_of(sketch_ref[...])
+
+
+def border_sketch(x, columns, halos, kernel, test_matrix, gram, flat, sketch):
     rows, cols, channels = x.shape
     k = test_matrix.shape[1]
     width = 1024
-    edge = lambda n, at=0: pl.BlockSpec((n, width), lambda j, core: (at, j))
-    fixed = lambda n, at=0: pl.BlockSpec((n, k), lambda j, core: (at, 0))
+    edge = lambda n, at=0: pl.BlockSpec((n, width), lambda j: (at, j))
+    fixed = lambda n, at=0: pl.BlockSpec((n, k), lambda j: (at, 0))
     behind = rows * cols // BORDER
     return pl.pallas_call(
         border_body,
-        grid_spec=pltpu.PrefetchScalarGridSpec(
-            num_scalar_prefetch=1,
-            grid=(channels // width,),
-            in_specs=[
-                pl.BlockSpec((2, cols, width), lambda j, core: (0, 0, j)),
-                pl.BlockSpec((2, cols, width), lambda j, core: (rows // 2 - 1, 0, j)),
-                edge(rows + 8), edge(rows), edge(rows), edge(rows + 8),
-                edge(cols), edge(cols), edge(rows + 8), edge(rows + 8),
-                pl.BlockSpec((3, 3, width), lambda j, core: (0, 0, j)),
-                pl.BlockSpec((width, k), lambda j, core: (j, 0)),
-                fixed(k),
-                pl.BlockSpec(memory_space=pl.ANY),
-                pl.BlockSpec(memory_space=pl.ANY),
-            ],
-            out_specs=[edge(BORDER, behind), fixed(BORDER, behind), fixed(k // 2), fixed(k // 2)],
-        ),
+        grid=(channels // width,),
+        in_specs=[
+            pl.BlockSpec((2, cols, width), lambda j: (0, 0, j)),
+            pl.BlockSpec((2, cols, width), lambda j: (rows // 2 - 1, 0, j)),
+            edge(rows + 8), edge(rows), edge(rows), edge(rows + 8),
+            edge(cols), edge(cols), edge(rows + 8), edge(rows + 8),
+            pl.BlockSpec((3, 3, width), lambda j: (0, 0, j)),
+            pl.BlockSpec((width, k), lambda j: (j, 0)),
+            fixed(k),
+            pl.BlockSpec(memory_space=pl.ANY),
+            pl.BlockSpec(memory_space=pl.ANY),
+        ],
+        out_specs=[edge(BORDER, behind), fixed(BORDER, behind), fixed(k)],
         out_shape=[
             jax.ShapeDtypeStruct(flat.shape, flat.dtype),
             jax.ShapeDtypeStruct(sketch.shape, sketch.dtype),
-            jax.ShapeDtypeStruct((k // 2, k), jnp.float32),
-            jax.ShapeDtypeStruct((k // 2, k), jnp.float32),
-        ],
-        input_output_aliases={14: 0, 15: 1},
+            jax.ShapeDtypeStruct((k, k), jnp.float32),
+        ],
+        input_output_aliases={13: 0, 14: 1},
         compiler_params=params(52, 1),
         name="border_sketch",
-    )(core, x, x, *columns, *halos, kernel, test_matrix, gram, flat, sketch)
-
-
-def columns_body(low_ref, high_ref, top_ref, bot_ref, c0_ref, c1_ref, c2_ref, c3_ref):
+    )(x, x, *columns, *halos, kernel, test_matrix, gram, flat, sketch)
+
+
+def columns_body(low_ref, high_ref, c0_ref, c1_ref, c2_ref, c3_ref):
     rows, _, width = low_ref.shape
-    cols = top_ref.shape[0]
     f32, bf16 = jnp.float32, jnp.bfloat16
     out_id = lax.broadcasted_iota(jnp.int32, (2 * rows, 8 * rows), 0)
     in_id = lax.broadcasted_iota(jnp.int32, (2 * rows, 8 * rows), 1)
-    spare = jnp.zeros((6, width), f32)
+    spare = jnp.zeros((8, width), bf16)
 
     def cut(held_ref, at):
         wanted = (out_id % rows) * 8 + at + out_id // rows
         pick = jnp.where(in_id == wanted, 1.0, 0.0).astype(bf16)
         held = held_ref[...].reshape(8 * rows, width)
-        return jnp.dot(pick, held, preferred_element_type=f32)
-
-    def with_ends(column, place):
-        ends = [r[...].astype(f32)[place : place + 1] for r in (top_ref, bot_ref)]
-        return jnp.concatenate([column] + ends + [spare], axis=0).astype(bf16)
+        return jnp.dot(pick, held, preferred_element_type=f32).astype(bf16)
 
     low, high = cut(low_ref, 0), cut(high_ref, 6)
-    c0_ref[...] = with_ends(low[:rows], 0)
-    c1_ref[...] = low[rows:].astype(bf16)
-    c2_ref[...] = high[:rows].astype(bf16)
-    c3_ref[...] = with_ends(high[rows:], cols - 1)
-
-
-def edge_columns(x, top, bottom):
+    c0_ref[:rows] = low[:rows]
+    c0_ref[rows:] = spare
+    c1_ref[...] = low[rows:]
+    c2_ref[...] = high[:rows]
+    c3_ref[:rows] = high[rows:]
+    c3_ref[rows:] = spare
+
+
+def edge_columns(x):
     rows, cols, channels = x.shape
     width = 1024
     edge = lambda n: pl.BlockSpec((n, width), lambda j: (0, j))
@@ -291,15 +273,18 @@
         in_specs=[
             pl.BlockSpec((rows, 8, width), lambda j: (0, 0, j)),
             pl.BlockSpec((rows, 8, width), lambda j: (0, cols // 8 - 1, j)),
-            edge(cols), edge(cols),
         ],
         out_specs=[edge(rows + 8), edge(rows), edge(rows), edge(rows + 8)],
         out_shape=[
             jax.ShapeDtypeStruct((n, channels), x.dtype) for n in (rows + 8, rows, rows, rows + 8)
         ],
         compiler_params=params(52, 1),
+        cost_estimate=pl.CostEstimate(
+            flops=2 * 4 * rows * 8 * rows * channels, transcendentals=0,
+            bytes_accessed=2 * 20 * rows * channels,
+        ),
         name="edge_columns",
-    )(x, x, top, bottom)
+    )(x, x)
 
 
 def factor_block(panel, low, sub, lane):
@@ -371,13 +356,11 @@
 
 
 def project_body(
-    core_ref, mine_ref, other_ref, sketch_ref, flat_ref, out_ref, work_ref, basis_ref
+    core_ref, gram_ref, sketch_ref, flat_ref, out_ref, work_ref, basis_ref
 ):
     @pl.when(pl.program_id(0) == 0)
     def _():
-        half = mine_ref.shape[0]
-        work_ref[pl.ds(pl.multiple_of(core_ref[0] * half, half), half), :] = mine_ref[...]
-        work_ref[pl.ds(pl.multiple_of((1 - core_ref[0]) * half, half), half), :] = other_ref[...]
+        work_ref[...] = gram_ref[...]
         inverse = inverse_factor(work_ref)
         basis = times_transposed(sketch_ref[...], inverse)
         basis_ref[...] = basis.astype(jnp.bfloat16).T
@@ -386,7 +369,7 @@
     out_ref[0] = product.T
 
 
-def project(core, mine, other, sketch, flat):
+def project(core, gram, sketch, flat):
     pixels, channels = flat.shape
     k = sketch.shape[1]
     width = 512
@@ -398,7 +381,7 @@
             num_scalar_prefetch=1,
             grid=(channels // width,),
             in_specs=[
-                whole(k // 2, k), whole(k // 2, k), whole(pixels, k),
+                whole(k, k), whole(pixels, k),
                 pl.BlockSpec((pixels, width), lambda j, core: (0, j)),
             ],
             out_specs=pl.BlockSpec(
@@ -411,7 +394,7 @@
         out_shape=jax.ShapeDtypeStruct((2, channels // 2, k), jnp.float32),
         compiler_params=params(40, 1),
         name="project",
-    )(core, mine, other, sketch, flat)
+    )(core, gram, sketch, flat)
 
 
 def second_body(core_ref, flat_ref, range_ref, second_ref, out_ref, acc_ref):
@@ -534,20 +517,23 @@
 
     top = shift_permute(radiance[-1], "gy", 1)
     bottom = shift_permute(radiance[0], "gy", -1)
-    columns = edge_columns(radiance, top, bottom)
-    left = shift_permute(columns[3], "gx", 1)
-    right = shift_permute(columns[0], "gx", -1)
+    first, second, before_last, last = edge_columns(radiance)
+    first = lax.dynamic_update_slice(first, jnp.stack([top[0], bottom[0]]), (height, 0))
+    last = lax.dynamic_update_slice(last, jnp.stack([top[-1], bottom[-1]]), (height, 0))
+    columns = (first, second, before_last, last)
+    left = shift_permute(last, "gx", 1)
+    right = shift_permute(first, "gx", -1)
     halos = (top, bottom, left, right)
 
     flat, sketch, gram = smooth_sketch(radiance, kernel, test_matrix)
-    flat, sketch, mine, send = border_sketch(
-        core_arg, radiance, columns, halos, kernel, test_matrix, gram, flat, sketch
-    )
-    mine = mine + xor_permute(send, "gy", 1)
-    for axis, mask in (("gx", 1), ("gx", 3), ("gx", 4), ("gx", 12), ("gy", 2), ("gy", 6)):
-        mine = mine + xor_permute(mine, axis, mask)
-    other = xor_permute(mine, "gy", 1)
-    range_map = all_sum(project(core_arg, mine, other, sketch, flat), core, jnp.bfloat16)
+    flat, sketch, gram = border_sketch(
+        radiance, columns, halos, kernel, test_matrix, gram, flat, sketch
+    )
+    gram = gram + xor_permute(gram, "gy", 1)
+    for axis, masks in (("gx", (1, 2, 3)), ("gx", (4, 8, 12)), ("gy", (2, 4, 6))):
+        one, two, three = [xor_permute(gram, axis, mask) for mask in masks]
+        gram = (gram + one) + (two + three)
+    range_map = all_sum(project(core_arg, gram, sketch, flat), core, jnp.bfloat16)
     second, pair = second_step(core_arg, flat, range_map)
     moment = all_sum(pair, core, jnp.float32)
     scale = math.sqrt(pixel_count)

time: 248 us -> 242 us (0.976)
  waiting for transfers between devices: 25.2 us -> 22 us
    ppermute x4, waiting for transfers between devices: 5.77 us -> 0.12 us  [shift_permute(): return lax.ppermute(value, axis, pairs)]
    ppermute x12 -> x14, waiting for transfers between devices: 19.4 us -> 21.9 us  [xor_permute(): lax.ppermute(value, axis, [(i, i ^ mask) for i in range(lax.axis_size(axi...]
    ppermute x12 -> x14, starting transfers between devices: 28.2 us -> 25.9 us  [xor_permute(): lax.ppermute(value, axis, [(i, i ^ mask) for i in range(lax.axis_size(axi...]
  transfers between devices with their start and end apart: 16 -> 18, of which waited for: 14 -> 13; matrix products, arithmetic and copies ran while one was open for 0% -> 0% of each run, Pallas kernels for 14% -> 17%
where the time goes in v4:
time: 242 us; the launch traced here: 241 us
  Pallas kernels  92.3 us (38%)
  blocking collectives  82.6 us (34%)
  starting transfers between devices  37.3 us (15%)
  waiting for transfers between devices  22 us (9%)
  local copies, waits for them, and re-layouts  4.57 us (2%)
    all_to_all x4, blocking collectives, all_sum(): lax.all_to_all(v, BOTH, 0, 0, axis_index_groups=groups, tiled=True)  82.6 us
    pallas_call x1, Pallas kernels, smooth_sketch(): pl.pallas_call(smooth_body, grid=(channels // width,), in_specs=[pl.Block...  35.7 us
    ppermute x14, starting transfers between devices, xor_permute(): lax.ppermute(value, axis, [(i, i ^ mask) for i in range(lax.axis_size(axi...  25.9 us
    ppermute x14, waiting for transfers between devices, xor_permute(): lax.ppermute(value, axis, [(i, i ^ mask) for i in range(lax.axis_size(axi...  21.9 us
    pallas_call x1, Pallas kernels, project(): pl.pallas_call(project_body, grid_spec=pltpu.PrefetchScalarGridSpec(num_s...  17.3 us
    pallas_call x1, Pallas kernels, second_step(): pl.pallas_call(second_body, grid_spec=pltpu.PrefetchScalarGridSpec(num_sc...  14.4 us
    pallas_call x1, Pallas kernels, finish(): pl.pallas_call(body, out_shape=[jax.ShapeDtypeStruct(tile + (k,), jnp.flo...  11.9 us
    ppermute x4, starting transfers between devices, shift_permute(): return lax.ppermute(value, axis, pairs)  11.4 us
  transfers between devices with their start and end apart: 18, of which 13 were waited for; matrix products, arithmetic and copies ran while one was open for 0% of the time, Pallas kernels for 17%

profile of v4, /device:TPU:1, one launch (start us, length us, event | category | flops | bytes accessed | tf_op | source)
XLA Modules:
  0.0 241.2 jit_solution(1959789210024055627)
XLA Ops:
  0.6 1.1 slice_bitcast_fusion.4
  1.7 4.9 %collective-permute-start = (bf16[32,4096]{1,0:T(8,128)(2,1)S(1)}, bf16[32,4096]{1,0:T(8,128)(2,1)S(1)}, u32[]{:S(2)}, u32[]{:S(2)}) collective-permute-start(bf16[32,4096]{1,0:T(8,128)(2,1)S(1)} %get-tuple-element.26), channel_id=1, source_target_pairs={{0,16},{16,32},{32,48},{48,64},{64,80},{80,96},{96,112},{1,17},{17... | collective-permute-start | bytes 786440 | tf_op jit(solution)/shard_map/ppermute | solution.py:22
  6.6 1.9 collective-permute-start.1
  8.6 5.6 %edge_columns.1 = (bf16[72,4096]{1,0:T(8,128)(2,1)S(1)}, bf16[64,4096]{1,0:T(8,128)(2,1)S(1)}, bf16[64,4096]{1,0:T(8,128)(2,1)S(1)}, bf16[72,4096]{1,0:T(8,128)(2,1)}) custom-call(bf16[64,32,4096]{2,1,0:T(8,128)(2,1)} %lower_ref.1, bf16[64,32,4096]{2,1,0:T(8,128)(2,1)} %lower_ref.1), custom_call_target="tpu_custom_call" | custom-call | flops 1073741824 | bytes 10485760 | tf_op jit(solution)/shard_map/edge_columns/pallas_call | solution.py:270
  14.2 0.0 collective-permute-done.top_ref
  14.2 0.1 collective-permute-done.1.bot_ref
  14.4 0.7 maximum_dynamic-update-slice_fusion.1.c3_ref
  15.0 3.1 %collective-permute-start.2 = (bf16[72,4096]{1,0:T(8,128)(2,1)}, bf16[72,4096]{1,0:T(8,128)(2,1)S(1)}, u32[]{:S(2)}, u32[]{:S(2)}) collective-permute-start(bf16[72,4096]{1,0:T(8,128)(2,1)} %maximum_dynamic-update-slice_fusion.1.c3_ref), channel_id=1, source_target_pairs={{0,1},{1,2},{2,3},{3,4},{4,5},{5,6},{6,7},{7,8},{8,9},{9,10},{10,1... | collective-permute-start | bytes 1769480 | tf_op jit(solution)/shard_map/ppermute | solution.py:22
  18.2 0.1 maximum_dynamic-update-slice_fusion.c0_ref
  18.2 0.0 copy-start.2
  18.2 1.4 collective-permute-start.3
  19.7 35.7 %smooth_sketch.1 = (bf16[2304,4096]{1,0:T(8,128)(2,1)}, f32[2304,128]{1,0:T(8,128)}, f32[128,128]{1,0:T(8,128)}) custom-call(bf16[64,32,4096]{2,1,0:T(8,128)(2,1)} %lower_ref.1, f32[3,3,4096]{2,1,0:T(4,128)} %kern_ref.3, bf16[4096,128]{1,0:T(8,128)(2,1)} %test_ref.3), custom_call_target="tpu_custom_call" | custom-call | flops 17246978048 | bytes 33554432 | tf_op jit(solution)/shard_map/smooth_sketch/pallas_call | solution.py:115
  55.4 0.0 collective-permute-done.3.right_ref
  55.4 0.8 copy-done.4
  56.2 0.2 copy-done.5
  56.4 0.8 copy-done.3
  57.3 7.3 %border_sketch.1 = (bf16[2304,4096]{1,0:T(8,128)(2,1)}, f32[2304,128]{1,0:T(8,128)}, f32[128,128]{1,0:T(8,128)S(1)}) custom-call(bf16[64,32,4096]{2,1,0:T(8,128)(2,1)} %lower_ref.1, bf16[64,32,4096]{2,1,0:T(8,128)(2,1)} %lower_ref.1, bf16[72,4096]{1,0:T(8,128)(2,1)} %copy-done.1, ...), custom_call_target="tpu_custom_call", output_to_operand_aliasing={{0}: (13, {}), {1}: (14, {})} | custom-call | tf_op jit(solution)/shard_map/border_sketch/pallas_call | solution.py:218
  64.6 0.0 collective-permute-start.4
  64.6 1.2 collective-permute-done.4
  65.9 2.2 collective-permute-start.5
  68.0 2.4 collective-permute-start.6
  70.5 0.1 collective-permute-start.7
  70.5 3.4 %collective-permute-done.6 = f32[128,128]{1,0:T(8,128)S(1)} collective-permute-done((f32[128,128]{1,0:T(8,128)S(1)}, f32[128,128]{1,0:T(8,128)S(1)}, u32[]{:S(2)}, u32[]{:S(2)}) %collective-permute-start.6) | collective-permute-done | bytes 65568 | tf_op jit(solution)/shard_map/ppermute | solution.py:16
  73.9 1.0 collective-permute-done.7
  74.9 2.9 %collective-permute-start.10 = (f32[128,128]{1,0:T(8,128)S(1)}, f32[128,128]{1,0:T(8,128)S(1)}, u32[]{:S(2)}, u32[]{:S(2)}) collective-permute-start(f32[128,128]{1,0:T(8,128)S(1)} %add_add_fusion.2), channel_id=1, source_target_pairs={{0,12},{1,13},{2,14},{3,15},{4,8},{5,9},{6,10},{7,11},{8,4},{9,5},... | collective-permute-start | bytes 196616 | tf_op jit(solution)/shard_map/ppermute | solution.py:16
  77.9 1.3 collective-permute-start.9
  79.1 0.4 collective-permute-done.10
  79.5 1.8 collective-permute-done.8
  81.3 1.4 collective-permute-done.9
  82.7 2.0 collective-permute-start.11
  84.7 3.3 %collective-permute-start.12 = (f32[128,128]{1,0:T(8,128)S(1)}, f32[128,128]{1,0:T(8,128)S(1)}, u32[]{:S(2)}, u32[]{:S(2)}) collective-permute-start(f32[128,128]{1,0:T(8,128)S(1)} %add_add_fusion.1), channel_id=1, source_target_pairs={{0,64},{16,80},{32,96},{48,112},{64,0},{80,16},{96,32},{112,48},{1... | collective-permute-start | bytes 196616 | tf_op jit(solution)/shard_map/ppermute | solution.py:16
  88.0 0.0 collective-permute-start.13
  88.0 0.0 collective-permute-done.11
  88.0 2.3 collective-permute-done.12
  90.4 2.0 collective-permute-done.13
  92.4 0.0 copy-start
  92.4 1.3 copy-done
  93.7 17.3 %project.1 = f32[2,2048,128]{2,1,0:T(8,128)S(1)} custom-call(s32[1]{0:T(128)} %bitcast.core_ref, f32[128,128]{1,0:T(8,128)S(1)} %add_add_fusion.gram_ref, f32[2304,128]{1,0:T(8,128)S(1)} %copy-done, bf16[2304,4096]{1,0:T(8,128)(2,1)} %get-tuple-element.23.flat_ref), custom_call_target="tpu_custom_call" | custom-call | tf_op jit(solution)/shard_map/project/pallas_call | solution.py:378
  110.9 0.1 slice_bitcast_fusion
  111.0 5.0 %collective-permute-start.14 = (f32[2048,128]{1,0:T(8,128)S(1)}, f32[2048,128]{1,0:T(8,128)S(1)}, u32[]{:S(2)}, u32[]{:S(2)}) collective-permute-start(f32[2048,128]{1,0:T(8,128)S(1)} %slice_bitcast_fusion), channel_id=1, source_target_pairs={{0,16},{16,0},{32,48},{48,32},{64,80},{80,64},{96,112},{112,96},{1... | collective-permute-start | bytes 3145736 | tf_op jit(solution)/shard_map/ppermute | solution.py:16
  116.0 2.3 collective-permute-done.14
  118.3 0.1 fusion
  118.4 23.8 %all_to_all.20 = f32[64,32,128]{2,1,0:T(8,128)S(1)} all-to-all(f32[64,32,128]{2,1,0:T(8,128)S(1)} %bitcast.24), channel_id=1, replica_groups={{0,1,2,3,4,5,6,7,8,9,10,11,12,13,14,15,32,33,34,35,36,37,38,39,40,41,42..., dimensions={0} | all-to-all | bytes 2097152 | tf_op jit(solution)/shard_map/all_to_all | solution.py:500
  142.2 0.1 reduce_sum.18
  142.3 0.1 broadcast_in_dim.4
  142.4 15.5 %all_to_all.21 = bf16[64,32,128]{2,1,0:T(8,128)(2,1)S(1)} all-to-all(bf16[64,32,128]{2,1,0:T(8,128)(2,1)S(1)} %broadcast_in_dim.4), channel_id=1, replica_groups={{0,1,2,3,4,5,6,7,8,9,10,11,12,13,14,15,32,33,34,35,36,37,38,39,40,41,42..., dimensions={0} | all-to-all | bytes 1048576 | tf_op jit(solution)/shard_map/all_to_all | solution.py:500
  157.9 3.1 %collective-permute-start.15 = (bf16[2048,128]{1,0:T(8,128)(2,1)S(1)}, bf16[2048,128]{1,0:T(8,128)(2,1)S(1)}, u32[]{:S(2)}, u32[]{:S(2)}) collective-permute-start(bf16[2048,128]{1,0:T(8,128)(2,1)S(1)} %bitcast.26), channel_id=1, source_target_pairs={{0,16},{16,0},{32,48},{48,32},{64,80},{80,64},{96,112},{112,96},{1... | collective-permute-start | bytes 1572872 | tf_op jit(solution)/shard_map/ppermute | solution.py:16
  161.0 1.5 collective-permute-done.15
  162.5 0.1 broadcast_select_fusion.3
  162.6 0.1 pad_maximum_fusion.1.range_ref.refs_0_
  162.7 14.4 %second_step.1 = (f32[2304,128]{1,0:T(8,128)S(1)}, f32[2,2048,128]{2,1,0:T(8,128)S(1)}) custom-call(s32[1]{0:T(128)} %bitcast.core_ref, bf16[2304,4096]{1,0:T(8,128)(2,1)} %get-tuple-element.23.flat_ref, bf16[4096,128]{1,0:T(8,128)(2,1)S(1)} %pad_maximum_fusion.1.range_ref.refs_0_), custom_call_target="tpu_custom_call" | custom-call | tf_op jit(solution)/shard_map/second_step/pallas_call | solution.py:430
  177.1 0.1 slice_bitcast_fusion.2
  177.2 0.5 collective-permute-start.16
  177.6 2.3 collective-permute-done.16
  179.9 0.1 bitcast_add_fusion
  180.0 22.3 %all_to_all.22 = f32[64,32,128]{2,1,0:T(8,128)S(1)} all-to-all(f32[64,32,128]{2,1,0:T(8,128)S(1)} %bitcast.25), channel_id=1, replica_groups={{0,1,2,3,4,5,6,7,8,9,10,11,12,13,14,15,32,33,34,35,36,37,38,39,40,41,42..., dimensions={0} | all-to-all | bytes 2097152 | tf_op jit(solution)/shard_map/all_to_all | solution.py:500
  202.4 0.1 reduce_sum.19
  202.5 0.1 broadcast_in_dim.5
  202.6 21.0 %all_to_all.23 = f32[64,32,128]{2,1,0:T(8,128)S(1)} all-to-all(f32[64,32,128]{2,1,0:T(8,128)S(1)} %broadcast_in_dim.5), channel_id=1, replica_groups={{0,1,2,3,4,5,6,7,8,9,10,11,12,13,14,15,32,33,34,35,36,37,38,39,40,41,42..., dimensions={0} | all-to-all | bytes 2097152 | tf_op jit(solution)/shard_map/all_to_all | solution.py:500
  223.6 3.2 %collective-permute-start.17 = (f32[2048,128]{1,0:T(8,128)S(1)}, f32[2048,128]{1,0:T(8,128)S(1)}, u32[]{:S(2)}, u32[]{:S(2)}) collective-permute-start(f32[2048,128]{1,0:T(8,128)S(1)} %bitcast.23), channel_id=1, source_target_pairs={{0,16},{16,0},{32,48},{48,32},{64,80},{80,64},{96,112},{112,96},{1... | collective-permute-start | bytes 3145736 | tf_op jit(solution)/shard_map/ppermute | solution.py:16
  226.7 2.3 collective-permute-done.17
  229.0 0.1 broadcast_select_fusion.1
  229.2 0.1 pad_maximum_fusion.refs_1_
  229.3 11.9 %finish.1 = (f32[64,32,128]{2,1,0:T(8,128)}, f32[128,4096]{1,0:T(8,128)}) custom-call(bf16[4096,128]{1,0:T(8,128)(2,1)S(1)} %pad_maximum_fusion.1.range_ref.refs_0_, f32[4096,128]{1,0:T(8,128)S(1)} %pad_maximum_fusion.refs_1_, f32[2304,128]{1,0:T(8,128)S(1)} %get-tuple-element.25.refs_2_), custom_call_target="tpu_custom_call" | custom-call | tf_op jit(solution)/shard_map/finish/pallas_call | solution.py:483
  (15 shorter events, 0.1 us)
Async XLA Ops:
  1.7 12.5 %collective-permute-start = (bf16[32,4096]{1,0:T(8,128)(2,1)S(1)}, bf16[32,4096]{1,0:T(8,128)(2,1)S(1)}, u32[]{:S(2)}, u32[]{:S(2)}) collective-permute-start(bf16[32,4096]{1,0:T(8,128)(2,1)S(1)} %get-tuple-element.26), channel_id=1, source_target_pairs={{0,16},{16,32},{32,48},{48,64},{64,80},{80,96},{96,112},{1,17},{17... | collective-permute-start | bytes 786440 | tf_op jit(solution)/shard_map/ppermute | solution.py:22
  6.6 7.7 %collective-permute-start.1 = (bf16[32,4096]{1,0:T(8,128)(2,1)S(1)}, bf16[32,4096]{1,0:T(8,128)(2,1)S(1)}, u32[]{:S(2)}, u32[]{:S(2)}) collective-permute-start(bf16[32,4096]{1,0:T(8,128)(2,1)S(1)} %get-tuple-element.27), channel_id=1, source_target_pairs={{16,0},{32,16},{48,32},{64,48},{80,64},{96,80},{112,96},{17,1},{33... | collective-permute-start | bytes 786440 | tf_op jit(solution)/shard_map/ppermute | solution.py:22
  15.0 40.4 %collective-permute-start.2 = (bf16[72,4096]{1,0:T(8,128)(2,1)}, bf16[72,4096]{1,0:T(8,128)(2,1)S(1)}, u32[]{:S(2)}, u32[]{:S(2)}) collective-permute-start(bf16[72,4096]{1,0:T(8,128)(2,1)} %maximum_dynamic-update-slice_fusion.1.c3_ref), channel_id=1, source_target_pairs={{0,1},{1,2},{2,3},{3,4},{4,5},{5,6},{6,7},{7,8},{8,9},{9,10},{10,1... | collective-permute-start | bytes 1769480 | tf_op jit(solution)/shard_map/ppermute | solution.py:22
  18.2 37.2 %copy-start.1 = (bf16[72,4096]{1,0:T(8,128)(2,1)}, bf16[72,4096]{1,0:T(8,128)(2,1)S(1)}, u32[]{:S(2)}) copy-start(bf16[72,4096]{1,0:T(8,128)(2,1)S(1)} %maximum_dynamic-update-slice_fusion.c0_ref) | copy-start | bytes 1769476
  18.2 38.2 %copy-start.2 = (f32[3,3,4096]{2,1,0:T(4,128)S(1)}, f32[3,3,4096]{2,1,0:T(4,128)}, u32[]{:S(2)}) copy-start(f32[3,3,4096]{2,1,0:T(4,128)} %kern_ref.3) | copy-start | bytes 442372
  18.2 37.2 %collective-permute-start.3 = (bf16[72,4096]{1,0:T(8,128)(2,1)S(1)}, bf16[72,4096]{1,0:T(8,128)(2,1)S(1)}, u32[]{:S(2)}, u32[]{:S(2)}) collective-permute-start(bf16[72,4096]{1,0:T(8,128)(2,1)S(1)} %maximum_dynamic-update-slice_fusion.c0_ref), channel_id=1, source_target_pairs={{1,0},{2,1},{3,2},{4,3},{5,4},{6,5},{7,6},{8,7},{9,8},{10,9},{11,1... | collective-permute-start | bytes 1769480 | tf_op jit(solution)/shard_map/ppermute | solution.py:22
  55.4 0.8 copy-start.4
  55.4 1.0 copy-start.5
  56.4 0.8 copy-start.3
  64.6 1.3 collective-permute-start.4
  65.9 4.7 %collective-permute-start.5 = (f32[128,128]{1,0:T(8,128)S(1)}, f32[128,128]{1,0:T(8,128)S(1)}, u32[]{:S(2)}, u32[]{:S(2)}) collective-permute-start(f32[128,128]{1,0:T(8,128)S(1)} %add.41), channel_id=1, source_target_pairs={{0,1},{1,0},{2,3},{3,2},{4,5},{5,4},{6,7},{7,6},{8,9},{9,8},{10,11... | collective-permute-start | bytes 196616 | tf_op jit(solution)/shard_map/ppermute | solution.py:16
  68.0 5.8 %collective-permute-start.6 = (f32[128,128]{1,0:T(8,128)S(1)}, f32[128,128]{1,0:T(8,128)S(1)}, u32[]{:S(2)}, u32[]{:S(2)}) collective-permute-start(f32[128,128]{1,0:T(8,128)S(1)} %add.41), channel_id=1, source_target_pairs={{0,2},{1,3},{2,0},{3,1},{4,6},{5,7},{6,4},{7,5},{8,10},{9,11},{10,... | collective-permute-start | bytes 196616 | tf_op jit(solution)/shard_map/ppermute | solution.py:16
  70.5 4.5 %collective-permute-start.7 = (f32[128,128]{1,0:T(8,128)S(1)}, f32[128,128]{1,0:T(8,128)S(1)}, u32[]{:S(2)}, u32[]{:S(2)}) collective-permute-start(f32[128,128]{1,0:T(8,128)S(1)} %add.41), channel_id=1, source_target_pairs={{0,3},{1,2},{2,1},{3,0},{4,7},{5,6},{6,5},{7,4},{8,11},{9,10},{10,... | collective-permute-start | bytes 196616 | tf_op jit(solution)/shard_map/ppermute | solution.py:16
  74.9 4.6 %collective-permute-start.10 = (f32[128,128]{1,0:T(8,128)S(1)}, f32[128,128]{1,0:T(8,128)S(1)}, u32[]{:S(2)}, u32[]{:S(2)}) collective-permute-start(f32[128,128]{1,0:T(8,128)S(1)} %add_add_fusion.2), channel_id=1, source_target_pairs={{0,12},{1,13},{2,14},{3,15},{4,8},{5,9},{6,10},{7,11},{8,4},{9,5},... | collective-permute-start | bytes 196616 | tf_op jit(solution)/shard_map/ppermute | solution.py:16
  77.9 3.4 %collective-permute-start.8 = (f32[128,128]{1,0:T(8,128)S(1)}, f32[128,128]{1,0:T(8,128)S(1)}, u32[]{:S(2)}, u32[]{:S(2)}) collective-permute-start(f32[128,128]{1,0:T(8,128)S(1)} %add_add_fusion.2), channel_id=1, source_target_pairs={{0,4},{1,5},{2,6},{3,7},{4,0},{5,1},{6,2},{7,3},{8,12},{9,13},{10,... | collective-permute-start | bytes 196616 | tf_op jit(solution)/shard_map/ppermute | solution.py:16
  77.9 4.8 %collective-permute-start.9 = (f32[128,128]{1,0:T(8,128)S(1)}, f32[128,128]{1,0:T(8,128)S(1)}, u32[]{:S(2)}, u32[]{:S(2)}) collective-permute-start(f32[128,128]{1,0:T(8,128)S(1)} %add_add_fusion.2), channel_id=1, source_target_pairs={{0,8},{1,9},{2,10},{3,11},{4,12},{5,13},{6,14},{7,15},{8,0},{9,1},... | collective-permute-start | bytes 196616 | tf_op jit(solution)/shard_map/ppermute | solution.py:16
  82.7 5.4 %collective-permute-start.11 = (f32[128,128]{1,0:T(8,128)S(1)}, f32[128,128]{1,0:T(8,128)S(1)}, u32[]{:S(2)}, u32[]{:S(2)}) collective-permute-start(f32[128,128]{1,0:T(8,128)S(1)} %add_add_fusion.1), channel_id=1, source_target_pairs={{0,32},{16,48},{32,0},{48,16},{64,96},{80,112},{96,64},{112,80},{1... | collective-permute-start | bytes 196616 | tf_op jit(solution)/shard_map/ppermute | solution.py:16
  84.7 5.7 %collective-permute-start.12 = (f32[128,128]{1,0:T(8,128)S(1)}, f32[128,128]{1,0:T(8,128)S(1)}, u32[]{:S(2)}, u32[]{:S(2)}) collective-permute-start(f32[128,128]{1,0:T(8,128)S(1)} %add_add_fusion.1), channel_id=1, source_target_pairs={{0,64},{16,80},{32,96},{48,112},{64,0},{80,16},{96,32},{112,48},{1... | collective-permute-start | bytes 196616 | tf_op jit(solution)/shard_map/ppermute | solution.py:16
  88.0 4.3 %collective-permute-start.13 = (f32[128,128]{1,0:T(8,128)S(1)}, f32[128,128]{1,0:T(8,128)S(1)}, u32[]{:S(2)}, u32[]{:S(2)}) collective-permute-start(f32[128,128]{1,0:T(8,128)S(1)} %add_add_fusion.1), channel_id=1, source_target_pairs={{0,96},{16,112},{32,64},{48,80},{64,32},{80,48},{96,0},{112,16},{1... | collective-permute-start | bytes 196616 | tf_op jit(solution)/shard_map/ppermute | solution.py:16
  92.4 1.3 copy-start
  111.0 7.3 %collective-permute-start.14 = (f32[2048,128]{1,0:T(8,128)S(1)}, f32[2048,128]{1,0:T(8,128)S(1)}, u32[]{:S(2)}, u32[]{:S(2)}) collective-permute-start(f32[2048,128]{1,0:T(8,128)S(1)} %slice_bitcast_fusion), channel_id=1, source_target_pairs={{0,16},{16,0},{32,48},{48,32},{64,80},{80,64},{96,112},{112,96},{1... | collective-permute-start | bytes 3145736 | tf_op jit(solution)/shard_map/ppermute | solution.py:16
  157.9 4.6 %collective-permute-start.15 = (bf16[2048,128]{1,0:T(8,128)(2,1)S(1)}, bf16[2048,128]{1,0:T(8,128)(2,1)S(1)}, u32[]{:S(2)}, u32[]{:S(2)}) collective-permute-start(bf16[2048,128]{1,0:T(8,128)(2,1)S(1)} %bitcast.26), channel_id=1, source_target_pairs={{0,16},{16,0},{32,48},{48,32},{64,80},{80,64},{96,112},{112,96},{1... | collective-permute-start | bytes 1572872 | tf_op jit(solution)/shard_map/ppermute | solution.py:16
  177.2 2.7 %collective-permute-start.16 = (f32[2048,128]{1,0:T(8,128)S(1)}, f32[2048,128]{1,0:T(8,128)S(1)}, u32[]{:S(2)}, u32[]{:S(2)}) collective-permute-start(f32[2048,128]{1,0:T(8,128)S(1)} %slice_bitcast_fusion.2), channel_id=1, source_target_pairs={{0,16},{16,0},{32,48},{48,32},{64,80},{80,64},{96,112},{112,96},{1... | collective-permute-start | bytes 3145736 | tf_op jit(solution)/shard_map/ppermute | solution.py:16
  223.6 5.5 %collective-permute-start.17 = (f32[2048,128]{1,0:T(8,128)S(1)}, f32[2048,128]{1,0:T(8,128)S(1)}, u32[]{:S(2)}, u32[]{:S(2)}) collective-permute-start(f32[2048,128]{1,0:T(8,128)S(1)} %bitcast.23), channel_id=1, source_target_pairs={{0,16},{16,0},{32,48},{48,32},{64,80},{80,64},{96,112},{112,96},{1... | collective-permute-start | bytes 3145736 | tf_op jit(solution)/shard_map/ppermute | solution.py:16

commit v5 on v4

--- a/solution.py
+++ b/solution.py
@@ -44,7 +44,7 @@
         span = pl.ds(pl.multiple_of(g * group * cols, group * cols), group * cols)
         return span, jnp.dot(flat_ref[span, :], test_ref[...], preferred_element_type=f32)
 
-    def smooth_rows(g):
+    def smooth_rows(g, first=0, last=0):
         base = pl.multiple_of(g * group, group)
         for chunk in range(width // 128):
             lanes = slice(chunk * 128, chunk * 128 + 128)
@@ -55,18 +55,13 @@
             ]
 
             def fetch(q):
-                place = base + q - 1
-                if q == 0:
-                    place = jnp.maximum(place, 0)
-                elif q == group + 1:
-                    place = jnp.minimum(place, rows - 1)
-                row = x_ref[place, :, lanes].astype(f32)
+                row = x_ref[base + q - 1, :, lanes].astype(f32)
                 at = q * (cols + 16) + 8
                 pad[at : at + cols, :] = row
                 return [pad[at - 1 : at - 1 + cols, :], row, pad[at + 1 : at + 1 + cols, :]]
 
-            near = [fetch(0), fetch(1)]
-            for r in range(group):
+            near = [fetch(q) for q in (first, first + 1)]
+            for r in range(first, group - last):
                 near = near[-2:] + [fetch(r + 2)]
                 total = None
                 for a in range(3):
@@ -76,10 +71,6 @@
                 head = jnp.where(sub == 0, 0.0, total[:8])
                 tail = jnp.where(sub == 7, 0.0, total[cols - 8 :])
                 total = jnp.concatenate([head, total[8 : cols - 8], tail], axis=0)
-                if r == 0:
-                    total = jnp.where(g == 0, 0.0, total)
-                if r == group - 1:
-                    total = jnp.where(g == groups - 1, 0.0, total)
                 start = pl.multiple_of((base + r) * cols, cols)
                 flat_ref[pl.ds(start, cols), lanes] = total.astype(jnp.bfloat16)
 
@@ -89,8 +80,13 @@
         sketch_ref[span, :] += part
         return carry
 
-    smooth_rows(0)
-    lax.fori_loop(1, groups, body, 0)
+    flat_ref[:cols, :] = jnp.zeros((cols, width), jnp.bfloat16)
+    flat_ref[(rows - 1) * cols :, :] = jnp.zeros((cols, width), jnp.bfloat16)
+    smooth_rows(0, first=1)
+    lax.fori_loop(1, groups - 1, body, 0)
+    span, part = project_rows(groups - 2)
+    smooth_rows(groups - 1, last=1)
+    sketch_ref[span, :] += part
     span, part = project_rows(groups - 1)
     sketch_ref[span, :] += part
 
@@ -265,7 +261,7 @@
 
 def edge_columns(x):
     rows, cols, channels = x.shape
-    width = 1024
+    width = 2048
     edge = lambda n: pl.BlockSpec((n, width), lambda j: (0, j))
     return pl.pallas_call(
         columns_body,
@@ -355,9 +351,7 @@
     )
 
 
-def project_body(
-    core_ref, gram_ref, sketch_ref, flat_ref, out_ref, work_ref, basis_ref
-):
+def project_other_body(core_ref, gram_ref, sketch_ref, flat_ref, out_ref, basis_ref, work_ref):
     @pl.when(pl.program_id(0) == 0)
     def _():
         work_ref[...] = gram_ref[...]
@@ -366,35 +360,64 @@
         basis_ref[...] = basis.astype(jnp.bfloat16).T
 
     product = jnp.dot(basis_ref[...], flat_ref[...], preferred_element_type=jnp.float32)
-    out_ref[0] = product.T
-
-
-def project(core, gram, sketch, flat):
+    out_ref[...] = product.T
+
+
+def project_own_body(core_ref, basis_ref, flat_ref, out_ref):
+    product = jnp.dot(basis_ref[...], flat_ref[...], preferred_element_type=jnp.float32)
+    out_ref[...] = product.T
+
+
+def project_other(core, gram, sketch, flat):
     pixels, channels = flat.shape
     k = sketch.shape[1]
     width = 512
     half = channels // width // 2
     whole = lambda *shape: pl.BlockSpec(shape, lambda j, core: (0,) * len(shape))
     return pl.pallas_call(
-        project_body,
+        project_other_body,
         grid_spec=pltpu.PrefetchScalarGridSpec(
             num_scalar_prefetch=1,
-            grid=(channels // width,),
+            grid=(half,),
             in_specs=[
                 whole(k, k), whole(pixels, k),
-                pl.BlockSpec((pixels, width), lambda j, core: (0, j)),
+                pl.BlockSpec((pixels, width), lambda j, core: (0, (1 - core[0]) * half + j)),
             ],
-            out_specs=pl.BlockSpec(
-                (1, width, k), lambda j, core: ((j // half) ^ core[0], j % half, 0)
-            ),
-            scratch_shapes=[
-                pltpu.VMEM((k, k), jnp.float32), pltpu.VMEM((k, pixels), jnp.bfloat16),
+            out_specs=[pl.BlockSpec((width, k), lambda j, core: (j, 0)), whole(k, pixels)],
+            scratch_shapes=[pltpu.VMEM((k, k), jnp.float32)],
+        ),
+        out_shape=[
+            jax.ShapeDtypeStruct((channels // 2, k), jnp.float32),
+            jax.ShapeDtypeStruct((k, pixels), jnp.bfloat16),
+        ],
+        compiler_params=params(40, 1),
+        name="project_other",
+    )(core, gram, sketch, flat)
+
+
+def project_own(core, basis, flat):
+    pixels, channels = flat.shape
+    k = basis.shape[0]
+    width = 512
+    half = channels // width // 2
+    return pl.pallas_call(
+        project_own_body,
+        grid_spec=pltpu.PrefetchScalarGridSpec(
+            num_scalar_prefetch=1,
+            grid=(half,),
+            in_specs=[
+                pl.BlockSpec((k, pixels), lambda j, core: (0, 0)),
+                pl.BlockSpec((pixels, width), lambda j, core: (0, core[0] * half + j)),
             ],
+            out_specs=pl.BlockSpec((width, k), lambda j, core: (j, 0)),
         ),
-        out_shape=jax.ShapeDtypeStruct((2, channels // 2, k), jnp.float32),
+        out_shape=jax.ShapeDtypeStruct((channels // 2, k), jnp.float32),
         compiler_params=params(40, 1),
-        name="project",
-    )(core, gram, sketch, flat)
+        cost_estimate=pl.CostEstimate(
+            flops=4 * pixels * channels * k, transcendentals=0, bytes_accessed=pixels * channels
+        ),
+        name="project_own",
+    )(core, basis, flat)
 
 
 def second_body(core_ref, flat_ref, range_ref, second_ref, out_ref, acc_ref):
@@ -492,13 +515,13 @@
     )(range_map, moment, second)
 
 
-def all_sum(pair, core, dtype):
+def all_sum(own, received, core, dtype):
     gy, gx = lax.axis_size("gy"), lax.axis_size("gx")
     groups = [[y * gx + x for y in range(c, gy, 2) for x in range(gx)] for c in range(2)]
-    half, k = pair.shape[1:]
+    half, k = own.shape
     members = gy * gx // 2
     swap = lambda v: lax.all_to_all(v, BOTH, 0, 0, axis_index_groups=groups, tiled=True)
-    mine = pair[0] + xor_permute(pair[1], "gy", 1)
+    mine = own + received
     parts = swap(mine.reshape(members, half // members, k))
     chunk = jnp.sum(parts, axis=0).astype(dtype)
     chunk = lax.optimization_barrier(chunk)
@@ -533,9 +556,11 @@
     for axis, masks in (("gx", (1, 2, 3)), ("gx", (4, 8, 12)), ("gy", (2, 4, 6))):
         one, two, three = [xor_permute(gram, axis, mask) for mask in masks]
         gram = (gram + one) + (two + three)
-    range_map = all_sum(project(core_arg, gram, sketch, flat), core, jnp.bfloat16)
+    part, basis = project_other(core_arg, gram, sketch, flat)
+    received = xor_permute(part, "gy", 1)
+    range_map = all_sum(project_own(core_arg, basis, flat), received, core, jnp.bfloat16)
     second, pair = second_step(core_arg, flat, range_map)
-    moment = all_sum(pair, core, jnp.float32)
+    moment = all_sum(pair[0], xor_permute(pair[1], "gy", 1), core, jnp.float32)
     scale = math.sqrt(pixel_count)
     return finish(
         range_map, moment, second, (height, breadth),

time: 242 us -> 239 us (0.988)
    pallas_call x1 -> x2, Pallas kernels: 17.3 us -> 17.8 us  [the longest x1 12.4 us: project_other(): pl.pallas_call(project_other_body, grid_spec=pltpu.PrefetchScalarGridSpec...]
  transfers between devices with their start and end apart: 18 -> 18, of which waited for: 13 -> 12; matrix products, arithmetic and copies ran while one was open for 0% -> 0% of each run, Pallas kernels for 17% -> 19%
where the time goes in v5:
time: 239 us
  Pallas kernels  91.4 us (38%)
  blocking collectives  83.9 us (35%)
  starting transfers between devices  36 us (15%)
  waiting for transfers between devices  20.4 us (9%)
  local copies, waits for them, and re-layouts  4.5 us (2%)
    all_to_all x4, blocking collectives, all_sum(): lax.all_to_all(v, BOTH, 0, 0, axis_index_groups=groups, tiled=True)  83.9 us
    pallas_call x1, Pallas kernels, smooth_sketch(): pl.pallas_call(smooth_body, grid=(channels // width,), in_specs=[pl.Block...  34.9 us
    ppermute x14, starting transfers between devices, xor_permute(): lax.ppermute(value, axis, [(i, i ^ mask) for i in range(lax.axis_size(axi...  24.6 us
    ppermute x14, waiting for transfers between devices, xor_permute(): lax.ppermute(value, axis, [(i, i ^ mask) for i in range(lax.axis_size(axi...  19.6 us
    pallas_call x1, Pallas kernels, second_step(): pl.pallas_call(second_body, grid_spec=pltpu.PrefetchScalarGridSpec(num_sc...  14.4 us
    pallas_call x1, Pallas kernels, project_other(): pl.pallas_call(project_other_body, grid_spec=pltpu.PrefetchScalarGridSpec...  12.4 us
    pallas_call x1, Pallas kernels, finish(): pl.pallas_call(body, out_shape=[jax.ShapeDtypeStruct(tile + (k,), jnp.flo...  11.9 us
    ppermute x4, starting transfers between devices, shift_permute(): return lax.ppermute(value, axis, pairs)  11.4 us
  transfers between devices with their start and end apart: 18, of which 12 were waited for; matrix products, arithmetic and copies ran while one was open for 0% of the time, Pallas kernels for 19%

profile of v5, /device:TPU:1, one launch (start us, length us, event | category | flops | bytes accessed | tf_op | source)
XLA Modules:
  0.0 238.6 jit_solution(13264330224764458470)
XLA Ops:
  0.6 1.1 slice_bitcast_fusion.2
  1.7 4.9 %collective-permute-start = (bf16[32,4096]{1,0:T(8,128)(2,1)S(1)}, bf16[32,4096]{1,0:T(8,128)(2,1)S(1)}, u32[]{:S(2)}, u32[]{:S(2)}) collective-permute-start(bf16[32,4096]{1,0:T(8,128)(2,1)S(1)} %get-tuple-element.30), channel_id=1, source_target_pairs={{0,16},{16,32},{32,48},{48,64},{64,80},{80,96},{96,112},{1,17},{17... | collective-permute-start | bytes 786440 | tf_op jit(solution)/shard_map/ppermute | solution.py:22
  6.6 1.9 collective-permute-start.1
  8.6 5.0 %edge_columns.1 = (bf16[72,4096]{1,0:T(8,128)(2,1)S(1)}, bf16[64,4096]{1,0:T(8,128)(2,1)S(1)}, bf16[64,4096]{1,0:T(8,128)(2,1)S(1)}, bf16[72,4096]{1,0:T(8,128)(2,1)}) custom-call(bf16[64,32,4096]{2,1,0:T(8,128)(2,1)} %lower_ref.1, bf16[64,32,4096]{2,1,0:T(8,128)(2,1)} %lower_ref.1), custom_call_target="tpu_custom_call" | custom-call | flops 1073741824 | bytes 10485760 | tf_op jit(solution)/shard_map/edge_columns/pallas_call | solution.py:266
  13.5 0.0 collective-permute-done.top_ref
  13.6 0.7 collective-permute-done.1.bot_ref
  14.4 0.7 maximum_dynamic-update-slice_fusion.1.c3_ref
  15.0 3.1 %collective-permute-start.2 = (bf16[72,4096]{1,0:T(8,128)(2,1)}, bf16[72,4096]{1,0:T(8,128)(2,1)S(1)}, u32[]{:S(2)}, u32[]{:S(2)}) collective-permute-start(bf16[72,4096]{1,0:T(8,128)(2,1)} %maximum_dynamic-update-slice_fusion.1.c3_ref), channel_id=1, source_target_pairs={{0,1},{1,2},{2,3},{3,4},{4,5},{5,6},{6,7},{7,8},{8,9},{9,10},{10,1... | collective-permute-start | bytes 1769480 | tf_op jit(solution)/shard_map/ppermute | solution.py:22
  18.2 0.1 maximum_dynamic-update-slice_fusion.c0_ref
  18.2 0.0 copy-start.2
  18.2 1.4 collective-permute-start.3
  19.7 34.9 %smooth_sketch.1 = (bf16[2304,4096]{1,0:T(8,128)(2,1)}, f32[2304,128]{1,0:T(8,128)}, f32[128,128]{1,0:T(8,128)}) custom-call(bf16[64,32,4096]{2,1,0:T(8,128)(2,1)} %lower_ref.1, f32[3,3,4096]{2,1,0:T(4,128)} %kern_ref.3, bf16[4096,128]{1,0:T(8,128)(2,1)} %test_ref.3), custom_call_target="tpu_custom_call" | custom-call | flops 17246978048 | bytes 33554432 | tf_op jit(solution)/shard_map/smooth_sketch/pallas_call | solution.py:111
  54.6 0.0 collective-permute-done.2.left_ref
  54.6 0.8 copy-done.4
  55.4 0.2 copy-done.5
  55.6 0.8 copy-done.3
  56.4 7.3 %border_sketch.1 = (bf16[2304,4096]{1,0:T(8,128)(2,1)}, f32[2304,128]{1,0:T(8,128)}, f32[128,128]{1,0:T(8,128)S(1)}) custom-call(bf16[64,32,4096]{2,1,0:T(8,128)(2,1)} %lower_ref.1, bf16[64,32,4096]{2,1,0:T(8,128)(2,1)} %lower_ref.1, bf16[72,4096]{1,0:T(8,128)(2,1)} %copy-done.1, ...), custom_call_target="tpu_custom_call", output_to_operand_aliasing={{0}: (13, {}), {1}: (14, {})} | custom-call | tf_op jit(solution)/shard_map/border_sketch/pallas_call | solution.py:214
  63.8 0.0 collective-permute-start.4
  63.8 1.2 collective-permute-done.4
  65.0 2.2 collective-permute-start.5
  67.2 2.4 %collective-permute-start.6 = (f32[128,128]{1,0:T(8,128)S(1)}, f32[128,128]{1,0:T(8,128)S(1)}, u32[]{:S(2)}, u32[]{:S(2)}) collective-permute-start(f32[128,128]{1,0:T(8,128)S(1)} %add.41), channel_id=1, source_target_pairs={{0,2},{1,3},{2,0},{3,1},{4,6},{5,7},{6,4},{7,5},{8,10},{9,11},{10,... | collective-permute-start | bytes 196616 | tf_op jit(solution)/shard_map/ppermute | solution.py:16
  69.6 0.1 collective-permute-start.7
  69.7 0.0 collective-permute-done.5
  69.7 3.4 %collective-permute-done.6 = f32[128,128]{1,0:T(8,128)S(1)} collective-permute-done((f32[128,128]{1,0:T(8,128)S(1)}, f32[128,128]{1,0:T(8,128)S(1)}, u32[]{:S(2)}, u32[]{:S(2)}) %collective-permute-start.6) | collective-permute-done | bytes 65568 | tf_op jit(solution)/shard_map/ppermute | solution.py:16
  73.0 1.0 collective-permute-done.7
  74.1 2.9 %collective-permute-start.10 = (f32[128,128]{1,0:T(8,128)S(1)}, f32[128,128]{1,0:T(8,128)S(1)}, u32[]{:S(2)}, u32[]{:S(2)}) collective-permute-start(f32[128,128]{1,0:T(8,128)S(1)} %add_add_fusion.2), channel_id=1, source_target_pairs={{0,12},{1,13},{2,14},{3,15},{4,8},{5,9},{6,10},{7,11},{8,4},{9,5},... | collective-permute-start | bytes 196616 | tf_op jit(solution)/shard_map/ppermute | solution.py:16
  77.0 0.0 collective-permute-start.8
  77.0 1.3 collective-permute-start.9
  78.3 0.4 collective-permute-done.10
  78.7 1.8 collective-permute-done.8
  80.4 1.4 collective-permute-done.9
  81.9 1.7 collective-permute-start.11
  83.5 3.0 %collective-permute-start.12 = (f32[128,128]{1,0:T(8,128)S(1)}, f32[128,128]{1,0:T(8,128)S(1)}, u32[]{:S(2)}, u32[]{:S(2)}) collective-permute-start(f32[128,128]{1,0:T(8,128)S(1)} %add_add_fusion.1), channel_id=1, source_target_pairs={{0,64},{16,80},{32,96},{48,112},{64,0},{80,16},{96,32},{112,48},{1... | collective-permute-start | bytes 196616 | tf_op jit(solution)/shard_map/ppermute | solution.py:16
  86.6 0.0 collective-permute-start.13
  86.6 2.3 collective-permute-done.12
  88.9 2.0 collective-permute-done.13
  90.9 0.0 copy-start
  90.9 1.3 copy-done
  92.2 12.4 %project_other.1 = (f32[2048,128]{1,0:T(8,128)S(1)}, bf16[128,2304]{1,0:T(8,128)(2,1)S(1)}) custom-call(s32[1]{0:T(128)} %bitcast.core_ref, f32[128,128]{1,0:T(8,128)S(1)} %add_add_fusion.gram_ref, f32[2304,128]{1,0:T(8,128)S(1)} %copy-done, bf16[2304,4096]{1,0:T(8,128)(2,1)} %get-tuple-element.25.flat_ref), custom_call_target="tpu_custom_call" | custom-call | tf_op jit(solution)/shard_map/project_other/pallas_call | solution.py:377
  104.7 5.0 %collective-permute-start.14 = (f32[2048,128]{1,0:T(8,128)S(1)}, f32[2048,128]{1,0:T(8,128)S(1)}, u32[]{:S(2)}, u32[]{:S(2)}) collective-permute-start(f32[2048,128]{1,0:T(8,128)S(1)} %get-tuple-element.27), channel_id=1, source_target_pairs={{0,16},{16,0},{32,48},{48,32},{64,80},{80,64},{96,112},{112,96},{1... | collective-permute-start | bytes 3145736 | tf_op jit(solution)/shard_map/ppermute | solution.py:16
  109.6 5.4 %project_own.1 = f32[2048,128]{1,0:T(8,128)S(1)} custom-call(s32[1]{0:T(128)} %bitcast.core_ref, bf16[128,2304]{1,0:T(8,128)(2,1)S(1)} %get-tuple-element.26.basis_ref, bf16[2304,4096]{1,0:T(8,128)(2,1)} %get-tuple-element.25.flat_ref), custom_call_target="tpu_custom_call" | custom-call | flops 4831838208 | bytes 9437184 | tf_op jit(solution)/shard_map/project_own/pallas_call | solution.py:403
  115.0 0.1 add.51
  115.1 24.0 %all_to_all.20 = f32[64,32,128]{2,1,0:T(8,128)S(1)} all-to-all(f32[64,32,128]{2,1,0:T(8,128)S(1)} %bitcast.18), channel_id=1, replica_groups={{0,1,2,3,4,5,6,7,8,9,10,11,12,13,14,15,32,33,34,35,36,37,38,39,40,41,42..., dimensions={0} | all-to-all | bytes 2097152 | tf_op jit(solution)/shard_map/all_to_all | solution.py:523
  139.1 0.1 reduce_sum.18
  139.2 0.1 broadcast_in_dim.4
  139.3 16.6 %all_to_all.21 = bf16[64,32,128]{2,1,0:T(8,128)(2,1)S(1)} all-to-all(bf16[64,32,128]{2,1,0:T(8,128)(2,1)S(1)} %broadcast_in_dim.4), channel_id=1, replica_groups={{0,1,2,3,4,5,6,7,8,9,10,11,12,13,14,15,32,33,34,35,36,37,38,39,40,41,42..., dimensions={0} | all-to-all | bytes 1048576 | tf_op jit(solution)/shard_map/all_to_all | solution.py:523
  155.9 2.5 %collective-permute-start.15 = (bf16[2048,128]{1,0:T(8,128)(2,1)S(1)}, bf16[2048,128]{1,0:T(8,128)(2,1)S(1)}, u32[]{:S(2)}, u32[]{:S(2)}) collective-permute-start(bf16[2048,128]{1,0:T(8,128)(2,1)S(1)} %bitcast.20), channel_id=1, source_target_pairs={{0,16},{16,0},{32,48},{48,32},{64,80},{80,64},{96,112},{112,96},{1... | collective-permute-start | bytes 1572872 | tf_op jit(solution)/shard_map/ppermute | solution.py:16
  158.4 1.5 collective-permute-done.15
  159.9 0.1 broadcast_select_fusion.3
  160.0 0.1 pad_maximum_fusion.1.range_ref.refs_0_
  160.1 14.4 %second_step.1 = (f32[2304,128]{1,0:T(8,128)S(1)}, f32[2,2048,128]{2,1,0:T(8,128)S(1)}) custom-call(s32[1]{0:T(128)} %bitcast.core_ref, bf16[2304,4096]{1,0:T(8,128)(2,1)} %get-tuple-element.25.flat_ref, bf16[4096,128]{1,0:T(8,128)(2,1)S(1)} %pad_maximum_fusion.1.range_ref.refs_0_), custom_call_target="tpu_custom_call" | custom-call | tf_op jit(solution)/shard_map/second_step/pallas_call | solution.py:453
  174.5 0.1 slice_bitcast_fusion
  174.5 0.5 collective-permute-start.16
  175.0 2.3 collective-permute-done.16
  177.3 0.1 bitcast_add_fusion
  177.4 22.3 %all_to_all.22 = f32[64,32,128]{2,1,0:T(8,128)S(1)} all-to-all(f32[64,32,128]{2,1,0:T(8,128)S(1)} %bitcast.19), channel_id=1, replica_groups={{0,1,2,3,4,5,6,7,8,9,10,11,12,13,14,15,32,33,34,35,36,37,38,39,40,41,42..., dimensions={0} | all-to-all | bytes 2097152 | tf_op jit(solution)/shard_map/all_to_all | solution.py:523
  199.7 0.1 reduce_sum.19
  199.8 0.1 broadcast_in_dim.5
  200.0 21.0 %all_to_all.23 = f32[64,32,128]{2,1,0:T(8,128)S(1)} all-to-all(f32[64,32,128]{2,1,0:T(8,128)S(1)} %broadcast_in_dim.5), channel_id=1, replica_groups={{0,1,2,3,4,5,6,7,8,9,10,11,12,13,14,15,32,33,34,35,36,37,38,39,40,41,42..., dimensions={0} | all-to-all | bytes 2097152 | tf_op jit(solution)/shard_map/all_to_all | solution.py:523
  220.9 3.2 %collective-permute-start.17 = (f32[2048,128]{1,0:T(8,128)S(1)}, f32[2048,128]{1,0:T(8,128)S(1)}, u32[]{:S(2)}, u32[]{:S(2)}) collective-permute-start(f32[2048,128]{1,0:T(8,128)S(1)} %bitcast.17), channel_id=1, source_target_pairs={{0,16},{16,0},{32,48},{48,32},{64,80},{80,64},{96,112},{112,96},{1... | collective-permute-start | bytes 3145736 | tf_op jit(solution)/shard_map/ppermute | solution.py:16
  224.1 2.3 collective-permute-done.17
  226.4 0.1 broadcast_select_fusion.1
  226.5 0.1 pad_maximum_fusion.refs_1_
  226.7 11.9 %finish.1 = (f32[64,32,128]{2,1,0:T(8,128)}, f32[128,4096]{1,0:T(8,128)}) custom-call(bf16[4096,128]{1,0:T(8,128)(2,1)S(1)} %pad_maximum_fusion.1.range_ref.refs_0_, f32[4096,128]{1,0:T(8,128)S(1)} %pad_maximum_fusion.refs_1_, f32[2304,128]{1,0:T(8,128)S(1)} %get-tuple-element.29.refs_2_), custom_call_target="tpu_custom_call" | custom-call | tf_op jit(solution)/shard_map/finish/pallas_call | solution.py:506
  (15 shorter events, 0.1 us)
Async XLA Ops:
  1.7 11.8 %collective-permute-start = (bf16[32,4096]{1,0:T(8,128)(2,1)S(1)}, bf16[32,4096]{1,0:T(8,128)(2,1)S(1)}, u32[]{:S(2)}, u32[]{:S(2)}) collective-permute-start(bf16[32,4096]{1,0:T(8,128)(2,1)S(1)} %get-tuple-element.30), channel_id=1, source_target_pairs={{0,16},{16,32},{32,48},{48,64},{64,80},{80,96},{96,112},{1,17},{17... | collective-permute-start | bytes 786440 | tf_op jit(solution)/shard_map/ppermute | solution.py:22
  6.6 7.7 %collective-permute-start.1 = (bf16[32,4096]{1,0:T(8,128)(2,1)S(1)}, bf16[32,4096]{1,0:T(8,128)(2,1)S(1)}, u32[]{:S(2)}, u32[]{:S(2)}) collective-permute-start(bf16[32,4096]{1,0:T(8,128)(2,1)S(1)} %get-tuple-element.31), channel_id=1, source_target_pairs={{16,0},{32,16},{48,32},{64,48},{80,64},{96,80},{112,96},{17,1},{33... | collective-permute-start | bytes 786440 | tf_op jit(solution)/shard_map/ppermute | solution.py:22
  15.0 39.5 %collective-permute-start.2 = (bf16[72,4096]{1,0:T(8,128)(2,1)}, bf16[72,4096]{1,0:T(8,128)(2,1)S(1)}, u32[]{:S(2)}, u32[]{:S(2)}) collective-permute-start(bf16[72,4096]{1,0:T(8,128)(2,1)} %maximum_dynamic-update-slice_fusion.1.c3_ref), channel_id=1, source_target_pairs={{0,1},{1,2},{2,3},{3,4},{4,5},{5,6},{6,7},{7,8},{8,9},{9,10},{10,1... | collective-permute-start | bytes 1769480 | tf_op jit(solution)/shard_map/ppermute | solution.py:22
  18.2 36.3 %copy-start.1 = (bf16[72,4096]{1,0:T(8,128)(2,1)}, bf16[72,4096]{1,0:T(8,128)(2,1)S(1)}, u32[]{:S(2)}) copy-start(bf16[72,4096]{1,0:T(8,128)(2,1)S(1)} %maximum_dynamic-update-slice_fusion.c0_ref) | copy-start | bytes 1769476
  18.2 37.4 %copy-start.2 = (f32[3,3,4096]{2,1,0:T(4,128)S(1)}, f32[3,3,4096]{2,1,0:T(4,128)}, u32[]{:S(2)}) copy-start(f32[3,3,4096]{2,1,0:T(4,128)} %kern_ref.3) | copy-start | bytes 442372
  18.2 36.3 %collective-permute-start.3 = (bf16[72,4096]{1,0:T(8,128)(2,1)S(1)}, bf16[72,4096]{1,0:T(8,128)(2,1)S(1)}, u32[]{:S(2)}, u32[]{:S(2)}) collective-permute-start(bf16[72,4096]{1,0:T(8,128)(2,1)S(1)} %maximum_dynamic-update-slice_fusion.c0_ref), channel_id=1, source_target_pairs={{1,0},{2,1},{3,2},{4,3},{5,4},{6,5},{7,6},{8,7},{9,8},{10,9},{11,1... | collective-permute-start | bytes 1769480 | tf_op jit(solution)/shard_map/ppermute | solution.py:22
  54.6 0.8 copy-start.4
  54.6 1.0 copy-start.5
  55.6 0.8 copy-start.3
  63.8 1.3 collective-permute-start.4
  65.0 4.6 %collective-permute-start.5 = (f32[128,128]{1,0:T(8,128)S(1)}, f32[128,128]{1,0:T(8,128)S(1)}, u32[]{:S(2)}, u32[]{:S(2)}) collective-permute-start(f32[128,128]{1,0:T(8,128)S(1)} %add.41), channel_id=1, source_target_pairs={{0,1},{1,0},{2,3},{3,2},{4,5},{5,4},{6,7},{7,6},{8,9},{9,8},{10,11... | collective-permute-start | bytes 196616 | tf_op jit(solution)/shard_map/ppermute | solution.py:16
  67.2 5.9 %collective-permute-start.6 = (f32[128,128]{1,0:T(8,128)S(1)}, f32[128,128]{1,0:T(8,128)S(1)}, u32[]{:S(2)}, u32[]{:S(2)}) collective-permute-start(f32[128,128]{1,0:T(8,128)S(1)} %add.41), channel_id=1, source_target_pairs={{0,2},{1,3},{2,0},{3,1},{4,6},{5,7},{6,4},{7,5},{8,10},{9,11},{10,... | collective-permute-start | bytes 196616 | tf_op jit(solution)/shard_map/ppermute | solution.py:16
  69.6 4.5 %collective-permute-start.7 = (f32[128,128]{1,0:T(8,128)S(1)}, f32[128,128]{1,0:T(8,128)S(1)}, u32[]{:S(2)}, u32[]{:S(2)}) collective-permute-start(f32[128,128]{1,0:T(8,128)S(1)} %add.41), channel_id=1, source_target_pairs={{0,3},{1,2},{2,1},{3,0},{4,7},{5,6},{6,5},{7,4},{8,11},{9,10},{10,... | collective-permute-start | bytes 196616 | tf_op jit(solution)/shard_map/ppermute | solution.py:16
  74.1 4.6 %collective-permute-start.10 = (f32[128,128]{1,0:T(8,128)S(1)}, f32[128,128]{1,0:T(8,128)S(1)}, u32[]{:S(2)}, u32[]{:S(2)}) collective-permute-start(f32[128,128]{1,0:T(8,128)S(1)} %add_add_fusion.2), channel_id=1, source_target_pairs={{0,12},{1,13},{2,14},{3,15},{4,8},{5,9},{6,10},{7,11},{8,4},{9,5},... | collective-permute-start | bytes 196616 | tf_op jit(solution)/shard_map/ppermute | solution.py:16
  77.0 3.4 %collective-permute-start.8 = (f32[128,128]{1,0:T(8,128)S(1)}, f32[128,128]{1,0:T(8,128)S(1)}, u32[]{:S(2)}, u32[]{:S(2)}) collective-permute-start(f32[128,128]{1,0:T(8,128)S(1)} %add_add_fusion.2), channel_id=1, source_target_pairs={{0,4},{1,5},{2,6},{3,7},{4,0},{5,1},{6,2},{7,3},{8,12},{9,13},{10,... | collective-permute-start | bytes 196616 | tf_op jit(solution)/shard_map/ppermute | solution.py:16
  77.0 4.8 %collective-permute-start.9 = (f32[128,128]{1,0:T(8,128)S(1)}, f32[128,128]{1,0:T(8,128)S(1)}, u32[]{:S(2)}, u32[]{:S(2)}) collective-permute-start(f32[128,128]{1,0:T(8,128)S(1)} %add_add_fusion.2), channel_id=1, source_target_pairs={{0,8},{1,9},{2,10},{3,11},{4,12},{5,13},{6,14},{7,15},{8,0},{9,1},... | collective-permute-start | bytes 196616 | tf_op jit(solution)/shard_map/ppermute | solution.py:16
  81.9 4.7 %collective-permute-start.11 = (f32[128,128]{1,0:T(8,128)S(1)}, f32[128,128]{1,0:T(8,128)S(1)}, u32[]{:S(2)}, u32[]{:S(2)}) collective-permute-start(f32[128,128]{1,0:T(8,128)S(1)} %add_add_fusion.1), channel_id=1, source_target_pairs={{0,32},{16,48},{32,0},{48,16},{64,96},{80,112},{96,64},{112,80},{1... | collective-permute-start | bytes 196616 | tf_op jit(solution)/shard_map/ppermute | solution.py:16
  83.5 5.4 %collective-permute-start.12 = (f32[128,128]{1,0:T(8,128)S(1)}, f32[128,128]{1,0:T(8,128)S(1)}, u32[]{:S(2)}, u32[]{:S(2)}) collective-permute-start(f32[128,128]{1,0:T(8,128)S(1)} %add_add_fusion.1), channel_id=1, source_target_pairs={{0,64},{16,80},{32,96},{48,112},{64,0},{80,16},{96,32},{112,48},{1... | collective-permute-start | bytes 196616 | tf_op jit(solution)/shard_map/ppermute | solution.py:16
  86.6 4.3 %collective-permute-start.13 = (f32[128,128]{1,0:T(8,128)S(1)}, f32[128,128]{1,0:T(8,128)S(1)}, u32[]{:S(2)}, u32[]{:S(2)}) collective-permute-start(f32[128,128]{1,0:T(8,128)S(1)} %add_add_fusion.1), channel_id=1, source_target_pairs={{0,96},{16,112},{32,64},{48,80},{64,32},{80,48},{96,0},{112,16},{1... | collective-permute-start | bytes 196616 | tf_op jit(solution)/shard_map/ppermute | solution.py:16
  90.9 1.3 copy-start
  104.7 10.4 %collective-permute-start.14 = (f32[2048,128]{1,0:T(8,128)S(1)}, f32[2048,128]{1,0:T(8,128)S(1)}, u32[]{:S(2)}, u32[]{:S(2)}) collective-permute-start(f32[2048,128]{1,0:T(8,128)S(1)} %get-tuple-element.27), channel_id=1, source_target_pairs={{0,16},{16,0},{32,48},{48,32},{64,80},{80,64},{96,112},{112,96},{1... | collective-permute-start | bytes 3145736 | tf_op jit(solution)/shard_map/ppermute | solution.py:16
  155.9 4.0 %collective-permute-start.15 = (bf16[2048,128]{1,0:T(8,128)(2,1)S(1)}, bf16[2048,128]{1,0:T(8,128)(2,1)S(1)}, u32[]{:S(2)}, u32[]{:S(2)}) collective-permute-start(bf16[2048,128]{1,0:T(8,128)(2,1)S(1)} %bitcast.20), channel_id=1, source_target_pairs={{0,16},{16,0},{32,48},{48,32},{64,80},{80,64},{96,112},{112,96},{1... | collective-permute-start | bytes 1572872 | tf_op jit(solution)/shard_map/ppermute | solution.py:16
  174.5 2.7 %collective-permute-start.16 = (f32[2048,128]{1,0:T(8,128)S(1)}, f32[2048,128]{1,0:T(8,128)S(1)}, u32[]{:S(2)}, u32[]{:S(2)}) collective-permute-start(f32[2048,128]{1,0:T(8,128)S(1)} %slice_bitcast_fusion), channel_id=1, source_target_pairs={{0,16},{16,0},{32,48},{48,32},{64,80},{80,64},{96,112},{112,96},{1... | collective-permute-start | bytes 3145736 | tf_op jit(solution)/shard_map/ppermute | solution.py:16
  220.9 5.5 %collective-permute-start.17 = (f32[2048,128]{1,0:T(8,128)S(1)}, f32[2048,128]{1,0:T(8,128)S(1)}, u32[]{:S(2)}, u32[]{:S(2)}) collective-permute-start(f32[2048,128]{1,0:T(8,128)S(1)} %bitcast.17), channel_id=1, source_target_pairs={{0,16},{16,0},{32,48},{48,32},{64,80},{80,64},{96,112},{112,96},{1... | collective-permute-start | bytes 3145736 | tf_op jit(solution)/shard_map/ppermute | solution.py:16

commit v6 on v5

--- a/solution.py
+++ b/solution.py
@@ -480,10 +480,15 @@
 ):
     rows, cols, k = basis_ref.shape
     moment = moment_ref[...]
-    work_ref[...] = lax.dot_general(
-        range_ref[...].astype(jnp.float32), moment, (((0,), (0,)), ((), ())), precision=HIGH,
+    terms, left = [], moment
+    for _ in range(3):
+        terms.append(left.astype(jnp.bfloat16))
+        left = left - terms[-1].astype(jnp.float32)
+    gram = lax.dot_general(
+        range_ref[...], jnp.concatenate(terms, axis=1), (((0,), (0,)), ((), ())),
         preferred_element_type=jnp.float32,
     )
+    work_ref[...] = gram[:, :k] + (gram[:, k : 2 * k] + gram[:, 2 * k :])
     inverse = inverse_factor(work_ref)
     basis = times_transposed(second_ref[...], inverse) * basis_scale
     inner = basis[: rows * cols].reshape(rows, cols, k)

time: 239 us -> 238 us (level)
  no operation moved by 1% of the time
where the time goes in v6:
time: 238 us; the launch traced here: 237 us
  Pallas kernels  90.2 us (38%)
  blocking collectives  83.9 us (35%)
  starting transfers between devices  36 us (15%)
  waiting for transfers between devices  20.4 us (9%)
  local copies, waits for them, and re-layouts  4.5 us (2%)
    all_to_all x4, blocking collectives, all_sum(): lax.all_to_all(v, BOTH, 0, 0, axis_index_groups=groups, tiled=True)  83.9 us
    pallas_call x1, Pallas kernels, smooth_sketch(): pl.pallas_call(smooth_body, grid=(channels // width,), in_specs=[pl.Block...  34.9 us
    ppermute x14, starting transfers between devices, xor_permute(): lax.ppermute(value, axis, [(i, i ^ mask) for i in range(lax.axis_size(axi...  24.6 us
    ppermute x14, waiting for transfers between devices, xor_permute(): lax.ppermute(value, axis, [(i, i ^ mask) for i in range(lax.axis_size(axi...  19.6 us
    pallas_call x1, Pallas kernels, second_step(): pl.pallas_call(second_body, grid_spec=pltpu.PrefetchScalarGridSpec(num_sc...  14.4 us
    pallas_call x1, Pallas kernels, project_other(): pl.pallas_call(project_other_body, grid_spec=pltpu.PrefetchScalarGridSpec...  12.4 us
    ppermute x4, starting transfers between devices, shift_permute(): return lax.ppermute(value, axis, pairs)  11.4 us
    pallas_call x1, Pallas kernels, finish(): pl.pallas_call(body, out_shape=[jax.ShapeDtypeStruct(tile + (k,), jnp.flo...  10.8 us
  transfers between devices with their start and end apart: 18, of which 12 were waited for; matrix products, arithmetic and copies ran while one was open for 0% of the time, Pallas kernels for 19%

profile of v6, /device:TPU:1, one launch (start us, length us, event | category | flops | bytes accessed | tf_op | source)
XLA Modules:
  0.0 237.5 jit_solution(8068567800710359602)
XLA Ops:
  0.6 1.1 slice_bitcast_fusion.2
  1.7 4.9 %collective-permute-start = (bf16[32,4096]{1,0:T(8,128)(2,1)S(1)}, bf16[32,4096]{1,0:T(8,128)(2,1)S(1)}, u32[]{:S(2)}, u32[]{:S(2)}) collective-permute-start(bf16[32,4096]{1,0:T(8,128)(2,1)S(1)} %get-tuple-element.30), channel_id=1, source_target_pairs={{0,16},{16,32},{32,48},{48,64},{64,80},{80,96},{96,112},{1,17},{17... | collective-permute-start | bytes 786440 | tf_op jit(solution)/shard_map/ppermute | solution.py:22
  6.6 1.9 collective-permute-start.1
  8.6 5.0 %edge_columns.1 = (bf16[72,4096]{1,0:T(8,128)(2,1)S(1)}, bf16[64,4096]{1,0:T(8,128)(2,1)S(1)}, bf16[64,4096]{1,0:T(8,128)(2,1)S(1)}, bf16[72,4096]{1,0:T(8,128)(2,1)}) custom-call(bf16[64,32,4096]{2,1,0:T(8,128)(2,1)} %lower_ref.1, bf16[64,32,4096]{2,1,0:T(8,128)(2,1)} %lower_ref.1), custom_call_target="tpu_custom_call" | custom-call | flops 1073741824 | bytes 10485760 | tf_op jit(solution)/shard_map/edge_columns/pallas_call | solution.py:266
  13.6 0.7 collective-permute-done.1.bot_ref
  14.4 0.7 maximum_dynamic-update-slice_fusion.1.c3_ref
  15.0 3.1 %collective-permute-start.2 = (bf16[72,4096]{1,0:T(8,128)(2,1)}, bf16[72,4096]{1,0:T(8,128)(2,1)S(1)}, u32[]{:S(2)}, u32[]{:S(2)}) collective-permute-start(bf16[72,4096]{1,0:T(8,128)(2,1)} %maximum_dynamic-update-slice_fusion.1.c3_ref), channel_id=1, source_target_pairs={{0,1},{1,2},{2,3},{3,4},{4,5},{5,6},{6,7},{7,8},{8,9},{9,10},{10,1... | collective-permute-start | bytes 1769480 | tf_op jit(solution)/shard_map/ppermute | solution.py:22
  18.2 0.1 maximum_dynamic-update-slice_fusion.c0_ref
  18.2 0.0 copy-start.2
  18.2 1.4 collective-permute-start.3
  19.7 34.9 %smooth_sketch.1 = (bf16[2304,4096]{1,0:T(8,128)(2,1)}, f32[2304,128]{1,0:T(8,128)}, f32[128,128]{1,0:T(8,128)}) custom-call(bf16[64,32,4096]{2,1,0:T(8,128)(2,1)} %lower_ref.1, f32[3,3,4096]{2,1,0:T(4,128)} %kern_ref.3, bf16[4096,128]{1,0:T(8,128)(2,1)} %test_ref.3), custom_call_target="tpu_custom_call" | custom-call | flops 17246978048 | bytes 33554432 | tf_op jit(solution)/shard_map/smooth_sketch/pallas_call | solution.py:111
  54.6 0.0 collective-permute-done.2.left_ref
  54.6 0.0 collective-permute-done.3.right_ref
  54.6 0.8 copy-done.4
  55.4 0.2 copy-done.5
  55.6 0.8 copy-done.3
  56.4 7.3 %border_sketch.1 = (bf16[2304,4096]{1,0:T(8,128)(2,1)}, f32[2304,128]{1,0:T(8,128)}, f32[128,128]{1,0:T(8,128)S(1)}) custom-call(bf16[64,32,4096]{2,1,0:T(8,128)(2,1)} %lower_ref.1, bf16[64,32,4096]{2,1,0:T(8,128)(2,1)} %lower_ref.1, bf16[72,4096]{1,0:T(8,128)(2,1)} %copy-done.1, ...), custom_call_target="tpu_custom_call", output_to_operand_aliasing={{0}: (13, {}), {1}: (14, {})} | custom-call | tf_op jit(solution)/shard_map/border_sketch/pallas_call | solution.py:214
  63.8 0.0 collective-permute-start.4
  63.8 1.2 collective-permute-done.4
  65.0 2.2 collective-permute-start.5
  67.2 2.4 %collective-permute-start.6 = (f32[128,128]{1,0:T(8,128)S(1)}, f32[128,128]{1,0:T(8,128)S(1)}, u32[]{:S(2)}, u32[]{:S(2)}) collective-permute-start(f32[128,128]{1,0:T(8,128)S(1)} %add.41), channel_id=1, source_target_pairs={{0,2},{1,3},{2,0},{3,1},{4,6},{5,7},{6,4},{7,5},{8,10},{9,11},{10,... | collective-permute-start | bytes 196616 | tf_op jit(solution)/shard_map/ppermute | solution.py:16
  69.6 0.1 collective-permute-start.7
  69.7 3.4 %collective-permute-done.6 = f32[128,128]{1,0:T(8,128)S(1)} collective-permute-done((f32[128,128]{1,0:T(8,128)S(1)}, f32[128,128]{1,0:T(8,128)S(1)}, u32[]{:S(2)}, u32[]{:S(2)}) %collective-permute-start.6) | collective-permute-done | bytes 65568 | tf_op jit(solution)/shard_map/ppermute | solution.py:16
  73.0 1.0 collective-permute-done.7
  74.1 2.9 %collective-permute-start.10 = (f32[128,128]{1,0:T(8,128)S(1)}, f32[128,128]{1,0:T(8,128)S(1)}, u32[]{:S(2)}, u32[]{:S(2)}) collective-permute-start(f32[128,128]{1,0:T(8,128)S(1)} %add_add_fusion.2), channel_id=1, source_target_pairs={{0,12},{1,13},{2,14},{3,15},{4,8},{5,9},{6,10},{7,11},{8,4},{9,5},... | collective-permute-start | bytes 196616 | tf_op jit(solution)/shard_map/ppermute | solution.py:16
  77.0 1.3 collective-permute-start.9
  78.3 0.4 collective-permute-done.10
  78.7 1.8 collective-permute-done.8
  80.4 1.4 collective-permute-done.9
  81.9 1.7 collective-permute-start.11
  83.5 3.0 %collective-permute-start.12 = (f32[128,128]{1,0:T(8,128)S(1)}, f32[128,128]{1,0:T(8,128)S(1)}, u32[]{:S(2)}, u32[]{:S(2)}) collective-permute-start(f32[128,128]{1,0:T(8,128)S(1)} %add_add_fusion.1), channel_id=1, source_target_pairs={{0,64},{16,80},{32,96},{48,112},{64,0},{80,16},{96,32},{112,48},{1... | collective-permute-start | bytes 196616 | tf_op jit(solution)/shard_map/ppermute | solution.py:16
  86.6 0.0 collective-permute-start.13
  86.6 0.0 collective-permute-done.11
  86.6 2.3 collective-permute-done.12
  88.9 2.0 collective-permute-done.13
  90.9 0.0 copy-start
  90.9 1.3 copy-done
  92.2 12.4 %project_other.1 = (f32[2048,128]{1,0:T(8,128)S(1)}, bf16[128,2304]{1,0:T(8,128)(2,1)S(1)}) custom-call(s32[1]{0:T(128)} %bitcast.core_ref, f32[128,128]{1,0:T(8,128)S(1)} %add_add_fusion.gram_ref, f32[2304,128]{1,0:T(8,128)S(1)} %copy-done, bf16[2304,4096]{1,0:T(8,128)(2,1)} %get-tuple-element.25.flat_ref), custom_call_target="tpu_custom_call" | custom-call | tf_op jit(solution)/shard_map/project_other/pallas_call | solution.py:377
  104.7 5.0 %collective-permute-start.14 = (f32[2048,128]{1,0:T(8,128)S(1)}, f32[2048,128]{1,0:T(8,128)S(1)}, u32[]{:S(2)}, u32[]{:S(2)}) collective-permute-start(f32[2048,128]{1,0:T(8,128)S(1)} %get-tuple-element.27), channel_id=1, source_target_pairs={{0,16},{16,0},{32,48},{48,32},{64,80},{80,64},{96,112},{112,96},{1... | collective-permute-start | bytes 3145736 | tf_op jit(solution)/shard_map/ppermute | solution.py:16
  109.6 5.4 %project_own.1 = f32[2048,128]{1,0:T(8,128)S(1)} custom-call(s32[1]{0:T(128)} %bitcast.core_ref, bf16[128,2304]{1,0:T(8,128)(2,1)S(1)} %get-tuple-element.26.basis_ref, bf16[2304,4096]{1,0:T(8,128)(2,1)} %get-tuple-element.25.flat_ref), custom_call_target="tpu_custom_call" | custom-call | flops 4831838208 | bytes 9437184 | tf_op jit(solution)/shard_map/project_own/pallas_call | solution.py:403
  115.0 0.0 collective-permute-done.14
  115.0 0.1 add.51
  115.1 24.0 %all_to_all.20 = f32[64,32,128]{2,1,0:T(8,128)S(1)} all-to-all(f32[64,32,128]{2,1,0:T(8,128)S(1)} %bitcast.18), channel_id=1, replica_groups={{0,1,2,3,4,5,6,7,8,9,10,11,12,13,14,15,32,33,34,35,36,37,38,39,40,41,42..., dimensions={0} | all-to-all | bytes 2097152 | tf_op jit(solution)/shard_map/all_to_all | solution.py:528
  139.1 0.1 reduce_sum.18
  139.2 0.1 broadcast_in_dim.4
  139.3 16.6 %all_to_all.21 = bf16[64,32,128]{2,1,0:T(8,128)(2,1)S(1)} all-to-all(bf16[64,32,128]{2,1,0:T(8,128)(2,1)S(1)} %broadcast_in_dim.4), channel_id=1, replica_groups={{0,1,2,3,4,5,6,7,8,9,10,11,12,13,14,15,32,33,34,35,36,37,38,39,40,41,42..., dimensions={0} | all-to-all | bytes 1048576 | tf_op jit(solution)/shard_map/all_to_all | solution.py:528
  155.9 2.5 %collective-permute-start.15 = (bf16[2048,128]{1,0:T(8,128)(2,1)S(1)}, bf16[2048,128]{1,0:T(8,128)(2,1)S(1)}, u32[]{:S(2)}, u32[]{:S(2)}) collective-permute-start(bf16[2048,128]{1,0:T(8,128)(2,1)S(1)} %bitcast.20), channel_id=1, source_target_pairs={{0,16},{16,0},{32,48},{48,32},{64,80},{80,64},{96,112},{112,96},{1... | collective-permute-start | bytes 1572872 | tf_op jit(solution)/shard_map/ppermute | solution.py:16
  158.4 1.5 collective-permute-done.15
  159.9 0.1 broadcast_select_fusion.3
  160.0 0.1 pad_maximum_fusion.1.range_ref.refs_0_
  160.1 14.4 %second_step.1 = (f32[2304,128]{1,0:T(8,128)S(1)}, f32[2,2048,128]{2,1,0:T(8,128)S(1)}) custom-call(s32[1]{0:T(128)} %bitcast.core_ref, bf16[2304,4096]{1,0:T(8,128)(2,1)} %get-tuple-element.25.flat_ref, bf16[4096,128]{1,0:T(8,128)(2,1)S(1)} %pad_maximum_fusion.1.range_ref.refs_0_), custom_call_target="tpu_custom_call" | custom-call | tf_op jit(solution)/shard_map/second_step/pallas_call | solution.py:453
  174.5 0.1 slice_bitcast_fusion
  174.5 0.5 collective-permute-start.16
  175.0 2.3 collective-permute-done.16
  177.3 0.1 bitcast_add_fusion
  177.4 22.3 %all_to_all.22 = f32[64,32,128]{2,1,0:T(8,128)S(1)} all-to-all(f32[64,32,128]{2,1,0:T(8,128)S(1)} %bitcast.19), channel_id=1, replica_groups={{0,1,2,3,4,5,6,7,8,9,10,11,12,13,14,15,32,33,34,35,36,37,38,39,40,41,42..., dimensions={0} | all-to-all | bytes 2097152 | tf_op jit(solution)/shard_map/all_to_all | solution.py:528
  199.7 0.1 reduce_sum.19
  199.8 0.1 broadcast_in_dim.5
  200.0 21.0 %all_to_all.23 = f32[64,32,128]{2,1,0:T(8,128)S(1)} all-to-all(f32[64,32,128]{2,1,0:T(8,128)S(1)} %broadcast_in_dim.5), channel_id=1, replica_groups={{0,1,2,3,4,5,6,7,8,9,10,11,12,13,14,15,32,33,34,35,36,37,38,39,40,41,42..., dimensions={0} | all-to-all | bytes 2097152 | tf_op jit(solution)/shard_map/all_to_all | solution.py:528
  220.9 3.2 %collective-permute-start.17 = (f32[2048,128]{1,0:T(8,128)S(1)}, f32[2048,128]{1,0:T(8,128)S(1)}, u32[]{:S(2)}, u32[]{:S(2)}) collective-permute-start(f32[2048,128]{1,0:T(8,128)S(1)} %bitcast.17), channel_id=1, source_target_pairs={{0,16},{16,0},{32,48},{48,32},{64,80},{80,64},{96,112},{112,96},{1... | collective-permute-start | bytes 3145736 | tf_op jit(solution)/shard_map/ppermute | solution.py:16
  224.1 2.3 collective-permute-done.17
  226.4 0.1 broadcast_select_fusion.1
  226.5 0.1 pad_maximum_fusion.refs_1_
  226.7 10.8 %finish.1 = (f32[64,32,128]{2,1,0:T(8,128)}, f32[128,4096]{1,0:T(8,128)}) custom-call(bf16[4096,128]{1,0:T(8,128)(2,1)S(1)} %pad_maximum_fusion.1.range_ref.refs_0_, f32[4096,128]{1,0:T(8,128)S(1)} %pad_maximum_fusion.refs_1_, f32[2304,128]{1,0:T(8,128)S(1)} %get-tuple-element.29.refs_2_), custom_call_target="tpu_custom_call" | custom-call | tf_op jit(solution)/shard_map/finish/pallas_call | solution.py:511
  (15 shorter events, 0.1 us)
Async XLA Ops:
  1.7 11.8 %collective-permute-start = (bf16[32,4096]{1,0:T(8,128)(2,1)S(1)}, bf16[32,4096]{1,0:T(8,128)(2,1)S(1)}, u32[]{:S(2)}, u32[]{:S(2)}) collective-permute-start(bf16[32,4096]{1,0:T(8,128)(2,1)S(1)} %get-tuple-element.30), channel_id=1, source_target_pairs={{0,16},{16,32},{32,48},{48,64},{64,80},{80,96},{96,112},{1,17},{17... | collective-permute-start | bytes 786440 | tf_op jit(solution)/shard_map/ppermute | solution.py:22
  6.6 7.7 %collective-permute-start.1 = (bf16[32,4096]{1,0:T(8,128)(2,1)S(1)}, bf16[32,4096]{1,0:T(8,128)(2,1)S(1)}, u32[]{:S(2)}, u32[]{:S(2)}) collective-permute-start(bf16[32,4096]{1,0:T(8,128)(2,1)S(1)} %get-tuple-element.31), channel_id=1, source_target_pairs={{16,0},{32,16},{48,32},{64,48},{80,64},{96,80},{112,96},{17,1},{33... | collective-permute-start | bytes 786440 | tf_op jit(solution)/shard_map/ppermute | solution.py:22
  15.0 39.5 %collective-permute-start.2 = (bf16[72,4096]{1,0:T(8,128)(2,1)}, bf16[72,4096]{1,0:T(8,128)(2,1)S(1)}, u32[]{:S(2)}, u32[]{:S(2)}) collective-permute-start(bf16[72,4096]{1,0:T(8,128)(2,1)} %maximum_dynamic-update-slice_fusion.1.c3_ref), channel_id=1, source_target_pairs={{0,1},{1,2},{2,3},{3,4},{4,5},{5,6},{6,7},{7,8},{8,9},{9,10},{10,1... | collective-permute-start | bytes 1769480 | tf_op jit(solution)/shard_map/ppermute | solution.py:22
  18.2 36.3 %copy-start.1 = (bf16[72,4096]{1,0:T(8,128)(2,1)}, bf16[72,4096]{1,0:T(8,128)(2,1)S(1)}, u32[]{:S(2)}) copy-start(bf16[72,4096]{1,0:T(8,128)(2,1)S(1)} %maximum_dynamic-update-slice_fusion.c0_ref) | copy-start | bytes 1769476
  18.2 37.4 %copy-start.2 = (f32[3,3,4096]{2,1,0:T(4,128)S(1)}, f32[3,3,4096]{2,1,0:T(4,128)}, u32[]{:S(2)}) copy-start(f32[3,3,4096]{2,1,0:T(4,128)} %kern_ref.3) | copy-start | bytes 442372
  18.2 36.3 %collective-permute-start.3 = (bf16[72,4096]{1,0:T(8,128)(2,1)S(1)}, bf16[72,4096]{1,0:T(8,128)(2,1)S(1)}, u32[]{:S(2)}, u32[]{:S(2)}) collective-permute-start(bf16[72,4096]{1,0:T(8,128)(2,1)S(1)} %maximum_dynamic-update-slice_fusion.c0_ref), channel_id=1, source_target_pairs={{1,0},{2,1},{3,2},{4,3},{5,4},{6,5},{7,6},{8,7},{9,8},{10,9},{11,1... | collective-permute-start | bytes 1769480 | tf_op jit(solution)/shard_map/ppermute | solution.py:22
  54.6 0.8 copy-start.4
  54.6 1.0 copy-start.5
  55.6 0.8 copy-start.3
  63.8 1.3 collective-permute-start.4
  65.0 4.6 %collective-permute-start.5 = (f32[128,128]{1,0:T(8,128)S(1)}, f32[128,128]{1,0:T(8,128)S(1)}, u32[]{:S(2)}, u32[]{:S(2)}) collective-permute-start(f32[128,128]{1,0:T(8,128)S(1)} %add.41), channel_id=1, source_target_pairs={{0,1},{1,0},{2,3},{3,2},{4,5},{5,4},{6,7},{7,6},{8,9},{9,8},{10,11... | collective-permute-start | bytes 196616 | tf_op jit(solution)/shard_map/ppermute | solution.py:16
  67.2 5.9 %collective-permute-start.6 = (f32[128,128]{1,0:T(8,128)S(1)}, f32[128,128]{1,0:T(8,128)S(1)}, u32[]{:S(2)}, u32[]{:S(2)}) collective-permute-start(f32[128,128]{1,0:T(8,128)S(1)} %add.41), channel_id=1, source_target_pairs={{0,2},{1,3},{2,0},{3,1},{4,6},{5,7},{6,4},{7,5},{8,10},{9,11},{10,... | collective-permute-start | bytes 196616 | tf_op jit(solution)/shard_map/ppermute | solution.py:16
  69.6 4.5 %collective-permute-start.7 = (f32[128,128]{1,0:T(8,128)S(1)}, f32[128,128]{1,0:T(8,128)S(1)}, u32[]{:S(2)}, u32[]{:S(2)}) collective-permute-start(f32[128,128]{1,0:T(8,128)S(1)} %add.41), channel_id=1, source_target_pairs={{0,3},{1,2},{2,1},{3,0},{4,7},{5,6},{6,5},{7,4},{8,11},{9,10},{10,... | collective-permute-start | bytes 196616 | tf_op jit(solution)/shard_map/ppermute | solution.py:16
  74.1 4.6 %collective-permute-start.10 = (f32[128,128]{1,0:T(8,128)S(1)}, f32[128,128]{1,0:T(8,128)S(1)}, u32[]{:S(2)}, u32[]{:S(2)}) collective-permute-start(f32[128,128]{1,0:T(8,128)S(1)} %add_add_fusion.2), channel_id=1, source_target_pairs={{0,12},{1,13},{2,14},{3,15},{4,8},{5,9},{6,10},{7,11},{8,4},{9,5},... | collective-permute-start | bytes 196616 | tf_op jit(solution)/shard_map/ppermute | solution.py:16
  77.0 3.4 %collective-permute-start.8 = (f32[128,128]{1,0:T(8,128)S(1)}, f32[128,128]{1,0:T(8,128)S(1)}, u32[]{:S(2)}, u32[]{:S(2)}) collective-permute-start(f32[128,128]{1,0:T(8,128)S(1)} %add_add_fusion.2), channel_id=1, source_target_pairs={{0,4},{1,5},{2,6},{3,7},{4,0},{5,1},{6,2},{7,3},{8,12},{9,13},{10,... | collective-permute-start | bytes 196616 | tf_op jit(solution)/shard_map/ppermute | solution.py:16
  77.0 4.8 %collective-permute-start.9 = (f32[128,128]{1,0:T(8,128)S(1)}, f32[128,128]{1,0:T(8,128)S(1)}, u32[]{:S(2)}, u32[]{:S(2)}) collective-permute-start(f32[128,128]{1,0:T(8,128)S(1)} %add_add_fusion.2), channel_id=1, source_target_pairs={{0,8},{1,9},{2,10},{3,11},{4,12},{5,13},{6,14},{7,15},{8,0},{9,1},... | collective-permute-start | bytes 196616 | tf_op jit(solution)/shard_map/ppermute | solution.py:16
  81.9 4.7 %collective-permute-start.11 = (f32[128,128]{1,0:T(8,128)S(1)}, f32[128,128]{1,0:T(8,128)S(1)}, u32[]{:S(2)}, u32[]{:S(2)}) collective-permute-start(f32[128,128]{1,0:T(8,128)S(1)} %add_add_fusion.1), channel_id=1, source_target_pairs={{0,32},{16,48},{32,0},{48,16},{64,96},{80,112},{96,64},{112,80},{1... | collective-permute-start | bytes 196616 | tf_op jit(solution)/shard_map/ppermute | solution.py:16
  83.5 5.4 %collective-permute-start.12 = (f32[128,128]{1,0:T(8,128)S(1)}, f32[128,128]{1,0:T(8,128)S(1)}, u32[]{:S(2)}, u32[]{:S(2)}) collective-permute-start(f32[128,128]{1,0:T(8,128)S(1)} %add_add_fusion.1), channel_id=1, source_target_pairs={{0,64},{16,80},{32,96},{48,112},{64,0},{80,16},{96,32},{112,48},{1... | collective-permute-start | bytes 196616 | tf_op jit(solution)/shard_map/ppermute | solution.py:16
  86.6 4.3 %collective-permute-start.13 = (f32[128,128]{1,0:T(8,128)S(1)}, f32[128,128]{1,0:T(8,128)S(1)}, u32[]{:S(2)}, u32[]{:S(2)}) collective-permute-start(f32[128,128]{1,0:T(8,128)S(1)} %add_add_fusion.1), channel_id=1, source_target_pairs={{0,96},{16,112},{32,64},{48,80},{64,32},{80,48},{96,0},{112,16},{1... | collective-permute-start | bytes 196616 | tf_op jit(solution)/shard_map/ppermute | solution.py:16
  90.9 1.3 copy-start
  104.7 10.4 %collective-permute-start.14 = (f32[2048,128]{1,0:T(8,128)S(1)}, f32[2048,128]{1,0:T(8,128)S(1)}, u32[]{:S(2)}, u32[]{:S(2)}) collective-permute-start(f32[2048,128]{1,0:T(8,128)S(1)} %get-tuple-element.27), channel_id=1, source_target_pairs={{0,16},{16,0},{32,48},{48,32},{64,80},{80,64},{96,112},{112,96},{1... | collective-permute-start | bytes 3145736 | tf_op jit(solution)/shard_map/ppermute | solution.py:16
  155.9 4.0 %collective-permute-start.15 = (bf16[2048,128]{1,0:T(8,128)(2,1)S(1)}, bf16[2048,128]{1,0:T(8,128)(2,1)S(1)}, u32[]{:S(2)}, u32[]{:S(2)}) collective-permute-start(bf16[2048,128]{1,0:T(8,128)(2,1)S(1)} %bitcast.20), channel_id=1, source_target_pairs={{0,16},{16,0},{32,48},{48,32},{64,80},{80,64},{96,112},{112,96},{1... | collective-permute-start | bytes 1572872 | tf_op jit(solution)/shard_map/ppermute | solution.py:16
  174.5 2.7 %collective-permute-start.16 = (f32[2048,128]{1,0:T(8,128)S(1)}, f32[2048,128]{1,0:T(8,128)S(1)}, u32[]{:S(2)}, u32[]{:S(2)}) collective-permute-start(f32[2048,128]{1,0:T(8,128)S(1)} %slice_bitcast_fusion), channel_id=1, source_target_pairs={{0,16},{16,0},{32,48},{48,32},{64,80},{80,64},{96,112},{112,96},{1... | collective-permute-start | bytes 3145736 | tf_op jit(solution)/shard_map/ppermute | solution.py:16
  220.9 5.5 %collective-permute-start.17 = (f32[2048,128]{1,0:T(8,128)S(1)}, f32[2048,128]{1,0:T(8,128)S(1)}, u32[]{:S(2)}, u32[]{:S(2)}) collective-permute-start(f32[2048,128]{1,0:T(8,128)S(1)} %bitcast.17), channel_id=1, source_target_pairs={{0,16},{16,0},{32,48},{48,32},{64,80},{80,64},{96,112},{112,96},{1... | collective-permute-start | bytes 3145736 | tf_op jit(solution)/shard_map/ppermute | solution.py:16
